TPU v7x, 128 devices: a whole 4x4x4 slice. The times are simulated.
128 devices in a mesh: grp: 16 (over z, y), tp: 8 (over x, core).
Axes of the slice: x: 4, y: 4, z: 4, core: 2. Of those that a mesh axis runs over, the one named last changes fastest.
Arguments:
- tokens: bfloat16 [1024, 4, 8192], P('grp', None, 'tp'), may hold values from -6 to 6
- adapter_id: int32 [1024], P('grp'), may hold values from 0 to 127, as said below
- pool_slot: int32 [128], replicated, may hold values from 0 to 127, as said below
- lengths: int32 [1024], P('grp'), may hold values from 1 to 64, as said below
- w_query: bfloat16 [8192, 8192], P(None, 'tp'), may hold values from -0.0625 to 0.0625
- w_key: bfloat16 [8192, 1024], P(None, 'tp'), may hold values from -0.0625 to 0.0625
- w_value: bfloat16 [8192, 1024], P(None, 'tp'), may hold values from -0.0625 to 0.0625
- pooled_down_weights: bfloat16 [128, 8192, 64], P('grp', 'tp'), may hold values from -0.0625 to 0.0625
- pool_up: bfloat16 [128, 64, 8192], P('grp', None, 'tp'), may hold values from -0.75 to 0.75
- cache_key: bfloat16 [1024, 64, 1024], P('grp', None, 'tp')
- cache_value: bfloat16 [1024, 64, 1024], P('grp', None, 'tp'), may hold values from -6 to 6
Outputs:
- attended: bfloat16 [1024, 4, 8192], P('grp', None, 'tp')
Inputs may be any that keep to these rules, and one draw needn't show every extreme that they name: `adapter_id`: each aligned block of 64 rows (one group) uses adapters of exactly 8 owners (owner = pool_slot // 8), 8 rows each, and at most 2 distinct adapters of one owner, reached in every block; a single owner, the same for all blocks, serves 8 rows of every block. `pool_slot`: A permutation. `lengths`: each aligned block of 64 rows has a row of length 64.
All inputs are finite; a program needn't handle non-finite values.
Results may differ from a plain program's by a relative error of at most 0.012.
The roundings to bfloat16 on the way count: a program that leaves them out, or rounds other values in their place, can miss the bound.
Values may be sent and summed in bfloat16 or wider, within the bound.
A program may use at most 128 MiB of HBM per device.

v0:
```python
import math

import jax
import jax.numpy as jnp
from jax import lax
from jax.experimental import pallas as pl
from jax.experimental.pallas import tpu as pltpu
from jax.sharding import PartitionSpec as P

MESH = pl.DeviceIdType.MESH

HD = 128
CAP = 8


rope_base = 500000.0


def rotate(values, position):
    half_width = values.shape[-1] // 2
    inv_freq = jnp.exp(
        jnp.arange(half_width, dtype=jnp.float32) * (-2.0 * math.log(rope_base) / values.shape[-1])
    )
    angles = position.astype(jnp.float32)[:, :, None, None] * inv_freq
    cosine = jnp.cos(angles)
    sines = jnp.sin(angles)
    front_half = values[..., :half_width]
    back_half = values[..., half_width:]
    return jnp.concatenate(
        [front_half * cosine - back_half * sines, back_half * cosine + front_half * sines], axis=-1
    )


def attend(queries, key_new, value_new, cache_key, cache_value, lengths):
    score_scale = 1.0 / math.sqrt(queries.shape[-1])
    cached = (
        jnp.einsum("rskgd,rlkd->rskgl", queries, cache_key, preferred_element_type=jnp.float32)
        * score_scale
    )
    fresh_scores = (
        jnp.einsum("rskgd,rtkd->rskgt", queries, key_new, preferred_element_type=jnp.float32)
        * score_scale
    )
    live_mask = jnp.arange(cache_key.shape[1], dtype=jnp.int32)[None, :] < lengths[:, None]
    cached = jnp.where(live_mask[:, None, None, None, :], cached, -1e30)
    steps_here = key_new.shape[1]
    causal = (
        jnp.arange(steps_here, dtype=jnp.int32)[:, None]
        >= jnp.arange(steps_here, dtype=jnp.int32)[None, :]
    )
    fresh_scores = jnp.where(causal[None, :, None, None, :], fresh_scores, -1e30)
    row_max = jnp.maximum(jnp.max(cached, axis=-1), jnp.max(fresh_scores, axis=-1))
    cache_exp = jnp.exp(cached - row_max[..., None])
    fresh_exp = jnp.exp(fresh_scores - row_max[..., None])
    weight_sum = jnp.sum(cache_exp, axis=-1) + jnp.sum(fresh_exp, axis=-1)
    cache_weights = (cache_exp / weight_sum[..., None]).astype(jnp.bfloat16)
    fresh_weights = (fresh_exp / weight_sum[..., None]).astype(jnp.bfloat16)
    combined = jnp.einsum(
        "rskgl,rlkd->rskgd", cache_weights, cache_value, preferred_element_type=jnp.float32
    )
    combined = combined + jnp.einsum(
        "rskgt,rtkd->rskgd", fresh_weights, value_new, preferred_element_type=jnp.float32
    )
    return combined.astype(jnp.bfloat16)


def exchange_kernel(axis, count, send_ref, got_ref, send_sem, recv_sem, local_sem):
    me = lax.axis_index(axis)
    barrier = pltpu.get_barrier_semaphore()
    for offset in range(1, count):
        peer = lax.rem(me + offset, count)
        pl.semaphore_signal(barrier, inc=1, device_id={axis: peer}, device_id_type=MESH)
    pl.semaphore_wait(barrier, count - 1)
    local = pltpu.make_async_copy(send_ref.at[me], got_ref.at[me], local_sem)
    local.start()
    outgoing = []
    for offset in range(1, count):
        peer = lax.rem(me + offset, count)
        copy = pltpu.make_async_remote_copy(
            src_ref=send_ref.at[peer],
            dst_ref=got_ref.at[me],
            send_sem=send_sem.at[offset],
            recv_sem=recv_sem.at[offset],
            device_id={axis: peer},
            device_id_type=MESH,
        )
        copy.start()
        outgoing.append(copy)
    for offset in range(1, count):
        outgoing[offset - 1].wait_send()
        source = lax.rem(me + count - offset, count)
        incoming = pltpu.make_async_remote_copy(
            src_ref=send_ref.at[source],
            dst_ref=got_ref.at[source],
            send_sem=send_sem.at[offset],
            recv_sem=recv_sem.at[offset],
            device_id={axis: source},
            device_id_type=MESH,
        )
        incoming.wait_recv()
    local.wait()


def exchange(values, axis, count, collective):
    return pl.pallas_call(
        lambda *refs: exchange_kernel(axis, count, *refs),
        out_shape=jax.ShapeDtypeStruct(values.shape, values.dtype),
        in_specs=[pl.BlockSpec(memory_space=pltpu.VMEM)],
        out_specs=pl.BlockSpec(memory_space=pltpu.VMEM),
        scratch_shapes=[
            pltpu.SemaphoreType.DMA((count,)),
            pltpu.SemaphoreType.DMA((count,)),
            pltpu.SemaphoreType.DMA(()),
        ],
        compiler_params=pltpu.CompilerParams(collective_id=collective, has_side_effects=True),
    )(values)


def sum_kernel(axis, count, part_ref, total_ref, held, send_sem, recv_sem):
    me = lax.axis_index(axis)
    barrier = pltpu.get_barrier_semaphore()
    for offset in range(1, count):
        peer = lax.rem(me + offset, count)
        pl.semaphore_signal(barrier, inc=1, device_id={axis: peer}, device_id_type=MESH)
    pl.semaphore_wait(barrier, count - 1)
    outgoing = []
    for offset in range(1, count):
        peer = lax.rem(me + offset, count)
        copy = pltpu.make_async_remote_copy(
            src_ref=part_ref,
            dst_ref=held.at[me],
            send_sem=send_sem.at[offset],
            recv_sem=recv_sem.at[offset],
            device_id={axis: peer},
            device_id_type=MESH,
        )
        copy.start()
        outgoing.append(copy)
    held[me] = part_ref[...]
    for offset in range(1, count):
        outgoing[offset - 1].wait_send()
        source = lax.rem(me + count - offset, count)
        incoming = pltpu.make_async_remote_copy(
            src_ref=part_ref,
            dst_ref=held.at[source],
            send_sem=send_sem.at[offset],
            recv_sem=recv_sem.at[offset],
            device_id={axis: source},
            device_id_type=MESH,
        )
        incoming.wait_recv()
    total = held[0]
    for index in range(1, count):
        total = total + held[index]
    total_ref[...] = total.astype(total_ref.dtype)


def axis_sum(values, axis, count, collective, out_dtype):
    return pl.pallas_call(
        lambda *refs: sum_kernel(axis, count, *refs),
        out_shape=jax.ShapeDtypeStruct(values.shape, out_dtype),
        in_specs=[pl.BlockSpec(memory_space=pltpu.VMEM)],
        out_specs=pl.BlockSpec(memory_space=pltpu.VMEM),
        scratch_shapes=[
            pltpu.VMEM((count,) + values.shape, values.dtype),
            pltpu.SemaphoreType.DMA((count,)),
            pltpu.SemaphoreType.DMA((count,)),
        ],
        compiler_params=pltpu.CompilerParams(collective_id=collective, has_side_effects=True),
    )(values)


def owner_adapter_term(received, slot_ids, down_local, up_local):
    sources, rows, part_width = received.shape
    local_adapters, unused_item, adapter_rank = down_local.shape
    query_width = up_local.shape[2]
    token_rows = received.reshape(sources * rows, part_width)
    every_down = jnp.einsum(
        "td,adr->tar", token_rows, down_local, preferred_element_type=jnp.float32
    )
    pick = slot_ids.reshape(sources * rows)[:, None] == jnp.arange(local_adapters, dtype=jnp.int32)[None, :]
    partial_value_sum = jnp.sum(jnp.where(pick[:, :, None], every_down, 0.0), axis=1)
    tp_count = lax.axis_size("tp")
    summed = axis_sum(partial_value_sum.reshape(-1, 128), "tp", tp_count, 2, jnp.bfloat16)
    adapter_middle = summed.reshape(sources * rows, adapter_rank)
    spread_rows = jnp.where(pick[:, :, None], adapter_middle[:, None, :], jnp.zeros((), jnp.bfloat16))
    spread_rows = spread_rows.reshape(sources * rows, local_adapters * adapter_rank)
    adapter_output = jnp.dot(
        spread_rows,
        up_local.reshape(local_adapters * adapter_rank, query_width),
        preferred_element_type=jnp.float32,
    ).astype(jnp.bfloat16)
    return adapter_output.reshape(sources, rows, query_width)


def body(
    tokens,
    adapter_id,
    pool_slot,
    lengths,
    w_query,
    w_key,
    w_value,
    pooled_down_weights,
    pool_up,
    cache_key,
    cache_value,
):
    group_count = lax.axis_size("grp")
    tp_count = lax.axis_size("tp")
    row_count, step_count, part_width = tokens.shape
    local_adapter_rows, unused_item, adapter_rank = pooled_down_weights.shape
    query_width = w_query.shape[1]
    kv_width = w_key.shape[1]
    kv_local = kv_width // HD
    q_local = query_width // HD
    group_size = q_local // kv_local
    count_of_tokens = row_count * step_count
    adapter_span = jnp.arange(pool_slot.shape[0], dtype=jnp.int32)
    pool_pos = jnp.sum(
        jnp.where(adapter_id[:, None] == adapter_span[None, :], pool_slot[None, :], 0), axis=1
    )
    owner_grp = pool_pos // local_adapter_rows
    local_slot = pool_pos % local_adapter_rows
    row_span = jnp.arange(row_count, dtype=jnp.int32)
    same_owner = (owner_grp[:, None] == owner_grp[None, :]) & (row_span[None, :] < row_span[:, None])
    owner_rank = jnp.sum(same_owner.astype(jnp.int32), axis=1)
    send_slot = owner_grp * CAP + owner_rank
    slot_span = jnp.arange(group_count * CAP, dtype=jnp.int32)
    place = (slot_span[:, None] == send_slot[None, :]).astype(jnp.bfloat16)
    token_flat = tokens.reshape(row_count, step_count * part_width)
    send_tokens = jnp.dot(place, token_flat, preferred_element_type=jnp.float32).astype(jnp.bfloat16)
    send_ids = jnp.dot(
        place, local_slot.astype(jnp.bfloat16)[:, None], preferred_element_type=jnp.float32
    ).astype(jnp.bfloat16)
    send_ids = jnp.broadcast_to(
        send_ids.reshape(group_count * CAP, 1, 1), (group_count * CAP, step_count, 128)
    )
    packed = jnp.concatenate(
        [send_tokens.reshape(group_count * CAP, step_count, part_width), send_ids], axis=2
    ).reshape(group_count, CAP * step_count, part_width + 128)
    got = exchange(packed, "grp", group_count, 0)
    got_tokens = got[:, :, :part_width]
    got_ids = got[:, :, part_width].astype(jnp.int32)
    owner_out = owner_adapter_term(got_tokens, got_ids, pooled_down_weights, pool_up)
    back = exchange(owner_out, "grp", group_count, 1)
    back = back.reshape(group_count * CAP, step_count * query_width)
    adapter_output = jnp.dot(
        jnp.transpose(place), back, preferred_element_type=jnp.float32
    ).reshape(count_of_tokens, query_width)

    pieces = lax.all_gather(tokens.reshape(count_of_tokens, part_width), "tp", axis=0, tiled=False)

    def add_term(matrix):
        return jnp.einsum(
            "ptd,pdo->to",
            pieces,
            matrix.reshape(tp_count, part_width, matrix.shape[1]),
            preferred_element_type=jnp.float32,
        )

    base_query_rows = add_term(w_query)
    key_base = add_term(w_key)
    value_base = add_term(w_value)
    base_query_rows = base_query_rows + adapter_output
    position = lengths[:, None] + jnp.arange(step_count, dtype=jnp.int32)[None, :]
    queries = rotate(base_query_rows.reshape(row_count, step_count, q_local, HD), position)
    queries = queries.astype(jnp.bfloat16).reshape(row_count, step_count, kv_local, group_size, HD)
    key_new = rotate(key_base.reshape(row_count, step_count, kv_local, HD), position).astype(
        jnp.bfloat16
    )
    value_new = value_base.reshape(row_count, step_count, kv_local, HD).astype(jnp.bfloat16)
    cache_keys = cache_key.reshape(row_count, cache_key.shape[1], kv_local, HD)
    cache_values = cache_value.reshape(row_count, cache_value.shape[1], kv_local, HD)
    combined = attend(queries, key_new, value_new, cache_keys, cache_values, lengths)
    return combined.reshape(row_count, step_count, query_width)


def solution(mesh):
    in_specs = (
        P("grp", None, "tp"),
        P("grp"),
        P(),
        P("grp"),
        P(None, "tp"),
        P(None, "tp"),
        P(None, "tp"),
        P("grp", "tp", None),
        P("grp", None, "tp"),
        P("grp", None, "tp"),
        P("grp", None, "tp"),
    )
    out_specs = P("grp", None, "tp")
    return jax.shard_map(body, mesh=mesh, in_specs=in_specs, out_specs=out_specs, check_vma=False)
```

profile of v0, /device:TPU:1, one launch (start us, length us, event | category | flops | bytes accessed | tf_op | source)
XLA Modules:
  0.0 137.1 jit_solution(13866180040148440829)
XLA Ops:
  6.5 2.1 %all_gather_reshape.3 = bf16[1,256,1024]{2,1,0:T(8,128)(2,1)} reshape(bf16[64,4,1024]{2,1,0:T(4,128)(2,1)} %param.11) | data formatting | bytes 1048576 | tf_op jit(solution)/shard_map/all_gather;reshape | solution.py:252
  8.7 0.8 select_reduce_fusion.1
  10.2 1.2 copy.64
  11.4 1.4 %convolution_convert_fusion = bf16[128,4096]{1,0:T(8,128)(2,1)} fusion(bf16[64,4096]{1,0:T(8,128)(2,1)S(1)} %bitcast.120, s32[64]{0:T(128)S(1)} %multiply_add_fusion), kind=kOutput, calls=%fused_computation | convolution fusion | flops 67641344 | bytes 1573120 | tf_op jit(solution)/shard_map/dot_general | solution.py:232
  12.8 1.7 %concatenate.24 = bf16[16,32,1024]{2,1,0:T(8,128)(2,1)S(1)} reshape(bf16[128,4096]{1,0:T(8,128)(2,1)} %convolution_convert_fusion) | data formatting | bytes 2097152 | tf_op jit(solution)/shard_map/concatenate | solution.py:239
  14.6 1.1 pad_maximum_fusion.refs_0_
  15.7 24.4 %shard_map.109 = bf16[16,32,1152]{2,1,0:T(8,128)(2,1)} custom-call(bf16[16,32,1152]{2,1,0:T(8,128)(2,1)} %pad_maximum_fusion.refs_0_), custom_call_target="tpu_custom_call" | custom-call | tf_op jit(solution)/shard_map/pallas_call | solution.py:105
  40.2 1.3 slice.19
  41.5 1.3 convert_reduce_fusion
  42.9 2.0 %fusion.70 = f32[512,512]{0,1:S(1)} fusion(bf16[512,1024]{1,0:T(8,128)(2,1)S(1)} %bitcast.122, bf16[1024,512]{0,1:T(8,128)(2,1)} %bitcast.126), kind=kOutput, calls=%fused_computation.98 | convolution fusion | flops 536870912 | bytes 3145728
  45.1 0.8 reshape.292.refs_0_
  45.8 19.3 %shard_map.110 = bf16[256,128]{1,0:T(8,128)(2,1)} custom-call(f32[256,128]{1,0:T(8,128)} %reshape.292.refs_0_), custom_call_target="tpu_custom_call" | custom-call | tf_op jit(solution)/shard_map/pallas_call | solution.py:159
  65.2 0.9 broadcast_in_dim.117
  66.2 2.9 %bitcast_convert_fusion = bf16[512,1024]{1,0:T(8,128)(2,1)} fusion(bf16[8,64,1024]{2,1,0:T(8,128)(2,1)} %param.19, pred[512,8]{0,1:T(8,128)(4,1)S(1)} %iota_compare_fusion.7, bf16[512,64]{0,1:T(8,128)(2,1)S(1)} %copy.46), kind=kOutput, calls=%fused_computation.6 | convolution fusion | flops 537657344 | bytes 2166784 | tf_op jit(solution)/shard_map/dot_general | solution.py:188
  69.1 20.9 %shard_map.111 = bf16[16,32,1024]{2,1,0:T(8,128)(2,1)} custom-call(bf16[16,32,1024]{2,1,0:T(8,128)(2,1)} %bitcast.123), custom_call_target="tpu_custom_call" | custom-call | tf_op jit(solution)/shard_map/pallas_call | solution.py:105
  90.1 1.7 %reshape.294 = bf16[128,4096]{1,0:T(8,128)(2,1)S(1)} reshape(bf16[16,32,1024]{2,1,0:T(8,128)(2,1)} %shard_map.111) | data formatting | bytes 2097152 | tf_op jit(solution)/shard_map/reshape | solution.py:247
  91.8 1.3 fusion.51
  93.1 1.5 %reshape.295 = f32[256,1024]{1,0:T(8,128)S(1)} reshape(f32[64,4096]{1,0:T(8,128)} %fusion.51) | data formatting | bytes 2097152 | tf_op jit(solution)/shard_map/reshape | solution.py:250
  94.8 3.9 %copy.49 = bf16[8,1024,128]{1,2,0:T(8,128)(2,1)} copy(bf16[8,1024,128]{2,1,0:T(8,128)(2,1)} %bitcast.118) | data formatting | bytes 4194304 | tf_op jit(solution)/shard_map/reshape | solution.py:258
  98.8 1.1 multiply_cosine_fusion.1
  100.0 9.6 %fusion.6 = f32[32,8,8,128]{3,1,2,0:T(8,128)S(1)} fusion(f32[256,1024]{1,0:T(8,128)S(1)} %reshape.295, bf16[8,256,1024]{2,1,0:T(8,128)(2,1)} %all-gather.2.cloned.1.call-done, bf16[8,1024,1024]{2,1,0:T(8,128)(2,1)} %bitcast.125), kind=kOutput, calls=%fused_computation.9 | convolution fusion | flops 4295229440 | bytes 23068672 | tf_op jit(solution)/shard_map/ptd,pdo->to/dot_general | solution.py:255
  109.8 2.3 %copy.48 = bf16[8,256,1024]{2,0,1:T(8,128)(2,1)S(1)} copy(bf16[8,256,1024]{2,1,0:T(8,128)(2,1)S(1)} %copy-done.1) | data formatting | bytes 8388608 | tf_op jit(solution)/shard_map/all_gather | solution.py:252
  112.2 4.7 %fusion.13 = f32[64,4,1,128]{3,0,1,2:T(8,128)S(1)} fusion(bf16[8,1024,128]{1,2,0:T(8,128)(2,1)S(1)} %copy-done.2, bf16[64,4,1024,8]{2,3,1,0:T(8,128)(2,1)S(1)} %bitcast.116), kind=kOutput, calls=%fused_computation.21 | convolution fusion | flops 536870912 | bytes 6422528 | tf_op jit(solution)/shard_map/ptd,pdo->to/dot_general | solution.py:255
  116.9 0.6 fusion.53
  117.6 0.5 subtract_convert_fusion
  118.1 2.6 %fusion.69 = (f32[64,4,8]{2,1,0:T(4,128)S(1)}, f32[64,4,1,8,4]{3,4,1,0,2:T(4,128)S(1)}) fusion(bf16[64,4,8,64]{3,2,1,0:T(8,128)(2,1)S(1)} %get-tuple-element.6, bf16[64,4,8,64]{3,2,1,0:T(8,128)(2,1)S(1)} %get-tuple-element.5, bf16[64,4,128,1]{2,0,1,3:T(8,128)(2,1)S(1)} %maximum_bitcast_fusion, pred[4,4]{1,0:T(4,128)(4,1)S(1)} %iota_compare_fusion.8), kind=kOutput, calls=%fused_computation.97 | convolution fusion | flops 3168256 | bytes 630800 | tf_op jit(solution)/shard_map/rskgd,rtkd->rskgt/dot_general | solution.py:41
  120.7 0.9 fusion.68
  122.1 1.0 fusion.31
  123.1 4.8 %fusion.24 = bf16[64,4,128,1]{2,0,1,3:T(8,128)(2,1)S(1)} fusion(bf16[8,1024,128,1]{2,1,0,3:T(8,128)(2,1)S(1)} %bitcast.114, bf16[64,4,1024,8]{2,3,1,0:T(8,128)(2,1)S(1)} %bitcast.117), kind=kOutput, calls=%fused_computation.24 | convolution fusion | flops 536903680 | bytes 6356992 | tf_op jit(solution)/shard_map/ptd,pdo->to/dot_general | solution.py:255
  127.9 0.9 convolution_bitcast_fusion.1
  128.8 0.5 fusion.11
  129.3 0.9 reshape.301
  (39 shorter events, 2.3 us)
Async XLA Ops:
  6.5 116.5 %copy-start = (bf16[8192,128]{1,0:T(8,128)(2,1)S(1)}, bf16[8192,128]{1,0:T(8,128)(2,1)}, u32[]{:S(2)}) copy-start(bf16[8192,128]{1,0:T(8,128)(2,1)} %param.17) | copy-start | bytes 6291460
  6.5 93.4 %all-gather.2.cloned.1.call-start = ((), (), s32[]{:S(2)}) async-start(), calls=%async_computation | async-start | bytes 4718592 | tf_op jit(solution)/shard_map/all_gather | solution.py:252
  91.8 2.9 %copy-start.4 = (s32[64]{0:T(128)S(1)}, s32[64]{0:T(128)}, u32[]{:S(2)}) copy-start(s32[64]{0:T(128)} %param.14) | copy-start | bytes 772
  99.9 9.9 %copy-start.1 = (bf16[8,256,1024]{2,1,0:T(8,128)(2,1)S(1)}, bf16[8,256,1024]{2,1,0:T(8,128)(2,1)}, u32[]{:S(2)}) copy-start(bf16[8,256,1024]{2,1,0:T(8,128)(2,1)} %all-gather.2.cloned.1.call-done) | copy-start | bytes 12582916
  109.8 2.3 %copy-start.2 = (bf16[8,1024,128]{1,2,0:T(8,128)(2,1)S(1)}, bf16[8,1024,128]{1,2,0:T(8,128)(2,1)}, u32[]{:S(2)}) copy-start(bf16[8,1024,128]{1,2,0:T(8,128)(2,1)} %copy.49) | copy-start | bytes 6291460
  117.6 3.1 %copy-start.3 = (bf16[64,64,128]{2,1,0:T(8,128)(2,1)S(1)}, bf16[64,64,128]{2,1,0:T(8,128)(2,1)}, u32[]{:S(2)}) copy-start(bf16[64,64,128]{2,1,0:T(8,128)(2,1)} %param.20) | copy-start | bytes 3145732
  123.0 4.8 %copy-start.5 = (bf16[64,64,128]{2,1,0:T(8,128)(2,1)S(1)}, bf16[64,64,128]{2,1,0:T(8,128)(2,1)}, u32[]{:S(2)}) copy-start(bf16[64,64,128]{2,1,0:T(8,128)(2,1)} %param.21) | copy-start | bytes 3145732
Sparse Core Ops, SparseCore 0:
  9.1 35.7 all-gather.1
where the time goes:
time: 138 us; the launch traced here: 137 us
  Pallas kernels  64.6 us (47%)
  matrix products  31.7 us (23%)
  local copies, waits for them, and re-layouts  19.5 us (14%)
  between operations  13.7 us (10%)
  other arithmetic  7.47 us (5%)
    pallas_call x2, Pallas kernels, exchange(): pl.pallas_call(lambda *refs: exchange_kernel(axis, count, *refs), out_sha...  45.3 us
    pallas_call x1, Pallas kernels, axis_sum(): pl.pallas_call(lambda *refs: sum_kernel(axis, count, *refs), out_shape=ja...  19.3 us
    dot_general x3, matrix products, add_term(): jnp.einsum('ptd,pdo->to', pieces, matrix.reshape(tp_count, part_width, ma...  19.1 us
    reshape x1, local copies, waits for them, and re-layouts, add_term(): matrix.reshape(tp_count, part_width, matrix.shape[1])  3.93 us
    dot_general x1, matrix products, owner_adapter_term(): jnp.dot(spread_rows, up_local.reshape(local_adapters * adapter_rank, quer...  2.94 us
  transfers between devices with their start and end apart: 1, of which 0 were waited for; matrix products, arithmetic and copies ran while one was open for 19% of the time, Pallas kernels for 47%

commit v1 on v0

--- a/solution.py
+++ b/solution.py
@@ -116,7 +116,7 @@
     )(values)
 
 
-def sum_kernel(axis, count, part_ref, total_ref, held, send_sem, recv_sem):
+def sum_kernel(axis, count, part_ref, total_ref, held, first_send, first_recv, second_send, second_recv):
     me = lax.axis_index(axis)
     barrier = pltpu.get_barrier_semaphore()
     for offset in range(1, count):
@@ -127,24 +127,24 @@
     for offset in range(1, count):
         peer = lax.rem(me + offset, count)
         copy = pltpu.make_async_remote_copy(
-            src_ref=part_ref,
+            src_ref=part_ref.at[peer],
             dst_ref=held.at[me],
-            send_sem=send_sem.at[offset],
-            recv_sem=recv_sem.at[offset],
+            send_sem=first_send.at[offset],
+            recv_sem=first_recv.at[offset],
             device_id={axis: peer},
             device_id_type=MESH,
         )
         copy.start()
         outgoing.append(copy)
-    held[me] = part_ref[...]
+    held[me] = part_ref[me]
     for offset in range(1, count):
         outgoing[offset - 1].wait_send()
         source = lax.rem(me + count - offset, count)
         incoming = pltpu.make_async_remote_copy(
-            src_ref=part_ref,
+            src_ref=part_ref.at[source],
             dst_ref=held.at[source],
-            send_sem=send_sem.at[offset],
-            recv_sem=recv_sem.at[offset],
+            send_sem=first_send.at[offset],
+            recv_sem=first_recv.at[offset],
             device_id={axis: source},
             device_id_type=MESH,
         )
@@ -152,22 +152,51 @@
     total = held[0]
     for index in range(1, count):
         total = total + held[index]
-    total_ref[...] = total.astype(total_ref.dtype)
+    total_ref[me] = total.astype(total_ref.dtype)
+    outgoing = []
+    for offset in range(1, count):
+        peer = lax.rem(me + offset, count)
+        copy = pltpu.make_async_remote_copy(
+            src_ref=total_ref.at[me],
+            dst_ref=total_ref.at[me],
+            send_sem=second_send.at[offset],
+            recv_sem=second_recv.at[offset],
+            device_id={axis: peer},
+            device_id_type=MESH,
+        )
+        copy.start()
+        outgoing.append(copy)
+    for offset in range(1, count):
+        outgoing[offset - 1].wait_send()
+        source = lax.rem(me + count - offset, count)
+        incoming = pltpu.make_async_remote_copy(
+            src_ref=total_ref.at[source],
+            dst_ref=total_ref.at[source],
+            send_sem=second_send.at[offset],
+            recv_sem=second_recv.at[offset],
+            device_id={axis: source},
+            device_id_type=MESH,
+        )
+        incoming.wait_recv()
 
 
 def axis_sum(values, axis, count, collective, out_dtype):
-    return pl.pallas_call(
+    chunks = values.reshape(count, -1, 128)
+    summed = pl.pallas_call(
         lambda *refs: sum_kernel(axis, count, *refs),
-        out_shape=jax.ShapeDtypeStruct(values.shape, out_dtype),
+        out_shape=jax.ShapeDtypeStruct(chunks.shape, out_dtype),
         in_specs=[pl.BlockSpec(memory_space=pltpu.VMEM)],
         out_specs=pl.BlockSpec(memory_space=pltpu.VMEM),
         scratch_shapes=[
-            pltpu.VMEM((count,) + values.shape, values.dtype),
+            pltpu.VMEM(chunks.shape, values.dtype),
+            pltpu.SemaphoreType.DMA((count,)),
+            pltpu.SemaphoreType.DMA((count,)),
             pltpu.SemaphoreType.DMA((count,)),
             pltpu.SemaphoreType.DMA((count,)),
         ],
         compiler_params=pltpu.CompilerParams(collective_id=collective, has_side_effects=True),
-    )(values)
+    )(chunks)
+    return summed.reshape(values.shape)
 
 
 def owner_adapter_term(received, slot_ids, down_local, up_local):

time: 138 us -> 132 us (0.957)
  Pallas kernels: 64.6 us -> 59.2 us
    pallas_call x1, Pallas kernels: 19.3 us -> 13.8 us  [axis_sum(): pl.pallas_call(lambda *refs: sum_kernel(axis, count, *refs), out_shape=ja...]
  transfers between devices with their start and end apart: 1 -> 1, of which waited for: 0 -> 0; matrix products, arithmetic and copies ran while one was open for 19% -> 20% of each run, Pallas kernels for 47% -> 45%
where the time goes in v1:
time: 132 us
  Pallas kernels  59.2 us (45%)
  matrix products  31.7 us (24%)
  local copies, waits for them, and re-layouts  19.5 us (15%)
  between operations  13.7 us (10%)
  other arithmetic  7.47 us (6%)
    pallas_call x2, Pallas kernels, exchange(): pl.pallas_call(lambda *refs: exchange_kernel(axis, count, *refs), out_sha...  45.4 us
    dot_general x3, matrix products, add_term(): jnp.einsum('ptd,pdo->to', pieces, matrix.reshape(tp_count, part_width, ma...  19.1 us
    pallas_call x1, Pallas kernels, axis_sum(): pl.pallas_call(lambda *refs: sum_kernel(axis, count, *refs), out_shape=ja...  13.8 us
    reshape x1, local copies, waits for them, and re-layouts, add_term(): matrix.reshape(tp_count, part_width, matrix.shape[1])  3.93 us
    dot_general x1, matrix products, owner_adapter_term(): jnp.dot(spread_rows, up_local.reshape(local_adapters * adapter_rank, quer...  2.94 us
  transfers between devices with their start and end apart: 1, of which 0 were waited for; matrix products, arithmetic and copies ran while one was open for 20% of the time, Pallas kernels for 45%

profile of v1, /device:TPU:1, one launch (start us, length us, event | category | flops | bytes accessed | tf_op | source)
XLA Modules:
  0.0 131.6 jit_solution(16601063003331774470)
XLA Ops:
  6.5 2.1 %all_gather_reshape.3 = bf16[1,256,1024]{2,1,0:T(8,128)(2,1)} reshape(bf16[64,4,1024]{2,1,0:T(4,128)(2,1)} %param.11) | data formatting | bytes 1048576 | tf_op jit(solution)/shard_map/all_gather;reshape | solution.py:281
  8.7 0.8 select_reduce_fusion.1
  10.2 1.2 copy.64
  11.4 1.4 %convolution_convert_fusion = bf16[128,4096]{1,0:T(8,128)(2,1)} fusion(bf16[64,4096]{1,0:T(8,128)(2,1)S(1)} %bitcast.120, s32[64]{0:T(128)S(1)} %multiply_add_fusion), kind=kOutput, calls=%fused_computation | convolution fusion | flops 67641344 | bytes 1573120 | tf_op jit(solution)/shard_map/dot_general | solution.py:261
  12.8 1.7 %concatenate.24 = bf16[16,32,1024]{2,1,0:T(8,128)(2,1)S(1)} reshape(bf16[128,4096]{1,0:T(8,128)(2,1)} %convolution_convert_fusion) | data formatting | bytes 2097152 | tf_op jit(solution)/shard_map/concatenate | solution.py:268
  14.6 1.1 pad_maximum_fusion.refs_0_
  15.7 24.4 %shard_map.109 = bf16[16,32,1152]{2,1,0:T(8,128)(2,1)} custom-call(bf16[16,32,1152]{2,1,0:T(8,128)(2,1)} %pad_maximum_fusion.refs_0_), custom_call_target="tpu_custom_call" | custom-call | tf_op jit(solution)/shard_map/pallas_call | solution.py:105
  40.2 1.3 %slice.19 = bf16[16,32,1024]{2,1,0:T(8,128)(2,1)S(1)} slice(bf16[16,32,1152]{2,1,0:T(8,128)(2,1)} %shard_map.109), slice={[0:16], [0:32], [0:1024]} | slice | bytes 2097152 | tf_op jit(solution)/shard_map/slice | solution.py:272
  41.5 1.3 convert_reduce_fusion
  42.9 2.0 %fusion.70 = f32[512,512]{0,1:S(1)} fusion(bf16[512,1024]{1,0:T(8,128)(2,1)S(1)} %bitcast.122, bf16[1024,512]{0,1:T(8,128)(2,1)} %bitcast.126), kind=kOutput, calls=%fused_computation.98 | convolution fusion | flops 536870912 | bytes 3145728
  45.1 0.8 reshape_reshape.3.refs_0_
  45.8 13.8 %shard_map.110 = bf16[8,32,128]{2,1,0:T(8,128)(2,1)} custom-call(f32[8,32,128]{2,1,0:T(8,128)} %reshape_reshape.3.refs_0_), custom_call_target="tpu_custom_call" | custom-call | tf_op jit(solution)/shard_map/pallas_call | solution.py:185
  59.6 0.9 broadcast_in_dim.117
  60.7 2.9 %bitcast_convert_fusion = bf16[512,1024]{1,0:T(8,128)(2,1)} fusion(bf16[8,64,1024]{2,1,0:T(8,128)(2,1)} %param.19, pred[512,8]{0,1:T(8,128)(4,1)S(1)} %iota_compare_fusion.7, bf16[512,64]{0,1:T(8,128)(2,1)S(1)} %copy.46), kind=kOutput, calls=%fused_computation.6 | convolution fusion | flops 537657344 | bytes 2166784 | tf_op jit(solution)/shard_map/dot_general | solution.py:217
  63.6 21.0 %shard_map.111 = bf16[16,32,1024]{2,1,0:T(8,128)(2,1)} custom-call(bf16[16,32,1024]{2,1,0:T(8,128)(2,1)} %bitcast.123), custom_call_target="tpu_custom_call" | custom-call | tf_op jit(solution)/shard_map/pallas_call | solution.py:105
  84.6 1.7 %reshape.290 = bf16[128,4096]{1,0:T(8,128)(2,1)S(1)} reshape(bf16[16,32,1024]{2,1,0:T(8,128)(2,1)} %shard_map.111) | data formatting | bytes 2097152 | tf_op jit(solution)/shard_map/reshape | solution.py:276
  86.3 1.3 %fusion.51 = f32[64,4096]{1,0:T(8,128)} fusion(bf16[128,4096]{1,0:T(8,128)(2,1)S(1)} %reshape.290, s32[64]{0:T(128)S(1)} %multiply_add_fusion), kind=kOutput, calls=%fused_computation.65 | convolution fusion | flops 67117056 | bytes 2097408 | tf_op jit(solution)/shard_map/dot_general | solution.py:277
  87.7 1.5 %reshape.291 = f32[256,1024]{1,0:T(8,128)S(1)} reshape(f32[64,4096]{1,0:T(8,128)} %fusion.51) | data formatting | bytes 2097152 | tf_op jit(solution)/shard_map/reshape | solution.py:279
  89.3 3.9 %copy.49 = bf16[8,1024,128]{1,2,0:T(8,128)(2,1)} copy(bf16[8,1024,128]{2,1,0:T(8,128)(2,1)} %bitcast.118) | data formatting | bytes 4194304 | tf_op jit(solution)/shard_map/reshape | solution.py:287
  93.3 1.1 multiply_cosine_fusion.1
  94.5 9.6 %fusion.6 = f32[32,8,8,128]{3,1,2,0:T(8,128)S(1)} fusion(f32[256,1024]{1,0:T(8,128)S(1)} %reshape.291, bf16[8,256,1024]{2,1,0:T(8,128)(2,1)} %all-gather.2.cloned.1.call-done, bf16[8,1024,1024]{2,1,0:T(8,128)(2,1)} %bitcast.125), kind=kOutput, calls=%fused_computation.9 | convolution fusion | flops 4295229440 | bytes 23068672 | tf_op jit(solution)/shard_map/ptd,pdo->to/dot_general | solution.py:284
  104.4 2.3 %copy.48 = bf16[8,256,1024]{2,0,1:T(8,128)(2,1)S(1)} copy(bf16[8,256,1024]{2,1,0:T(8,128)(2,1)S(1)} %copy-done.1) | data formatting | bytes 8388608 | tf_op jit(solution)/shard_map/all_gather | solution.py:281
  106.7 4.7 %fusion.13 = f32[64,4,1,128]{3,0,1,2:T(8,128)S(1)} fusion(bf16[8,1024,128]{1,2,0:T(8,128)(2,1)S(1)} %copy-done.2, bf16[64,4,1024,8]{2,3,1,0:T(8,128)(2,1)S(1)} %bitcast.116), kind=kOutput, calls=%fused_computation.21 | convolution fusion | flops 536870912 | bytes 6422528 | tf_op jit(solution)/shard_map/ptd,pdo->to/dot_general | solution.py:284
  111.4 0.6 fusion.53
  112.1 0.5 subtract_convert_fusion
  112.6 2.6 %fusion.69 = (f32[64,4,8]{2,1,0:T(4,128)S(1)}, f32[64,4,1,8,4]{3,4,1,0,2:T(4,128)S(1)}) fusion(bf16[64,4,8,64]{3,2,1,0:T(8,128)(2,1)S(1)} %get-tuple-element.6, bf16[64,4,8,64]{3,2,1,0:T(8,128)(2,1)S(1)} %get-tuple-element.5, bf16[64,4,128,1]{2,0,1,3:T(8,128)(2,1)S(1)} %maximum_bitcast_fusion, pred[4,4]{1,0:T(4,128)(4,1)S(1)} %iota_compare_fusion.8), kind=kOutput, calls=%fused_computation.97 | convolution fusion | flops 3168256 | bytes 630800 | tf_op jit(solution)/shard_map/rskgd,rtkd->rskgt/dot_general | solution.py:41
  115.2 0.9 fusion.68
  116.6 1.0 fusion.31
  117.6 4.8 %fusion.24 = bf16[64,4,128,1]{2,0,1,3:T(8,128)(2,1)S(1)} fusion(bf16[8,1024,128,1]{2,1,0,3:T(8,128)(2,1)S(1)} %bitcast.114, bf16[64,4,1024,8]{2,3,1,0:T(8,128)(2,1)S(1)} %bitcast.117), kind=kOutput, calls=%fused_computation.24 | convolution fusion | flops 536903680 | bytes 6356992 | tf_op jit(solution)/shard_map/ptd,pdo->to/dot_general | solution.py:284
  122.4 0.9 convolution_bitcast_fusion.1
  123.4 0.5 fusion.11
  123.9 0.9 reshape.297
  (39 shorter events, 2.3 us)
Async XLA Ops:
  6.5 111.0 %copy-start = (bf16[8192,128]{1,0:T(8,128)(2,1)S(1)}, bf16[8192,128]{1,0:T(8,128)(2,1)}, u32[]{:S(2)}) copy-start(bf16[8192,128]{1,0:T(8,128)(2,1)} %param.17) | copy-start | bytes 6291460
  6.5 87.9 %all-gather.2.cloned.1.call-start = ((), (), s32[]{:S(2)}) async-start(), calls=%async_computation | async-start | bytes 4718592 | tf_op jit(solution)/shard_map/all_gather | solution.py:281
  86.3 2.9 %copy-start.4 = (s32[64]{0:T(128)S(1)}, s32[64]{0:T(128)}, u32[]{:S(2)}) copy-start(s32[64]{0:T(128)} %param.14) | copy-start | bytes 772
  94.5 9.9 %copy-start.1 = (bf16[8,256,1024]{2,1,0:T(8,128)(2,1)S(1)}, bf16[8,256,1024]{2,1,0:T(8,128)(2,1)}, u32[]{:S(2)}) copy-start(bf16[8,256,1024]{2,1,0:T(8,128)(2,1)} %all-gather.2.cloned.1.call-done) | copy-start | bytes 12582916
  104.4 2.3 %copy-start.2 = (bf16[8,1024,128]{1,2,0:T(8,128)(2,1)S(1)}, bf16[8,1024,128]{1,2,0:T(8,128)(2,1)}, u32[]{:S(2)}) copy-start(bf16[8,1024,128]{1,2,0:T(8,128)(2,1)} %copy.49) | copy-start | bytes 6291460
  112.1 3.1 %copy-start.3 = (bf16[64,64,128]{2,1,0:T(8,128)(2,1)S(1)}, bf16[64,64,128]{2,1,0:T(8,128)(2,1)}, u32[]{:S(2)}) copy-start(bf16[64,64,128]{2,1,0:T(8,128)(2,1)} %param.20) | copy-start | bytes 3145732
  117.6 4.8 %copy-start.5 = (bf16[64,64,128]{2,1,0:T(8,128)(2,1)S(1)}, bf16[64,64,128]{2,1,0:T(8,128)(2,1)}, u32[]{:S(2)}) copy-start(bf16[64,64,128]{2,1,0:T(8,128)(2,1)} %param.21) | copy-start | bytes 3145732
Sparse Core Ops, SparseCore 0:
  9.1 35.7 all-gather.1

commit v2 on v1

--- a/solution.py
+++ b/solution.py
@@ -114,6 +114,105 @@
         ],
         compiler_params=pltpu.CompilerParams(collective_id=collective, has_side_effects=True),
     )(values)
+
+
+def exchange_project_kernel(
+    axis, count, send_ref, pieces_ref, wq_hbm, wk_ref, wv_ref,
+    got_ref, q_ref, k_ref, v_ref,
+    wq_buf, send_sem, recv_sem, local_sem, wq_sem,
+):
+    me = lax.axis_index(axis)
+    barrier = pltpu.get_barrier_semaphore()
+    for offset in range(1, count):
+        peer = lax.rem(me + offset, count)
+        pl.semaphore_signal(barrier, inc=1, device_id={axis: peer}, device_id_type=MESH)
+    pl.semaphore_wait(barrier, count - 1)
+    local = pltpu.make_async_copy(send_ref.at[me], got_ref.at[me], local_sem)
+    local.start()
+    outgoing = []
+    for offset in range(1, count):
+        peer = lax.rem(me + offset, count)
+        copy = pltpu.make_async_remote_copy(
+            src_ref=send_ref.at[peer],
+            dst_ref=got_ref.at[me],
+            send_sem=send_sem.at[offset],
+            recv_sem=recv_sem.at[offset],
+            device_id={axis: peer},
+            device_id_type=MESH,
+        )
+        copy.start()
+        outgoing.append(copy)
+
+    piece_count, unused_item, piece_width = pieces_ref.shape
+
+    def chunk_copy(index, slot):
+        return pltpu.make_async_copy(
+            wq_hbm.at[pl.ds(pl.multiple_of(index * piece_width, piece_width), piece_width)],
+            wq_buf.at[slot],
+            wq_sem.at[slot],
+        )
+
+    chunk_copy(0, 0).start()
+    q_ref[...] = jnp.zeros_like(q_ref)
+    k_ref[...] = jnp.zeros_like(k_ref)
+    v_ref[...] = jnp.zeros_like(v_ref)
+
+    def project(index, carry):
+        slot = lax.rem(index, 2)
+        chunk_copy(index, slot).wait()
+
+        @pl.when(index + 1 < piece_count)
+        def _():
+            chunk_copy(index + 1, 1 - slot).start()
+
+        rows = pl.ds(pl.multiple_of(index * piece_width, piece_width), piece_width)
+        piece = pieces_ref[index]
+        q_ref[...] += jnp.dot(piece, wq_buf[slot], preferred_element_type=jnp.float32)
+        k_ref[...] += jnp.dot(piece, wk_ref[rows, :], preferred_element_type=jnp.float32)
+        v_ref[...] += jnp.dot(piece, wv_ref[rows, :], preferred_element_type=jnp.float32)
+        return carry
+
+    lax.fori_loop(0, piece_count, project, 0)
+
+    for offset in range(1, count):
+        outgoing[offset - 1].wait_send()
+        source = lax.rem(me + count - offset, count)
+        incoming = pltpu.make_async_remote_copy(
+            src_ref=send_ref.at[source],
+            dst_ref=got_ref.at[source],
+            send_sem=send_sem.at[offset],
+            recv_sem=recv_sem.at[offset],
+            device_id={axis: source},
+            device_id_type=MESH,
+        )
+        incoming.wait_recv()
+    local.wait()
+
+
+def exchange_project(values, pieces, w_query, w_key, w_value, axis, count, collective):
+    piece_count, token_count, piece_width = pieces.shape
+    vmem = pl.BlockSpec(memory_space=pltpu.VMEM)
+    return pl.pallas_call(
+        lambda *refs: exchange_project_kernel(axis, count, *refs),
+        out_shape=(
+            jax.ShapeDtypeStruct(values.shape, values.dtype),
+            jax.ShapeDtypeStruct((token_count, w_query.shape[1]), jnp.float32),
+            jax.ShapeDtypeStruct((token_count, w_key.shape[1]), jnp.float32),
+            jax.ShapeDtypeStruct((token_count, w_value.shape[1]), jnp.float32),
+        ),
+        in_specs=[vmem, vmem, pl.BlockSpec(memory_space=pl.ANY), vmem, vmem],
+        out_specs=(vmem, vmem, vmem, vmem),
+        scratch_shapes=[
+            pltpu.VMEM((2, piece_width, w_query.shape[1]), w_query.dtype),
+            pltpu.SemaphoreType.DMA((count,)),
+            pltpu.SemaphoreType.DMA((count,)),
+            pltpu.SemaphoreType.DMA(()),
+            pltpu.SemaphoreType.DMA((2,)),
+        ],
+        compiler_params=pltpu.CompilerParams(
+            collective_id=collective, has_side_effects=True, vmem_limit_bytes=60 * 1024 * 1024
+        ),
+    )(values, pieces, w_query, w_key, w_value)
 
 
 def sum_kernel(axis, count, part_ref, total_ref, held, first_send, first_recv, second_send, second_recv):
@@ -272,25 +371,14 @@
     got_tokens = got[:, :, :part_width]
     got_ids = got[:, :, part_width].astype(jnp.int32)
     owner_out = owner_adapter_term(got_tokens, got_ids, pooled_down_weights, pool_up)
-    back = exchange(owner_out, "grp", group_count, 1)
+    pieces = lax.all_gather(tokens.reshape(count_of_tokens, part_width), "tp", axis=0, tiled=False)
+    back, base_query_rows, key_base, value_base = exchange_project(
+        owner_out, pieces, w_query, w_key, w_value, "grp", group_count, 1
+    )
     back = back.reshape(group_count * CAP, step_count * query_width)
     adapter_output = jnp.dot(
         jnp.transpose(place), back, preferred_element_type=jnp.float32
     ).reshape(count_of_tokens, query_width)
-
-    pieces = lax.all_gather(tokens.reshape(count_of_tokens, part_width), "tp", axis=0, tiled=False)
-
-    def add_term(matrix):
-        return jnp.einsum(
-            "ptd,pdo->to",
-            pieces,
-            matrix.reshape(tp_count, part_width, matrix.shape[1]),
-            preferred_element_type=jnp.float32,
-        )
-
-    base_query_rows = add_term(w_query)
-    key_base = add_term(w_key)
-    value_base = add_term(w_value)
     base_query_rows = base_query_rows + adapter_output
     position = lengths[:, None] + jnp.arange(step_count, dtype=jnp.int32)[None, :]
     queries = rotate(base_query_rows.reshape(row_count, step_count, q_local, HD), position)

time: 132 us -> 105 us (0.80)
  matrix products: 31.7 us -> 9.47 us
  local copies, waits for them, and re-layouts: 19.5 us -> 10.8 us
  Pallas kernels: 59.2 us -> 62.4 us
    pallas_call x0 -> x1, Pallas kernels: none -> 24.2 us  [exchange_project(): pl.pallas_call(lambda *refs: exchange_project_kernel(axis, count, *refs),...]
    pallas_call x2 -> x1, Pallas kernels: 45.4 us -> 24.4 us  [exchange(): pl.pallas_call(lambda *refs: exchange_kernel(axis, count, *refs), out_sha...]
    dot_general x3 -> x0, matrix products: 19.1 us -> none  [add_term(): jnp.einsum('ptd,pdo->to', pieces, matrix.reshape(tp_count, part_width, ma...]
    reshape x1 -> x0, local copies, waits for them, and re-layouts: 3.93 us -> none  [add_term(): matrix.reshape(tp_count, part_width, matrix.shape[1])]
    all_gather x1 -> x0, local copies, waits for them, and re-layouts: 2.33 us -> none  [body(): lax.all_gather(tokens.reshape(count_of_tokens, part_width), 'tp', axis=0,...]
    unnamed x0 -> x1, other arithmetic: none -> 1.4 us
    slice x1 -> x2, local copies, waits for them, and re-layouts: 1.34 us -> 0.01 us  [body(): got_tokens = got[:, :, :part_width]]
    unnamed x14 -> x16, local copies, waits for them, and re-layouts: 1.46 us -> 2.72 us
  transfers between devices with their start and end apart: 1 -> 1, of which waited for: 0 -> 0; matrix products, arithmetic and copies ran while one was open for 20% -> 12% of each run, Pallas kernels for 45% -> 37%
where the time goes in v2:
time: 105 us
  Pallas kernels  62.4 us (59%)
  between operations  13.7 us (13%)
  local copies, waits for them, and re-layouts  10.8 us (10%)
  matrix products  9.47 us (9%)
  other arithmetic  8.32 us (8%)
    pallas_call x1, Pallas kernels, exchange(): pl.pallas_call(lambda *refs: exchange_kernel(axis, count, *refs), out_sha...  24.4 us
    pallas_call x1, Pallas kernels, exchange_project(): pl.pallas_call(lambda *refs: exchange_project_kernel(axis, count, *refs),...  24.2 us
    pallas_call x1, Pallas kernels, axis_sum(): pl.pallas_call(lambda *refs: sum_kernel(axis, count, *refs), out_shape=ja...  13.8 us
    dot_general x1, matrix products, owner_adapter_term(): jnp.dot(spread_rows, up_local.reshape(local_adapters * adapter_rank, quer...  2.94 us
    unnamed x16, local copies, waits for them, and re-layouts  2.72 us
    dot_general x1, matrix products, attend(): jnp.einsum('rskgd,rtkd->rskgt', queries, key_new, preferred_element_type=...  2.58 us
  transfers between devices with their start and end apart: 1, of which 0 were waited for; matrix products, arithmetic and copies ran while one was open for 12% of the time, Pallas kernels for 37%

profile of v2, /device:TPU:1, one launch (start us, length us, event | category | flops | bytes accessed | tf_op | source)
XLA Modules:
  0.0 104.7 jit_solution(15056275493257379529)
XLA Ops:
  6.5 2.0 %all_gather_reshape.3 = bf16[1,256,1024]{2,1,0:T(8,128)(2,1)} reshape(bf16[64,4,1024]{2,1,0:T(4,128)(2,1)} %param.11) | data formatting | bytes 1048576 | tf_op jit(solution)/shard_map/all_gather;reshape | solution.py:374
  8.6 0.8 select_reduce_fusion.1
  9.5 0.2 convert_reduce_fusion.1
  9.7 0.1 fusion.7
  10.1 1.2 %copy.28 = bf16[8,8,4,1024]{3,1,2,0:T(8,128)(2,1)S(1)} copy(bf16[8,8,4,1024]{3,2,1,0:T(4,128)(2,1)} %bitcast.92) | data formatting | bytes 1048576
  11.3 0.4 convolution_convert_fusion
  11.8 0.7 concatenate.24
  12.6 1.1 %pad_maximum_fusion.refs_0_ = bf16[16,32,1152]{2,1,0:T(8,128)(2,1)} fusion(bf16[16,32,128]{2,1,0:T(8,128)(2,1)S(1)} %broadcast_in_dim.114, bf16[16,32,1024]{2,1,0:T(8,128)(2,1)S(1)} %concatenate.24), kind=kLoop, calls=%fused_computation.12 | loop fusion | flops 2359296 | bytes 2359296 | tf_op jit(solution)/shard_map/concatenate | solution.py:367
  13.7 24.4 %shard_map.109 = bf16[16,32,1152]{2,1,0:T(8,128)(2,1)} custom-call(bf16[16,32,1152]{2,1,0:T(8,128)(2,1)} %pad_maximum_fusion.refs_0_), custom_call_target="tpu_custom_call" | custom-call | tf_op jit(solution)/shard_map/pallas_call | solution.py:105
  38.1 1.3 %copy-done.1 = bf16[16,32,1152]{2,1,0:T(8,128)(2,1)S(1)} copy-done((bf16[16,32,1152]{2,1,0:T(8,128)(2,1)S(1)}, bf16[16,32,1152]{2,1,0:T(8,128)(2,1)}, u32[]{:S(2)}) %copy-start.1) | copy-done | bytes 1179672
  39.4 0.3 convert_reduce_fusion
  39.8 0.7 fusion.49
  40.9 0.8 reshape_reshape.3.refs_0_
  41.6 13.8 %shard_map.110 = bf16[8,32,128]{2,1,0:T(8,128)(2,1)} custom-call(f32[8,32,128]{2,1,0:T(8,128)} %reshape_reshape.3.refs_0_), custom_call_target="tpu_custom_call" | custom-call | tf_op jit(solution)/shard_map/pallas_call | solution.py:284
  55.4 0.9 broadcast_in_dim.117
  56.7 1.1 %multiply_cosine_fusion.1 = (f32[64,4,64]{2,1,0:T(4,128)S(1)}, f32[64,4,64]{2,1,0:T(4,128)S(1)}) fusion(f32[64]{0:T(128)S(1)} %multiply_exponential_fusion, f32[64,4]{1,0:T(8,128)S(1)} %add_convert_fusion.1), kind=kLoop, calls=%fused_computation.41 | loop fusion | flops 16384 | bytes 132352 | tf_op jit(solution)/shard_map/cos | solution.py:25
  57.8 2.9 %bitcast_convert_fusion = bf16[512,1024]{1,0:T(8,128)(2,1)} fusion(bf16[8,64,1024]{2,1,0:T(8,128)(2,1)} %param.19, pred[512,8]{0,1:T(8,128)(4,1)S(1)} %iota_compare_fusion.7, bf16[512,64]{0,1:T(8,128)(2,1)S(1)} %copy.23), kind=kOutput, calls=%fused_computation.1 | convolution fusion | flops 537657344 | bytes 2166784 | tf_op jit(solution)/shard_map/dot_general | solution.py:316
  60.7 24.2 %shard_map.111 = (bf16[16,32,1024]{2,1,0:T(8,128)(2,1)}, f32[256,1024]{1,0:T(8,128)}, f32[256,128]{1,0:T(8,128)}, f32[256,128]{1,0:T(8,128)}) custom-call(bf16[16,32,1024]{2,1,0:T(8,128)(2,1)} %bitcast.94, bf16[8,256,1024]{2,1,0:T(8,128)(2,1)} %all-gather.2.cloned.1.call-done.refs_1_, bf16[8192,1024]{1,0:T(8,128)(2,1)} %refs_2_.1, ...), custom_call_target="tpu_custom_call" | custom-call | tf_op jit(solution)/shard_map/pallas_call | solution.py:195
  84.9 1.7 %reshape.278 = bf16[128,4096]{1,0:T(8,128)(2,1)S(1)} reshape(bf16[16,32,1024]{2,1,0:T(8,128)(2,1)} %get-tuple-element.10) | data formatting | bytes 2097152 | tf_op jit(solution)/shard_map/reshape | solution.py:378
  86.6 0.4 fusion.30
  87.0 0.3 reshape.279
  87.3 1.4 %add_bitcast_fusion = f32[32,8,8,128]{3,1,2,0:T(8,128)S(1)} fusion(f32[256,1024]{1,0:T(8,128)} %get-tuple-element.9, f32[256,1024]{1,0:T(8,128)S(1)} %reshape.279), kind=kLoop, calls=%fused_computation.22 | loop fusion | flops 262144 | bytes 3145728
  88.7 0.2 copy.29
  88.9 1.2 %fusion.32 = (bf16[64,4,64]{2,1,0:T(4,128)(2,1)S(1)}, bf16[64,4,64]{2,1,0:T(4,128)(2,1)S(1)}) fusion(f32[64,4,1,128]{3,1,0,2:T(4,128)S(1)} %bitcast.96, f32[64]{0:T(128)S(1)} %multiply_exponential_fusion, f32[64,4]{1,0:T(8,128)S(1)} %add_convert_fusion.1), kind=kLoop, calls=%fused_computation.56 | loop fusion | flops 147456 | bytes 197888 | tf_op jit(solution)/shard_map/concatenate | solution.py:29
  90.1 0.5 subtract_convert_fusion
  90.7 0.9 fusion.47
  91.5 2.6 %fusion.48 = (f32[64,4,8]{2,1,0:T(4,128)S(1)}, f32[64,4,1,8,4]{3,4,1,0,2:T(4,128)S(1)}) fusion(bf16[64,4,8,64]{3,2,1,0:T(8,128)(2,1)S(1)} %get-tuple-element.14, bf16[64,4,8,64]{3,2,1,0:T(8,128)(2,1)S(1)} %get-tuple-element.13, bf16[64,4,64]{2,1,0:T(4,128)(2,1)S(1)} %get-tuple-element.16, bf16[64,4,64]{2,1,0:T(4,128)(2,1)S(1)} %get-tuple-element.15, ...), kind=kOutput, calls=%fused_computation.86 | convolution fusion | flops 3299328 | bytes 630800 | tf_op jit(solution)/shard_map/rskgd,rtkd->rskgt/dot_general | solution.py:41
  94.2 0.5 fusion.15
  94.7 0.8 fusion.10
  95.5 0.9 convolution_bitcast_fusion
  96.4 0.5 fusion.4
  96.9 0.9 reshape.284
  (37 shorter events, 1.2 us)
Async XLA Ops:
  6.5 33.3 %copy-start = (bf16[8,1024,64]{1,2,0:T(8,128)(2,1)S(1)}, bf16[8,1024,64]{1,2,0:T(8,128)(2,1)}, u32[]{:S(2)}) copy-start(bf16[8,1024,64]{1,2,0:T(8,128)(2,1)} %param.18) | copy-start | bytes 3145732
  6.5 54.2 %all-gather.2.cloned.1.call-start = ((), (), s32[]{:S(2)}) async-start(), calls=%async_computation | async-start | bytes 4718592 | tf_op jit(solution)/shard_map/all_gather | solution.py:374
  38.1 1.3 %copy-start.1 = (bf16[16,32,1152]{2,1,0:T(8,128)(2,1)S(1)}, bf16[16,32,1152]{2,1,0:T(8,128)(2,1)}, u32[]{:S(2)}) copy-start(bf16[16,32,1152]{2,1,0:T(8,128)(2,1)} %shard_map.109) | copy-start | bytes 3538948
  38.1 1.7 %slice-start = ((bf16[16,32,1152]{2,1,0:T(8,128)(2,1)}), bf16[16,32,1024]{2,1,0:T(8,128)(2,1)S(1)}, s32[]{:S(2)}) async-start(bf16[16,32,1152]{2,1,0:T(8,128)(2,1)} %shard_map.109), calls=%async_computation.1 | async-start | bytes 2097152 | tf_op jit(solution)/shard_map/slice | solution.py:371
  40.6 15.9 %copy-start.5 = (s32[64]{0:T(128)S(1)}, s32[64]{0:T(128)}, u32[]{:S(2)}) copy-start(s32[64]{0:T(128)} %param.14) | copy-start | bytes 772
  87.3 1.6 %copy-start.3 = (f32[256,128]{1,0:T(8,128)S(1)}, f32[256,128]{1,0:T(8,128)}, u32[]{:S(2)}) copy-start(f32[256,128]{1,0:T(8,128)} %get-tuple-element.11) | copy-start | bytes 393220
  88.9 1.7 %copy-start.2 = (bf16[64,64,128]{2,1,0:T(8,128)(2,1)S(1)}, bf16[64,64,128]{2,1,0:T(8,128)(2,1)}, u32[]{:S(2)}) copy-start(bf16[64,64,128]{2,1,0:T(8,128)(2,1)} %param.20) | copy-start | bytes 3145732
  91.5 3.9 %copy-start.4 = (f32[256,128]{1,0:T(8,128)S(1)}, f32[256,128]{1,0:T(8,128)}, u32[]{:S(2)}) copy-start(f32[256,128]{1,0:T(8,128)} %get-tuple-element.12) | copy-start | bytes 393220
  91.5 3.9 %copy-start.6 = (bf16[64,64,128]{2,1,0:T(8,128)(2,1)S(1)}, bf16[64,64,128]{2,1,0:T(8,128)(2,1)}, u32[]{:S(2)}) copy-start(bf16[64,64,128]{2,1,0:T(8,128)(2,1)} %param.21) | copy-start | bytes 3145732
Sparse Core Ops, SparseCore 0:
  9.1 35.7 all-gather.1

commit v3 on v2

--- a/solution.py
+++ b/solution.py
@@ -64,18 +64,40 @@
     return combined.astype(jnp.bfloat16)
 
 
+TORUS_ORDER = (
+    (0, 1), (1, 0), (0, 3), (3, 0), (1, 1), (3, 3), (1, 3), (3, 1),
+    (0, 2), (2, 0), (2, 1), (1, 2), (2, 3), (3, 2), (2, 2),
+)
+
+
+def peer_offsets(count):
+    if count == 16:
+        def shifted(me, dz, dy):
+            return lax.rem(me // 4 + dz, 4) * 4 + lax.rem(lax.rem(me, 4) + dy, 4)
+
+        return [
+            (lambda me, a=dz, b=dy: shifted(me, a, b), lambda me, a=dz, b=dy: shifted(me, 4 - a, 4 - b))
+            for dz, dy in TORUS_ORDER
+        ]
+    return [
+        (lambda me, d=offset: lax.rem(me + d, count), lambda me, d=offset: lax.rem(me + count - d, count))
+        for offset in range(1, count)
+    ]
+
+
 def exchange_kernel(axis, count, send_ref, got_ref, send_sem, recv_sem, local_sem):
     me = lax.axis_index(axis)
     barrier = pltpu.get_barrier_semaphore()
-    for offset in range(1, count):
-        peer = lax.rem(me + offset, count)
+    offsets = peer_offsets(count)
+    for offset in range(1, count):
+        peer = offsets[offset - 1][0](me)
         pl.semaphore_signal(barrier, inc=1, device_id={axis: peer}, device_id_type=MESH)
     pl.semaphore_wait(barrier, count - 1)
     local = pltpu.make_async_copy(send_ref.at[me], got_ref.at[me], local_sem)
     local.start()
     outgoing = []
     for offset in range(1, count):
-        peer = lax.rem(me + offset, count)
+        peer = offsets[offset - 1][0](me)
         copy = pltpu.make_async_remote_copy(
             src_ref=send_ref.at[peer],
             dst_ref=got_ref.at[me],
@@ -88,7 +110,7 @@
         outgoing.append(copy)
     for offset in range(1, count):
         outgoing[offset - 1].wait_send()
-        source = lax.rem(me + count - offset, count)
+        source = offsets[offset - 1][1](me)
         incoming = pltpu.make_async_remote_copy(
             src_ref=send_ref.at[source],
             dst_ref=got_ref.at[source],
@@ -123,15 +145,16 @@
 ):
     me = lax.axis_index(axis)
     barrier = pltpu.get_barrier_semaphore()
-    for offset in range(1, count):
-        peer = lax.rem(me + offset, count)
+    offsets = peer_offsets(count)
+    for offset in range(1, count):
+        peer = offsets[offset - 1][0](me)
         pl.semaphore_signal(barrier, inc=1, device_id={axis: peer}, device_id_type=MESH)
     pl.semaphore_wait(barrier, count - 1)
     local = pltpu.make_async_copy(send_ref.at[me], got_ref.at[me], local_sem)
     local.start()
     outgoing = []
     for offset in range(1, count):
-        peer = lax.rem(me + offset, count)
+        peer = offsets[offset - 1][0](me)
         copy = pltpu.make_async_remote_copy(
             src_ref=send_ref.at[peer],
             dst_ref=got_ref.at[me],
@@ -176,7 +199,7 @@
 
     for offset in range(1, count):
         outgoing[offset - 1].wait_send()
-        source = lax.rem(me + count - offset, count)
+        source = offsets[offset - 1][1](me)
         incoming = pltpu.make_async_remote_copy(
             src_ref=send_ref.at[source],
             dst_ref=got_ref.at[source],

time: 105 us -> 104 us (level)
  Pallas kernels: 62.4 us -> 61 us
    pallas_call x1, Pallas kernels: 24.2 us -> 22.9 us  [exchange_project(): pl.pallas_call(lambda *refs: exchange_project_kernel(axis, count, *refs),...]
where the time goes in v3:
time: 104 us; the launch traced here: 103 us
  Pallas kernels  61 us (59%)
  between operations  13.7 us (13%)
  local copies, waits for them, and re-layouts  10.8 us (10%)
  matrix products  9.47 us (9%)
  other arithmetic  8.32 us (8%)
    pallas_call x1, Pallas kernels, exchange(): pl.pallas_call(lambda *refs: exchange_kernel(axis, count, *refs), out_sha...  24.2 us
    pallas_call x1, Pallas kernels, exchange_project(): pl.pallas_call(lambda *refs: exchange_project_kernel(axis, count, *refs),...  22.9 us
    pallas_call x1, Pallas kernels, axis_sum(): pl.pallas_call(lambda *refs: sum_kernel(axis, count, *refs), out_shape=ja...  13.9 us
    dot_general x1, matrix products, owner_adapter_term(): jnp.dot(spread_rows, up_local.reshape(local_adapters * adapter_rank, quer...  2.94 us
    unnamed x16, local copies, waits for them, and re-layouts  2.73 us
    dot_general x1, matrix products, attend(): jnp.einsum('rskgd,rtkd->rskgt', queries, key_new, preferred_element_type=...  2.58 us
  transfers between devices with their start and end apart: 1, of which 0 were waited for; matrix products, arithmetic and copies ran while one was open for 12% of the time, Pallas kernels for 37%

profile of v3, /device:TPU:1, one launch (start us, length us, event | category | flops | bytes accessed | tf_op | source)
XLA Modules:
  0.0 103.3 jit_solution(11437475336284250719)
XLA Ops:
  6.5 2.0 %all_gather_reshape.3 = bf16[1,256,1024]{2,1,0:T(8,128)(2,1)} reshape(bf16[64,4,1024]{2,1,0:T(4,128)(2,1)} %param.11) | data formatting | bytes 1048576 | tf_op jit(solution)/shard_map/all_gather;reshape | solution.py:397
  8.6 0.8 select_reduce_fusion.1
  9.5 0.2 convert_reduce_fusion.1
  9.7 0.1 fusion.7
  10.1 1.2 %copy.28 = bf16[8,8,4,1024]{3,1,2,0:T(8,128)(2,1)S(1)} copy(bf16[8,8,4,1024]{3,2,1,0:T(4,128)(2,1)} %bitcast.92) | data formatting | bytes 1048576
  11.3 0.4 convolution_convert_fusion
  11.8 0.7 concatenate.24
  12.6 1.1 %pad_maximum_fusion.refs_0_ = bf16[16,32,1152]{2,1,0:T(8,128)(2,1)} fusion(bf16[16,32,128]{2,1,0:T(8,128)(2,1)S(1)} %broadcast_in_dim.114, bf16[16,32,1024]{2,1,0:T(8,128)(2,1)S(1)} %concatenate.24), kind=kLoop, calls=%fused_computation.12 | loop fusion | flops 2359296 | bytes 2359296 | tf_op jit(solution)/shard_map/concatenate | solution.py:390
  13.7 24.2 %shard_map.109 = bf16[16,32,1152]{2,1,0:T(8,128)(2,1)} custom-call(bf16[16,32,1152]{2,1,0:T(8,128)(2,1)} %pad_maximum_fusion.refs_0_), custom_call_target="tpu_custom_call" | custom-call | tf_op jit(solution)/shard_map/pallas_call | solution.py:127
  38.0 1.3 %copy-done.1 = bf16[16,32,1152]{2,1,0:T(8,128)(2,1)S(1)} copy-done((bf16[16,32,1152]{2,1,0:T(8,128)(2,1)S(1)}, bf16[16,32,1152]{2,1,0:T(8,128)(2,1)}, u32[]{:S(2)}) %copy-start.1) | copy-done | bytes 1179672
  39.2 0.3 convert_reduce_fusion
  39.7 0.7 fusion.49
  40.7 0.8 reshape_reshape.3.refs_0_
  41.5 13.9 %shard_map.110 = bf16[8,32,128]{2,1,0:T(8,128)(2,1)} custom-call(f32[8,32,128]{2,1,0:T(8,128)} %reshape_reshape.3.refs_0_), custom_call_target="tpu_custom_call" | custom-call | tf_op jit(solution)/shard_map/pallas_call | solution.py:307
  55.3 0.9 broadcast_in_dim.117
  56.6 1.1 %multiply_cosine_fusion.1 = (f32[64,4,64]{2,1,0:T(4,128)S(1)}, f32[64,4,64]{2,1,0:T(4,128)S(1)}) fusion(f32[64]{0:T(128)S(1)} %multiply_exponential_fusion, f32[64,4]{1,0:T(8,128)S(1)} %add_convert_fusion.1), kind=kLoop, calls=%fused_computation.41 | loop fusion | flops 16384 | bytes 132352 | tf_op jit(solution)/shard_map/cos | solution.py:25
  57.7 2.9 %bitcast_convert_fusion = bf16[512,1024]{1,0:T(8,128)(2,1)} fusion(bf16[8,64,1024]{2,1,0:T(8,128)(2,1)} %param.19, pred[512,8]{0,1:T(8,128)(4,1)S(1)} %iota_compare_fusion.7, bf16[512,64]{0,1:T(8,128)(2,1)S(1)} %copy.23), kind=kOutput, calls=%fused_computation.1 | convolution fusion | flops 537657344 | bytes 2166784 | tf_op jit(solution)/shard_map/dot_general | solution.py:339
  60.6 22.9 %shard_map.111 = (bf16[16,32,1024]{2,1,0:T(8,128)(2,1)}, f32[256,1024]{1,0:T(8,128)}, f32[256,128]{1,0:T(8,128)}, f32[256,128]{1,0:T(8,128)}) custom-call(bf16[16,32,1024]{2,1,0:T(8,128)(2,1)} %bitcast.94, bf16[8,256,1024]{2,1,0:T(8,128)(2,1)} %all-gather.2.cloned.1.call-done.refs_1_, bf16[8192,1024]{1,0:T(8,128)(2,1)} %refs_2_.1, ...), custom_call_target="tpu_custom_call" | custom-call | tf_op jit(solution)/shard_map/pallas_call | solution.py:218
  83.5 1.7 %reshape.278 = bf16[128,4096]{1,0:T(8,128)(2,1)S(1)} reshape(bf16[16,32,1024]{2,1,0:T(8,128)(2,1)} %get-tuple-element.10) | data formatting | bytes 2097152 | tf_op jit(solution)/shard_map/reshape | solution.py:401
  85.2 0.4 fusion.30
  85.5 0.3 reshape.279
  85.9 1.4 %add_bitcast_fusion = f32[32,8,8,128]{3,1,2,0:T(8,128)S(1)} fusion(f32[256,1024]{1,0:T(8,128)} %get-tuple-element.9, f32[256,1024]{1,0:T(8,128)S(1)} %reshape.279), kind=kLoop, calls=%fused_computation.22 | loop fusion | flops 262144 | bytes 3145728
  87.3 0.2 copy.29
  87.5 1.2 %fusion.32 = (bf16[64,4,64]{2,1,0:T(4,128)(2,1)S(1)}, bf16[64,4,64]{2,1,0:T(4,128)(2,1)S(1)}) fusion(f32[64,4,1,128]{3,1,0,2:T(4,128)S(1)} %bitcast.96, f32[64]{0:T(128)S(1)} %multiply_exponential_fusion, f32[64,4]{1,0:T(8,128)S(1)} %add_convert_fusion.1), kind=kLoop, calls=%fused_computation.56 | loop fusion | flops 147456 | bytes 197888 | tf_op jit(solution)/shard_map/concatenate | solution.py:29
  88.7 0.5 subtract_convert_fusion
  89.2 0.9 fusion.47
  90.1 2.6 %fusion.48 = (f32[64,4,8]{2,1,0:T(4,128)S(1)}, f32[64,4,1,8,4]{3,4,1,0,2:T(4,128)S(1)}) fusion(bf16[64,4,8,64]{3,2,1,0:T(8,128)(2,1)S(1)} %get-tuple-element.14, bf16[64,4,8,64]{3,2,1,0:T(8,128)(2,1)S(1)} %get-tuple-element.13, bf16[64,4,64]{2,1,0:T(4,128)(2,1)S(1)} %get-tuple-element.16, bf16[64,4,64]{2,1,0:T(4,128)(2,1)S(1)} %get-tuple-element.15, ...), kind=kOutput, calls=%fused_computation.86 | convolution fusion | flops 3299328 | bytes 630800 | tf_op jit(solution)/shard_map/rskgd,rtkd->rskgt/dot_general | solution.py:41
  92.7 0.5 fusion.15
  93.2 0.8 fusion.10
  94.1 0.9 convolution_bitcast_fusion
  95.0 0.5 fusion.4
  95.5 0.9 reshape.284
  (37 shorter events, 1.2 us)
Async XLA Ops:
  6.5 33.1 %copy-start = (bf16[8,1024,64]{1,2,0:T(8,128)(2,1)S(1)}, bf16[8,1024,64]{1,2,0:T(8,128)(2,1)}, u32[]{:S(2)}) copy-start(bf16[8,1024,64]{1,2,0:T(8,128)(2,1)} %param.18) | copy-start | bytes 3145732
  6.5 54.1 %all-gather.2.cloned.1.call-start = ((), (), s32[]{:S(2)}) async-start(), calls=%async_computation | async-start | bytes 4718592 | tf_op jit(solution)/shard_map/all_gather | solution.py:397
  37.9 1.3 %copy-start.1 = (bf16[16,32,1152]{2,1,0:T(8,128)(2,1)S(1)}, bf16[16,32,1152]{2,1,0:T(8,128)(2,1)}, u32[]{:S(2)}) copy-start(bf16[16,32,1152]{2,1,0:T(8,128)(2,1)} %shard_map.109) | copy-start | bytes 3538948
  37.9 1.7 %slice-start = ((bf16[16,32,1152]{2,1,0:T(8,128)(2,1)}), bf16[16,32,1024]{2,1,0:T(8,128)(2,1)S(1)}, s32[]{:S(2)}) async-start(bf16[16,32,1152]{2,1,0:T(8,128)(2,1)} %shard_map.109), calls=%async_computation.1 | async-start | bytes 2097152 | tf_op jit(solution)/shard_map/slice | solution.py:394
  40.4 16.0 %copy-start.5 = (s32[64]{0:T(128)S(1)}, s32[64]{0:T(128)}, u32[]{:S(2)}) copy-start(s32[64]{0:T(128)} %param.14) | copy-start | bytes 772
  85.9 1.6 %copy-start.3 = (f32[256,128]{1,0:T(8,128)S(1)}, f32[256,128]{1,0:T(8,128)}, u32[]{:S(2)}) copy-start(f32[256,128]{1,0:T(8,128)} %get-tuple-element.11) | copy-start | bytes 393220
  87.5 1.7 %copy-start.2 = (bf16[64,64,128]{2,1,0:T(8,128)(2,1)S(1)}, bf16[64,64,128]{2,1,0:T(8,128)(2,1)}, u32[]{:S(2)}) copy-start(bf16[64,64,128]{2,1,0:T(8,128)(2,1)} %param.20) | copy-start | bytes 3145732
  90.1 3.9 %copy-start.4 = (f32[256,128]{1,0:T(8,128)S(1)}, f32[256,128]{1,0:T(8,128)}, u32[]{:S(2)}) copy-start(f32[256,128]{1,0:T(8,128)} %get-tuple-element.12) | copy-start | bytes 393220
  90.1 3.9 %copy-start.6 = (bf16[64,64,128]{2,1,0:T(8,128)(2,1)S(1)}, bf16[64,64,128]{2,1,0:T(8,128)(2,1)}, u32[]{:S(2)}) copy-start(bf16[64,64,128]{2,1,0:T(8,128)(2,1)} %param.21) | copy-start | bytes 3145732
Sparse Core Ops, SparseCore 0:
  9.1 35.7 all-gather.1

commit v4 on v3

--- a/solution.py
+++ b/solution.py
@@ -85,7 +85,10 @@
     ]
 
 
-def exchange_kernel(axis, count, send_ref, got_ref, send_sem, recv_sem, local_sem):
+def exchange_kernel(axis, count, arrays, *refs):
+    send_refs = refs[:arrays]
+    got_refs = refs[arrays : 2 * arrays]
+    send_sem, recv_sem, local_sem = refs[2 * arrays :]
     me = lax.axis_index(axis)
     barrier = pltpu.get_barrier_semaphore()
     offsets = peer_offsets(count)
@@ -93,49 +96,59 @@
         peer = offsets[offset - 1][0](me)
         pl.semaphore_signal(barrier, inc=1, device_id={axis: peer}, device_id_type=MESH)
     pl.semaphore_wait(barrier, count - 1)
-    local = pltpu.make_async_copy(send_ref.at[me], got_ref.at[me], local_sem)
-    local.start()
+    locals_ = []
+    for which in range(arrays):
+        local = pltpu.make_async_copy(
+            send_refs[which].at[me], got_refs[which].at[me], local_sem.at[which]
+        )
+        local.start()
+        locals_.append(local)
     outgoing = []
     for offset in range(1, count):
         peer = offsets[offset - 1][0](me)
-        copy = pltpu.make_async_remote_copy(
-            src_ref=send_ref.at[peer],
-            dst_ref=got_ref.at[me],
-            send_sem=send_sem.at[offset],
-            recv_sem=recv_sem.at[offset],
-            device_id={axis: peer},
-            device_id_type=MESH,
-        )
-        copy.start()
-        outgoing.append(copy)
-    for offset in range(1, count):
-        outgoing[offset - 1].wait_send()
+        for which in range(arrays):
+            copy = pltpu.make_async_remote_copy(
+                src_ref=send_refs[which].at[peer],
+                dst_ref=got_refs[which].at[me],
+                send_sem=send_sem.at[which, offset],
+                recv_sem=recv_sem.at[which, offset],
+                device_id={axis: peer},
+                device_id_type=MESH,
+            )
+            copy.start()
+            outgoing.append(copy)
+    for offset in range(1, count):
         source = offsets[offset - 1][1](me)
-        incoming = pltpu.make_async_remote_copy(
-            src_ref=send_ref.at[source],
-            dst_ref=got_ref.at[source],
-            send_sem=send_sem.at[offset],
-            recv_sem=recv_sem.at[offset],
-            device_id={axis: source},
-            device_id_type=MESH,
-        )
-        incoming.wait_recv()
-    local.wait()
+        for which in range(arrays):
+            outgoing[(offset - 1) * arrays + which].wait_send()
+            incoming = pltpu.make_async_remote_copy(
+                src_ref=send_refs[which].at[source],
+                dst_ref=got_refs[which].at[source],
+                send_sem=send_sem.at[which, offset],
+                recv_sem=recv_sem.at[which, offset],
+                device_id={axis: source},
+                device_id_type=MESH,
+            )
+            incoming.wait_recv()
+    for local in locals_:
+        local.wait()
 
 
 def exchange(values, axis, count, collective):
+    arrays = len(values)
+    vmem = pl.BlockSpec(memory_space=pltpu.VMEM)
     return pl.pallas_call(
-        lambda *refs: exchange_kernel(axis, count, *refs),
-        out_shape=jax.ShapeDtypeStruct(values.shape, values.dtype),
-        in_specs=[pl.BlockSpec(memory_space=pltpu.VMEM)],
-        out_specs=pl.BlockSpec(memory_space=pltpu.VMEM),
+        lambda *refs: exchange_kernel(axis, count, arrays, *refs),
+        out_shape=tuple(jax.ShapeDtypeStruct(v.shape, v.dtype) for v in values),
+        in_specs=[vmem] * arrays,
+        out_specs=tuple([vmem] * arrays),
         scratch_shapes=[
-            pltpu.SemaphoreType.DMA((count,)),
-            pltpu.SemaphoreType.DMA((count,)),
-            pltpu.SemaphoreType.DMA(()),
+            pltpu.SemaphoreType.DMA((arrays, count)),
+            pltpu.SemaphoreType.DMA((arrays, count)),
+            pltpu.SemaphoreType.DMA((arrays,)),
         ],
         compiler_params=pltpu.CompilerParams(collective_id=collective, has_side_effects=True),
-    )(values)
+    )(*values)
 
 
 def exchange_project_kernel(
@@ -379,29 +392,29 @@
     send_slot = owner_grp * CAP + owner_rank
     slot_span = jnp.arange(group_count * CAP, dtype=jnp.int32)
     place = (slot_span[:, None] == send_slot[None, :]).astype(jnp.bfloat16)
-    token_flat = tokens.reshape(row_count, step_count * part_width)
-    send_tokens = jnp.dot(place, token_flat, preferred_element_type=jnp.float32).astype(jnp.bfloat16)
+    token_slot = (send_slot[:, None] * step_count + jnp.arange(step_count, dtype=jnp.int32)[None, :]).reshape(-1)
+    token_span = jnp.arange(group_count * CAP * step_count, dtype=jnp.int32)
+    place_tokens = (token_span[:, None] == token_slot[None, :]).astype(jnp.bfloat16)
+    token_rows = tokens.reshape(count_of_tokens, part_width)
+    send_tokens = jnp.dot(place_tokens, token_rows, preferred_element_type=jnp.float32).astype(jnp.bfloat16)
+    send_tokens = send_tokens.reshape(group_count, CAP * step_count, part_width)
     send_ids = jnp.dot(
         place, local_slot.astype(jnp.bfloat16)[:, None], preferred_element_type=jnp.float32
     ).astype(jnp.bfloat16)
-    send_ids = jnp.broadcast_to(
-        send_ids.reshape(group_count * CAP, 1, 1), (group_count * CAP, step_count, 128)
-    )
-    packed = jnp.concatenate(
-        [send_tokens.reshape(group_count * CAP, step_count, part_width), send_ids], axis=2
-    ).reshape(group_count, CAP * step_count, part_width + 128)
-    got = exchange(packed, "grp", group_count, 0)
-    got_tokens = got[:, :, :part_width]
-    got_ids = got[:, :, part_width].astype(jnp.int32)
+    send_ids = jnp.broadcast_to(send_ids.reshape(group_count, CAP, 1), (group_count, CAP, 128))
+    send_ids = jnp.concatenate([send_ids, jnp.zeros_like(send_ids)], axis=1)
+    got_tokens, got_ids = exchange((send_tokens, send_ids), "grp", group_count, 0)
+    got_ids = jnp.repeat(got_ids[:, :CAP, 0].astype(jnp.int32), step_count, axis=1)
     owner_out = owner_adapter_term(got_tokens, got_ids, pooled_down_weights, pool_up)
-    pieces = lax.all_gather(tokens.reshape(count_of_tokens, part_width), "tp", axis=0, tiled=False)
+    pieces = lax.all_gather(token_rows, "tp", axis=0, tiled=False)
     back, base_query_rows, key_base, value_base = exchange_project(
         owner_out, pieces, w_query, w_key, w_value, "grp", group_count, 1
     )
-    back = back.reshape(group_count * CAP, step_count * query_width)
     adapter_output = jnp.dot(
-        jnp.transpose(place), back, preferred_element_type=jnp.float32
-    ).reshape(count_of_tokens, query_width)
+        jnp.transpose(place_tokens),
+        back.reshape(group_count * CAP * step_count, query_width),
+        preferred_element_type=jnp.float32,
+    )
     base_query_rows = base_query_rows + adapter_output
     position = lengths[:, None] + jnp.arange(step_count, dtype=jnp.int32)[None, :]
     queries = rotate(base_query_rows.reshape(row_count, step_count, q_local, HD), position)

time: 104 us -> 100 us (0.962)
  local copies, waits for them, and re-layouts: 10.8 us -> 7.57 us
  matrix products: 9.47 us -> 12.2 us
  other arithmetic: 8.32 us -> 5.63 us
    dot_general x2, matrix products: 0.77 us -> 3.48 us  [the longest x1 2.06 us: body(): jnp.dot(jnp.transpose(place_tokens), back.reshape(group_count * CAP * ste...]
    unnamed x16 -> x19, local copies, waits for them, and re-layouts: 2.73 us -> 0.24 us
    unnamed x1 -> x0, other arithmetic: 1.4 us -> none
    unnamed x1, matrix products: 0.74 us -> 1.99 us
    dot_general x1, matrix products: 2.94 us -> 1.72 us  [owner_adapter_term(): jnp.dot(spread_rows, up_local.reshape(local_adapters * adapter_rank, quer...]
    concatenate x1 -> x0, other arithmetic: 1.11 us -> none  [body(): jnp.concatenate([send_tokens.reshape(group_count * CAP, step_count, part_...]
  transfers between devices with their start and end apart: 1 -> 1, of which waited for: 0 -> 0; matrix products, arithmetic and copies ran while one was open for 12% -> 12% of each run, Pallas kernels for 37% -> 38%
where the time goes in v4:
time: 100 us; the launch traced here: 99.6 us
  Pallas kernels  60.5 us (60%)
  between operations  13.7 us (14%)
  matrix products  12.2 us (12%)
  local copies, waits for them, and re-layouts  7.57 us (8%)
  other arithmetic  5.63 us (6%)
    pallas_call x1, Pallas kernels, exchange(): pl.pallas_call(lambda *refs: exchange_kernel(axis, count, arrays, *refs),...  23.8 us
    pallas_call x1, Pallas kernels, exchange_project(): pl.pallas_call(lambda *refs: exchange_project_kernel(axis, count, *refs),...  22.9 us
    pallas_call x1, Pallas kernels, axis_sum(): pl.pallas_call(lambda *refs: sum_kernel(axis, count, *refs), out_shape=ja...  13.8 us
    dot_general x1, matrix products, attend(): jnp.einsum('rskgd,rtkd->rskgt', queries, key_new, preferred_element_type=...  2.58 us
    dot_general x1, matrix products, body(): jnp.dot(jnp.transpose(place_tokens), back.reshape(group_count * CAP * ste...  2.06 us
    another operation x1, local copies, waits for them, and re-layouts, body(): pieces = lax.all_gather(token_rows, 'tp', axis=0, tiled=False)  2.04 us
  transfers between devices with their start and end apart: 1, of which 0 were waited for; matrix products, arithmetic and copies ran while one was open for 12% of the time, Pallas kernels for 38%

profile of v4, /device:TPU:1, one launch (start us, length us, event | category | flops | bytes accessed | tf_op | source)
XLA Modules:
  0.0 99.6 jit_solution(17229108357760191408)
XLA Ops:
  6.5 2.0 %all_gather_reshape.3 = bf16[1,256,1024]{2,1,0:T(8,128)(2,1)} reshape(bf16[64,4,1024]{2,1,0:T(4,128)(2,1)} %param.11) | data formatting | bytes 1048576 | tf_op jit(solution)/shard_map/all_gather;reshape | solution.py:409
  8.6 1.2 %reshape.288 = bf16[256,1024]{1,0:T(8,128)(2,1)S(1)} reshape(bf16[64,4,1024]{2,1,0:T(4,128)(2,1)} %param.11) | data formatting | bytes 1048576 | tf_op jit(solution)/shard_map/reshape | solution.py:398
  9.8 0.2 select_reduce_fusion.1
  10.0 0.2 convert_reduce_fusion
  10.2 0.1 fusion.8
  10.5 0.1 add.100
  10.7 0.6 concatenate.21.refs_1_
  11.4 1.4 %convolution_convert_fusion = bf16[512,1024]{1,0:T(8,128)(2,1)} fusion(bf16[256,1024]{1,0:T(8,128)(2,1)S(1)} %reshape.288, s32[256]{0:T(256)S(1)} %add.100), kind=kOutput, calls=%fused_computation.1 | convolution fusion | flops 269090816 | bytes 1573888 | tf_op jit(solution)/shard_map/dot_general | solution.py:399
  12.8 23.8 %shard_map.109 = (bf16[16,32,1024]{2,1,0:T(8,128)(2,1)}, bf16[16,16,128]{2,1,0:T(8,128)(2,1)}) custom-call(bf16[16,32,1024]{2,1,0:T(8,128)(2,1)} %bitcast.92, bf16[16,16,128]{2,1,0:T(8,128)(2,1)} %concatenate.21.refs_1_), custom_call_target="tpu_custom_call" | custom-call | tf_op jit(solution)/shard_map/pallas_call | solution.py:140
  36.6 0.8 slice_convert_fusion
  37.4 0.2 copy.34
  37.6 0.1 eq.85
  37.7 2.0 %fusion.49 = f32[512,512]{0,1:S(1)} fusion(bf16[512,1024]{1,0:T(8,128)(2,1)} %bitcast.99, bf16[1024,512]{0,1:T(8,128)(2,1)S(1)} %bitcast.90), kind=kOutput, calls=%fused_computation.89 | convolution fusion | flops 536870912 | bytes 3145728
  39.8 0.1 select_reduce_fusion
  39.9 0.1 copy.28
  40.0 0.8 reshape_reshape.3.refs_0_
  40.8 13.8 %shard_map.110 = bf16[8,32,128]{2,1,0:T(8,128)(2,1)} custom-call(f32[8,32,128]{2,1,0:T(8,128)} %reshape_reshape.3.refs_0_), custom_call_target="tpu_custom_call" | custom-call | tf_op jit(solution)/shard_map/pallas_call | solution.py:320
  54.6 0.9 broadcast_in_dim.82
  55.9 1.1 %multiply_cosine_fusion.1 = (f32[64,4,64]{2,1,0:T(4,128)S(1)}, f32[64,4,64]{2,1,0:T(4,128)S(1)}) fusion(f32[64]{0:T(128)S(1)} %multiply_exponential_fusion, f32[64,4]{1,0:T(8,128)S(1)} %add_convert_fusion.1), kind=kLoop, calls=%fused_computation.43 | loop fusion | flops 16384 | bytes 132352 | tf_op jit(solution)/shard_map/cos | solution.py:25
  57.0 1.7 %bitcast_convert_fusion = bf16[512,1024]{1,0:T(8,128)(2,1)} fusion(bf16[8,64,1024]{2,1,0:T(8,128)(2,1)S(1)} %copy-done.5, pred[512,8]{0,1:T(8,128)(4,1)S(1)} %iota_compare_fusion.8, bf16[512,64]{0,1:T(8,128)(2,1)S(1)} %copy.29), kind=kOutput, calls=%fused_computation | convolution fusion | flops 537657344 | bytes 2166784 | tf_op jit(solution)/shard_map/dot_general | solution.py:352
  58.7 22.9 %shard_map.111 = (bf16[16,32,1024]{2,1,0:T(8,128)(2,1)}, f32[256,1024]{1,0:T(8,128)}, f32[256,128]{1,0:T(8,128)}, f32[256,128]{1,0:T(8,128)}) custom-call(bf16[16,32,1024]{2,1,0:T(8,128)(2,1)} %bitcast.93, bf16[8,256,1024]{2,1,0:T(8,128)(2,1)} %all-gather.2.cloned.1.call-done.refs_1_, bf16[8192,1024]{1,0:T(8,128)(2,1)} %refs_2_.1, ...), custom_call_target="tpu_custom_call" | custom-call | tf_op jit(solution)/shard_map/pallas_call | solution.py:231
  81.6 2.1 %fusion.1 = f32[32,8,8,128]{3,1,2,0:T(8,128)S(1)} fusion(f32[256,1024]{1,0:T(8,128)} %get-tuple-element.13, bf16[512,1024]{1,0:T(8,128)(2,1)} %bitcast.95, s32[256]{0:T(256)S(1)} %add.100), kind=kOutput, calls=%fused_computation.5 | convolution fusion | flops 268828672 | bytes 3146752 | tf_op jit(solution)/shard_map/dot_general | solution.py:413
  83.6 0.2 copy.35
  83.9 1.2 %fusion.34 = (bf16[64,4,64]{2,1,0:T(4,128)(2,1)S(1)}, bf16[64,4,64]{2,1,0:T(4,128)(2,1)S(1)}) fusion(f32[64,4,1,128]{3,1,0,2:T(4,128)S(1)} %bitcast.96, f32[64]{0:T(128)S(1)} %multiply_exponential_fusion, f32[64,4]{1,0:T(8,128)S(1)} %add_convert_fusion.1), kind=kLoop, calls=%fused_computation.57 | loop fusion | flops 147456 | bytes 197888 | tf_op jit(solution)/shard_map/concatenate | solution.py:29
  85.1 0.5 subtract_convert_fusion
  85.6 0.9 fusion.47
  86.5 2.6 %fusion.48 = (f32[64,4,8]{2,1,0:T(4,128)S(1)}, f32[64,4,1,8,4]{3,4,1,0,2:T(4,128)S(1)}) fusion(bf16[64,4,8,64]{3,2,1,0:T(8,128)(2,1)S(1)} %get-tuple-element.20, bf16[64,4,8,64]{3,2,1,0:T(8,128)(2,1)S(1)} %get-tuple-element.19, bf16[64,4,64]{2,1,0:T(4,128)(2,1)S(1)} %get-tuple-element.22, bf16[64,4,64]{2,1,0:T(4,128)(2,1)S(1)} %get-tuple-element.21, ...), kind=kOutput, calls=%fused_computation.88 | convolution fusion | flops 3299328 | bytes 630800 | tf_op jit(solution)/shard_map/rskgd,rtkd->rskgt/dot_general | solution.py:41
  89.1 0.5 fusion.16
  89.6 0.8 fusion.11
  90.4 0.9 convolution_bitcast_fusion
  91.4 0.5 fusion.5
  91.9 0.9 reshape.297
  (36 shorter events, 0.8 us)
Async XLA Ops:
  6.5 31.2 %copy-start = (bf16[8,1024,64]{1,2,0:T(8,128)(2,1)S(1)}, bf16[8,1024,64]{1,2,0:T(8,128)(2,1)}, u32[]{:S(2)}) copy-start(bf16[8,1024,64]{1,2,0:T(8,128)(2,1)} %param.18) | copy-start | bytes 3145732
  6.5 3.2 %copy-start.8 = (s32[64]{0:T(128)S(1)}, s32[64]{0:T(128)}, u32[]{:S(2)}) copy-start(s32[64]{0:T(128)} %param.12) | copy-start | bytes 772
  6.5 3.3 %copy-start.7 = (s32[128]{0:T(128)S(1)}, s32[128]{0:T(128)}, u32[]{:S(2)}) copy-start(s32[128]{0:T(128)} %param.13) | copy-start | bytes 1540
  6.5 52.1 %all-gather.2.cloned.1.call-start = ((), (), s32[]{:S(2)}) async-start(), calls=%async_computation | async-start | bytes 4718592 | tf_op jit(solution)/shard_map/all_gather | solution.py:409
  39.7 16.0 %copy-start.4 = (s32[64]{0:T(128)S(1)}, s32[64]{0:T(128)}, u32[]{:S(2)}) copy-start(s32[64]{0:T(128)} %param.14) | copy-start | bytes 772
  39.7 17.2 %copy-start.5 = (bf16[8,64,1024]{2,1,0:T(8,128)(2,1)S(1)}, bf16[8,64,1024]{2,1,0:T(8,128)(2,1)}, u32[]{:S(2)}) copy-start(bf16[8,64,1024]{2,1,0:T(8,128)(2,1)} %param.19) | copy-start | bytes 3145732
  81.6 2.3 %copy-start.2 = (f32[256,128]{1,0:T(8,128)S(1)}, f32[256,128]{1,0:T(8,128)}, u32[]{:S(2)}) copy-start(f32[256,128]{1,0:T(8,128)} %get-tuple-element.15) | copy-start | bytes 393220
  83.8 1.7 %copy-start.1 = (bf16[64,64,128]{2,1,0:T(8,128)(2,1)S(1)}, bf16[64,64,128]{2,1,0:T(8,128)(2,1)}, u32[]{:S(2)}) copy-start(bf16[64,64,128]{2,1,0:T(8,128)(2,1)} %param.20) | copy-start | bytes 3145732
  86.5 3.9 %copy-start.3 = (f32[256,128]{1,0:T(8,128)S(1)}, f32[256,128]{1,0:T(8,128)}, u32[]{:S(2)}) copy-start(f32[256,128]{1,0:T(8,128)} %get-tuple-element.16) | copy-start | bytes 393220
  86.5 3.9 %copy-start.6 = (bf16[64,64,128]{2,1,0:T(8,128)(2,1)S(1)}, bf16[64,64,128]{2,1,0:T(8,128)(2,1)}, u32[]{:S(2)}) copy-start(bf16[64,64,128]{2,1,0:T(8,128)(2,1)} %param.21) | copy-start | bytes 3145732
Sparse Core Ops, SparseCore 0:
  9.1 35.6 all-gather.1

commit v5 on v4

--- a/solution.py
+++ b/solution.py
@@ -149,6 +149,163 @@
         ],
         compiler_params=pltpu.CompilerParams(collective_id=collective, has_side_effects=True),
     )(*values)
+
+
+def exchange_gather_kernel(
+    axis, count, gather_axis, chips, arrays, *refs
+):
+    send_refs = refs[:arrays]
+    piece_ref = refs[arrays]
+    got_refs = refs[arrays + 1 : 2 * arrays + 1]
+    pieces_ref = refs[2 * arrays + 1]
+    send_sem, recv_sem, local_sem, chip_send, chip_recv, core_send, core_recv, piece_sem = refs[
+        2 * arrays + 2 :
+    ]
+    me = lax.axis_index(axis)
+    mine = lax.axis_index(gather_axis)
+    chip = mine // 2
+    core = lax.rem(mine, 2)
+    partner = chip * 2 + (1 - core)
+
+    def chip_peer(step):
+        return lax.rem(chip + step, chips) * 2 + core
+
+    barrier = pltpu.get_barrier_semaphore()
+    offsets = peer_offsets(count)
+    for offset in range(1, count):
+        peer = offsets[offset - 1][0](me)
+        pl.semaphore_signal(barrier, inc=1, device_id={axis: peer}, device_id_type=MESH)
+    for step in range(1, chips):
+        pl.semaphore_signal(
+            barrier, inc=1, device_id={gather_axis: chip_peer(step)}, device_id_type=MESH
+        )
+    pl.semaphore_signal(barrier, inc=1, device_id={gather_axis: partner}, device_id_type=MESH)
+    pl.semaphore_wait(barrier, count - 1 + chips)
+
+    own_piece = pltpu.make_async_copy(piece_ref, pieces_ref.at[mine], piece_sem)
+    own_piece.start()
+    chip_copies = []
+    for step in range(1, chips):
+        copy = pltpu.make_async_remote_copy(
+            src_ref=piece_ref,
+            dst_ref=pieces_ref.at[mine],
+            send_sem=chip_send.at[step],
+            recv_sem=chip_recv.at[step],
+            device_id={gather_axis: chip_peer(step)},
+            device_id_type=MESH,
+        )
+        copy.start()
+        chip_copies.append(copy)
+    core_copies = []
+    copy = pltpu.make_async_remote_copy(
+        src_ref=piece_ref,
+        dst_ref=pieces_ref.at[mine],
+        send_sem=core_send.at[0],
+        recv_sem=core_recv.at[0],
+        device_id={gather_axis: partner},
+        device_id_type=MESH,
+    )
+    copy.start()
+    core_copies.append(copy)
+
+    locals_ = []
+    for which in range(arrays):
+        local = pltpu.make_async_copy(
+            send_refs[which].at[me], got_refs[which].at[me], local_sem.at[which]
+        )
+        local.start()
+        locals_.append(local)
+    outgoing = []
+    for offset in range(1, count):
+        peer = offsets[offset - 1][0](me)
+        for which in range(arrays):
+            copy = pltpu.make_async_remote_copy(
+                src_ref=send_refs[which].at[peer],
+                dst_ref=got_refs[which].at[me],
+                send_sem=send_sem.at[which, offset],
+                recv_sem=recv_sem.at[which, offset],
+                device_id={axis: peer},
+                device_id_type=MESH,
+            )
+            copy.start()
+            outgoing.append(copy)
+
+    for step in range(1, chips):
+        chip_copies[step - 1].wait_send()
+        source = chip_peer(chips - step)
+        incoming = pltpu.make_async_remote_copy(
+            src_ref=piece_ref,
+            dst_ref=pieces_ref.at[source],
+            send_sem=chip_send.at[step],
+            recv_sem=chip_recv.at[step],
+            device_id={gather_axis: source},
+            device_id_type=MESH,
+        )
+        incoming.wait_recv()
+        copy = pltpu.make_async_remote_copy(
+            src_ref=pieces_ref.at[source],
+            dst_ref=pieces_ref.at[source],
+            send_sem=core_send.at[step],
+            recv_sem=core_recv.at[step],
+            device_id={gather_axis: partner},
+            device_id_type=MESH,
+        )
+        copy.start()
+        core_copies.append(copy)
+    for step in range(chips):
+        core_copies[step].wait_send()
+        source = lax.rem(chip + chips - step, chips) * 2 + (1 - core)
+        incoming = pltpu.make_async_remote_copy(
+            src_ref=piece_ref,
+            dst_ref=pieces_ref.at[source],
+            send_sem=core_send.at[step],
+            recv_sem=core_recv.at[step],
+            device_id={gather_axis: partner},
+            device_id_type=MESH,
+        )
+        incoming.wait_recv()
+
+    for offset in range(1, count):
+        source = offsets[offset - 1][1](me)
+        for which in range(arrays):
+            outgoing[(offset - 1) * arrays + which].wait_send()
+            incoming = pltpu.make_async_remote_copy(
+                src_ref=send_refs[which].at[source],
+                dst_ref=got_refs[which].at[source],
+                send_sem=send_sem.at[which, offset],
+                recv_sem=recv_sem.at[which, offset],
+                device_id={axis: source},
+                device_id_type=MESH,
+            )
+            incoming.wait_recv()
+    for local in locals_:
+        local.wait()
+    own_piece.wait()
+
+
+def exchange_gather(values, piece, axis, count, gather_axis, gather_count, collective):
+    arrays = len(values)
+    chips = gather_count // 2
+    vmem = pl.BlockSpec(memory_space=pltpu.VMEM)
+    outs = pl.pallas_call(
+        lambda *refs: exchange_gather_kernel(axis, count, gather_axis, chips, arrays, *refs),
+        out_shape=tuple(jax.ShapeDtypeStruct(v.shape, v.dtype) for v in values)
+        + (jax.ShapeDtypeStruct((gather_count,) + piece.shape, piece.dtype),),
+        in_specs=[vmem] * (arrays + 1),
+        out_specs=tuple([vmem] * (arrays + 1)),
+        scratch_shapes=[
+            pltpu.SemaphoreType.DMA((arrays, count)),
+            pltpu.SemaphoreType.DMA((arrays, count)),
+            pltpu.SemaphoreType.DMA((arrays,)),
+            pltpu.SemaphoreType.DMA((chips,)),
+            pltpu.SemaphoreType.DMA((chips,)),
+            pltpu.SemaphoreType.DMA((chips,)),
+            pltpu.SemaphoreType.DMA((chips,)),
+            pltpu.SemaphoreType.DMA(()),
+        ],
+        compiler_params=pltpu.CompilerParams(collective_id=collective, has_side_effects=True),
+    )(*values, piece)
+    return outs[:arrays], outs[arrays]
 
 
 def exchange_project_kernel(
@@ -403,10 +560,11 @@
     ).astype(jnp.bfloat16)
     send_ids = jnp.broadcast_to(send_ids.reshape(group_count, CAP, 1), (group_count, CAP, 128))
     send_ids = jnp.concatenate([send_ids, jnp.zeros_like(send_ids)], axis=1)
-    got_tokens, got_ids = exchange((send_tokens, send_ids), "grp", group_count, 0)
+    (got_tokens, got_ids), pieces = exchange_gather(
+        (send_tokens, send_ids), token_rows, "grp", group_count, "tp", tp_count, 0
+    )
     got_ids = jnp.repeat(got_ids[:, :CAP, 0].astype(jnp.int32), step_count, axis=1)
     owner_out = owner_adapter_term(got_tokens, got_ids, pooled_down_weights, pool_up)
-    pieces = lax.all_gather(token_rows, "tp", axis=0, tiled=False)
     back, base_query_rows, key_base, value_base = exchange_project(
         owner_out, pieces, w_query, w_key, w_value, "grp", group_count, 1
     )

time: 100 us -> 98.5 us (0.985)
  between operations: 13.7 us -> 0.32 us
  Pallas kernels: 60.5 us -> 73.4 us
  local copies, waits for them, and re-layouts: 7.57 us -> 5.54 us
    pallas_call x1, Pallas kernels: 23.8 us -> 40.8 us  [exchange_gather(): pl.pallas_call(lambda *refs: exchange_gather_kernel(axis, count, gather_a...]
    pallas_call x1, Pallas kernels: 13.8 us -> 10.3 us  [axis_sum(): pl.pallas_call(lambda *refs: sum_kernel(axis, count, *refs), out_shape=ja...]
    another operation x1 -> x0, local copies, waits for them, and re-layouts: 2.04 us -> none  [body(): pieces = lax.all_gather(token_rows, 'tp', axis=0, tiled=False)]
  transfers between devices with their start and end apart: 1 -> 0, of which waited for: 0 -> 0; matrix products, arithmetic and copies ran while one was open for 12% -> 0% of each run, Pallas kernels for 38% -> 0%
where the time goes in v5:
time: 98.5 us; the launch traced here: 97.8 us
  Pallas kernels  73.4 us (75%)
  matrix products  12.1 us (12%)
  other arithmetic  6.39 us (6%)
  local copies, waits for them, and re-layouts  5.54 us (6%)
    pallas_call x1, Pallas kernels, exchange_gather(): pl.pallas_call(lambda *refs: exchange_gather_kernel(axis, count, gather_a...  40.8 us
    pallas_call x1, Pallas kernels, exchange_project(): pl.pallas_call(lambda *refs: exchange_project_kernel(axis, count, *refs),...  22.3 us
    pallas_call x1, Pallas kernels, axis_sum(): pl.pallas_call(lambda *refs: sum_kernel(axis, count, *refs), out_shape=ja...  10.3 us
    dot_general x1, matrix products, attend(): jnp.einsum('rskgd,rtkd->rskgt', queries, key_new, preferred_element_type=...  2.58 us
    dot_general x1, matrix products, body(): jnp.dot(jnp.transpose(place_tokens), back.reshape(group_count * CAP * ste...  2.03 us

profile of v5, /device:TPU:1, one launch (start us, length us, event | category | flops | bytes accessed | tf_op | source)
XLA Modules:
  0.0 97.8 jit_solution(16954075148017107061)
XLA Ops:
  0.0 0.9 select_reduce_fusion.1
  1.0 0.2 convert_reduce_fusion
  1.2 0.1 add.100
  1.4 1.2 %reshape.288.refs_2_ = bf16[256,1024]{1,0:T(8,128)(2,1)S(1)} reshape(bf16[64,4,1024]{2,1,0:T(4,128)(2,1)} %param.11) | data formatting | bytes 1048576 | tf_op jit(solution)/shard_map/reshape | solution.py:555
  2.5 1.4 %convolution_convert_fusion = bf16[512,1024]{1,0:T(8,128)(2,1)} fusion(bf16[256,1024]{1,0:T(8,128)(2,1)S(1)} %reshape.288.refs_2_, s32[256]{0:T(256)S(1)} %add.100), kind=kOutput, calls=%fused_computation.1 | convolution fusion | flops 269090816 | bytes 1573888 | tf_op jit(solution)/shard_map/dot_general | solution.py:556
  4.0 0.1 fusion.8
  4.3 0.6 concatenate.21.refs_1_
  4.9 40.8 %shard_map.109 = (bf16[16,32,1024]{2,1,0:T(8,128)(2,1)}, bf16[16,16,128]{2,1,0:T(8,128)(2,1)}, bf16[8,256,1024]{2,1,0:T(8,128)(2,1)}) custom-call(bf16[16,32,1024]{2,1,0:T(8,128)(2,1)} %bitcast.92, bf16[16,16,128]{2,1,0:T(8,128)(2,1)} %concatenate.21.refs_1_, bf16[256,1024]{1,0:T(8,128)(2,1)} %copy-done.1), custom_call_target="tpu_custom_call" | custom-call | tf_op jit(solution)/shard_map/pallas_call | solution.py:290
  45.7 0.8 slice_convert_fusion
  46.5 0.2 copy.34
  46.7 0.1 eq.85
  46.9 2.0 %fusion.49 = f32[512,512]{0,1:S(1)} fusion(bf16[512,1024]{1,0:T(8,128)(2,1)} %bitcast.99, bf16[1024,512]{0,1:T(8,128)(2,1)S(1)} %bitcast.90), kind=kOutput, calls=%fused_computation.89 | convolution fusion | flops 536870912 | bytes 3145728
  48.9 0.1 select_reduce_fusion
  49.0 0.1 copy.28
  49.1 0.8 reshape_reshape.3.refs_0_
  49.9 10.3 %shard_map.110 = bf16[8,32,128]{2,1,0:T(8,128)(2,1)} custom-call(f32[8,32,128]{2,1,0:T(8,128)} %reshape_reshape.3.refs_0_), custom_call_target="tpu_custom_call" | custom-call | tf_op jit(solution)/shard_map/pallas_call | solution.py:477
  60.2 0.9 broadcast_in_dim.82
  61.2 0.1 copy.29
  61.3 1.7 %bitcast_convert_fusion = bf16[512,1024]{1,0:T(8,128)(2,1)} fusion(bf16[8,64,1024]{2,1,0:T(8,128)(2,1)S(1)} %copy-done.6, pred[512,8]{0,1:T(8,128)(4,1)S(1)} %iota_compare_fusion.8, bf16[512,64]{0,1:T(8,128)(2,1)S(1)} %copy.29), kind=kOutput, calls=%fused_computation | convolution fusion | flops 537657344 | bytes 2166784 | tf_op jit(solution)/shard_map/dot_general | solution.py:509
  63.0 22.3 %shard_map.111 = (bf16[16,32,1024]{2,1,0:T(8,128)(2,1)}, f32[256,1024]{1,0:T(8,128)}, f32[256,128]{1,0:T(8,128)}, f32[256,128]{1,0:T(8,128)}) custom-call(bf16[16,32,1024]{2,1,0:T(8,128)(2,1)} %bitcast.93, bf16[8,256,1024]{2,1,0:T(8,128)(2,1)} %get-tuple-element.14.refs_1_, bf16[8192,1024]{1,0:T(8,128)(2,1)} %refs_2_.1, bf16[8192,128]{1,0:T(8,128)(2,1)} %refs_3_.1, ...), custom_call_target="tpu_custom_call" | custom-call | tf_op jit(solution)/shard_map/pallas_call | solution.py:388
  85.3 2.0 %fusion.1 = f32[32,8,8,128]{3,1,2,0:T(8,128)S(1)} fusion(f32[256,1024]{1,0:T(8,128)} %get-tuple-element.15, bf16[512,1024]{1,0:T(8,128)(2,1)} %bitcast.95, s32[256]{0:T(256)S(1)} %add.100), kind=kOutput, calls=%fused_computation.5 | convolution fusion | flops 268828672 | bytes 3146752 | tf_op jit(solution)/shard_map/dot_general | solution.py:571
  87.3 0.2 copy.35
  87.7 1.1 %multiply_cosine_fusion.1 = (f32[64,4,64]{2,1,0:T(4,128)S(1)}, f32[64,4,64]{2,1,0:T(4,128)S(1)}) fusion(f32[64]{0:T(128)S(1)} %multiply_exponential_fusion, f32[64,4]{1,0:T(8,128)S(1)} %add_convert_fusion.1), kind=kLoop, calls=%fused_computation.43 | loop fusion | flops 16384 | bytes 132352 | tf_op jit(solution)/shard_map/cos | solution.py:25
  88.8 0.5 subtract_convert_fusion
  89.3 1.2 %fusion.34 = (bf16[64,4,64]{2,1,0:T(4,128)(2,1)S(1)}, bf16[64,4,64]{2,1,0:T(4,128)(2,1)S(1)}) fusion(f32[64,4,1,128]{3,1,0,2:T(4,128)S(1)} %bitcast.96, f32[64]{0:T(128)S(1)} %multiply_exponential_fusion, f32[64,4]{1,0:T(8,128)S(1)} %add_convert_fusion.1), kind=kLoop, calls=%fused_computation.57 | loop fusion | flops 147456 | bytes 197888 | tf_op jit(solution)/shard_map/concatenate | solution.py:29
  90.5 2.6 %fusion.48 = (f32[64,4,8]{2,1,0:T(4,128)S(1)}, f32[64,4,1,8,4]{3,4,1,0,2:T(4,128)S(1)}) fusion(bf16[64,4,8,64]{3,2,1,0:T(8,128)(2,1)S(1)} %get-tuple-element.22, bf16[64,4,8,64]{3,2,1,0:T(8,128)(2,1)S(1)} %get-tuple-element.21, bf16[64,4,64]{2,1,0:T(4,128)(2,1)S(1)} %get-tuple-element.24, bf16[64,4,64]{2,1,0:T(4,128)(2,1)S(1)} %get-tuple-element.23, ...), kind=kOutput, calls=%fused_computation.88 | convolution fusion | flops 3299328 | bytes 630800 | tf_op jit(solution)/shard_map/rskgd,rtkd->rskgt/dot_general | solution.py:41
  93.2 0.9 fusion.47
  94.1 0.5 fusion.16
  94.6 0.8 fusion.11
  95.4 0.9 convolution_bitcast_fusion
  96.4 0.5 fusion.5
  96.9 0.9 reshape.297
  (30 shorter events, 0.7 us)
Async XLA Ops:
  0.0 46.9 %copy-start = (bf16[8,1024,64]{1,2,0:T(8,128)(2,1)S(1)}, bf16[8,1024,64]{1,2,0:T(8,128)(2,1)}, u32[]{:S(2)}) copy-start(bf16[8,1024,64]{1,2,0:T(8,128)(2,1)} %param.18) | copy-start | bytes 3145732
  2.5 2.4 %copy-start.1 = (bf16[256,1024]{1,0:T(8,128)(2,1)}, bf16[256,1024]{1,0:T(8,128)(2,1)S(1)}, u32[]{:S(2)}) copy-start(bf16[256,1024]{1,0:T(8,128)(2,1)S(1)} %reshape.288.refs_2_) | copy-start | bytes 1572868
  48.8 12.4 %copy-start.6 = (bf16[8,64,1024]{2,1,0:T(8,128)(2,1)S(1)}, bf16[8,64,1024]{2,1,0:T(8,128)(2,1)}, u32[]{:S(2)}) copy-start(bf16[8,64,1024]{2,1,0:T(8,128)(2,1)} %param.19) | copy-start | bytes 3145732
  85.3 2.3 %copy-start.5 = (s32[64]{0:T(128)S(1)}, s32[64]{0:T(128)}, u32[]{:S(2)}) copy-start(s32[64]{0:T(128)} %param.14) | copy-start | bytes 772
  87.5 1.7 %copy-start.3 = (f32[256,128]{1,0:T(8,128)S(1)}, f32[256,128]{1,0:T(8,128)}, u32[]{:S(2)}) copy-start(f32[256,128]{1,0:T(8,128)} %get-tuple-element.17) | copy-start | bytes 393220
  88.8 4.4 %copy-start.2 = (bf16[64,64,128]{2,1,0:T(8,128)(2,1)S(1)}, bf16[64,64,128]{2,1,0:T(8,128)(2,1)}, u32[]{:S(2)}) copy-start(bf16[64,64,128]{2,1,0:T(8,128)(2,1)} %param.20) | copy-start | bytes 3145732
  94.0 1.3 %copy-start.7 = (bf16[64,64,128]{2,1,0:T(8,128)(2,1)S(1)}, bf16[64,64,128]{2,1,0:T(8,128)(2,1)}, u32[]{:S(2)}) copy-start(bf16[64,64,128]{2,1,0:T(8,128)(2,1)} %param.21) | copy-start | bytes 3145732
  95.4 1.0 copy-start.4

commit v6 on v4

--- a/solution.py
+++ b/solution.py
@@ -152,17 +152,30 @@
 
 
 def exchange_project_kernel(
-    axis, count, send_ref, pieces_ref, wq_hbm, wk_ref, wv_ref,
+    axis, count, gather_axis, send_ref, chip_pieces, wq_hbm, wk_ref, wv_ref,
     got_ref, q_ref, k_ref, v_ref,
-    wq_buf, send_sem, recv_sem, local_sem, wq_sem,
+    partner_pieces, wq_buf, send_sem, recv_sem, local_sem, wq_sem, partner_send, partner_recv,
 ):
     me = lax.axis_index(axis)
+    mine = lax.axis_index(gather_axis)
+    core = lax.rem(mine, 2)
+    partner = (mine // 2) * 2 + (1 - core)
     barrier = pltpu.get_barrier_semaphore()
     offsets = peer_offsets(count)
     for offset in range(1, count):
         peer = offsets[offset - 1][0](me)
         pl.semaphore_signal(barrier, inc=1, device_id={axis: peer}, device_id_type=MESH)
-    pl.semaphore_wait(barrier, count - 1)
+    pl.semaphore_signal(barrier, inc=1, device_id={gather_axis: partner}, device_id_type=MESH)
+    pl.semaphore_wait(barrier, count)
+    to_partner = pltpu.make_async_remote_copy(
+        src_ref=chip_pieces,
+        dst_ref=partner_pieces,
+        send_sem=partner_send,
+        recv_sem=partner_recv,
+        device_id={gather_axis: partner},
+        device_id_type=MESH,
+    )
+    to_partner.start()
     local = pltpu.make_async_copy(send_ref.at[me], got_ref.at[me], local_sem)
     local.start()
     outgoing = []
@@ -179,9 +192,11 @@
         copy.start()
         outgoing.append(copy)
 
-    piece_count, unused_item, piece_width = pieces_ref.shape
-
-    def chunk_copy(index, slot):
+    chips, unused_item, piece_width = chip_pieces.shape
+    steps = 2 * chips
+
+    def chunk_copy(step, slot):
+        index = lax.rem(step, chips) * 2 + core + (step // chips) * (1 - 2 * core)
         return pltpu.make_async_copy(
             wq_hbm.at[pl.ds(pl.multiple_of(index * piece_width, piece_width), piece_width)],
             wq_buf.at[slot],
@@ -193,22 +208,32 @@
     k_ref[...] = jnp.zeros_like(k_ref)
     v_ref[...] = jnp.zeros_like(v_ref)
 
-    def project(index, carry):
-        slot = lax.rem(index, 2)
-        chunk_copy(index, slot).wait()
-
-        @pl.when(index + 1 < piece_count)
+    def project(step, piece):
+        slot = lax.rem(step, 2)
+        chunk_copy(step, slot).wait()
+
+        @pl.when(step + 1 < steps)
         def _():
-            chunk_copy(index + 1, 1 - slot).start()
-
+            chunk_copy(step + 1, 1 - slot).start()
+
+        index = lax.rem(step, chips) * 2 + core + (step // chips) * (1 - 2 * core)
         rows = pl.ds(pl.multiple_of(index * piece_width, piece_width), piece_width)
-        piece = pieces_ref[index]
         q_ref[...] += jnp.dot(piece, wq_buf[slot], preferred_element_type=jnp.float32)
         k_ref[...] += jnp.dot(piece, wk_ref[rows, :], preferred_element_type=jnp.float32)
         v_ref[...] += jnp.dot(piece, wv_ref[rows, :], preferred_element_type=jnp.float32)
+
+    def own_step(step, carry):
+        project(step, chip_pieces[step])
         return carry
 
-    lax.fori_loop(0, piece_count, project, 0)
+    def partner_step(step, carry):
+        project(step, partner_pieces[step - chips])
+        return carry
+
+    lax.fori_loop(0, chips, own_step, 0)
+    to_partner.wait_send()
+    to_partner.wait_recv()
+    lax.fori_loop(chips, steps, partner_step, 0)
 
     for offset in range(1, count):
         outgoing[offset - 1].wait_send()
@@ -225,11 +250,11 @@
     local.wait()
 
 
-def exchange_project(values, pieces, w_query, w_key, w_value, axis, count, collective):
-    piece_count, token_count, piece_width = pieces.shape
+def exchange_project(values, chip_pieces, w_query, w_key, w_value, axis, count, gather_axis, collective):
+    chips, token_count, piece_width = chip_pieces.shape
     vmem = pl.BlockSpec(memory_space=pltpu.VMEM)
     return pl.pallas_call(
-        lambda *refs: exchange_project_kernel(axis, count, *refs),
+        lambda *refs: exchange_project_kernel(axis, count, gather_axis, *refs),
         out_shape=(
             jax.ShapeDtypeStruct(values.shape, values.dtype),
             jax.ShapeDtypeStruct((token_count, w_query.shape[1]), jnp.float32),
@@ -239,20 +264,31 @@
         in_specs=[vmem, vmem, pl.BlockSpec(memory_space=pl.ANY), vmem, vmem],
         out_specs=(vmem, vmem, vmem, vmem),
         scratch_shapes=[
+            pltpu.VMEM(chip_pieces.shape, chip_pieces.dtype),
             pltpu.VMEM((2, piece_width, w_query.shape[1]), w_query.dtype),
             pltpu.SemaphoreType.DMA((count,)),
             pltpu.SemaphoreType.DMA((count,)),
             pltpu.SemaphoreType.DMA(()),
             pltpu.SemaphoreType.DMA((2,)),
+            pltpu.SemaphoreType.DMA(()),
+            pltpu.SemaphoreType.DMA(()),
         ],
         compiler_params=pltpu.CompilerParams(
             collective_id=collective, has_side_effects=True, vmem_limit_bytes=60 * 1024 * 1024
         ),
-    )(values, pieces, w_query, w_key, w_value)
-
-
-def sum_kernel(axis, count, part_ref, total_ref, held, first_send, first_recv, second_send, second_recv):
+    )(values, chip_pieces, w_query, w_key, w_value)
+
+
+def sum_kernel(axis, count, part_ref, piece_ref, total_ref, chip_pieces, held, first_send, first_recv,
+               second_send, second_recv, chip_send, chip_recv, piece_sem):
     me = lax.axis_index(axis)
+    chips = count // 2
+    chip = me // 2
+    core = lax.rem(me, 2)
+
+    def chip_peer(step):
+        return lax.rem(chip + step, chips) * 2 + core
+
     barrier = pltpu.get_barrier_semaphore()
     for offset in range(1, count):
         peer = lax.rem(me + offset, count)
@@ -271,6 +307,20 @@
         )
         copy.start()
         outgoing.append(copy)
+    own_piece = pltpu.make_async_copy(piece_ref, chip_pieces.at[chip], piece_sem)
+    own_piece.start()
+    chip_copies = []
+    for step in range(1, chips):
+        copy = pltpu.make_async_remote_copy(
+            src_ref=piece_ref,
+            dst_ref=chip_pieces.at[chip],
+            send_sem=chip_send.at[step],
+            recv_sem=chip_recv.at[step],
+            device_id={axis: chip_peer(step)},
+            device_id_type=MESH,
+        )
+        copy.start()
+        chip_copies.append(copy)
     held[me] = part_ref[me]
     for offset in range(1, count):
         outgoing[offset - 1].wait_send()
@@ -313,28 +363,49 @@
             device_id_type=MESH,
         )
         incoming.wait_recv()
-
-
-def axis_sum(values, axis, count, collective, out_dtype):
+    for step in range(1, chips):
+        chip_copies[step - 1].wait_send()
+        source_chip = lax.rem(chip + chips - step, chips)
+        incoming = pltpu.make_async_remote_copy(
+            src_ref=piece_ref,
+            dst_ref=chip_pieces.at[source_chip],
+            send_sem=chip_send.at[step],
+            recv_sem=chip_recv.at[step],
+            device_id={axis: source_chip * 2 + core},
+            device_id_type=MESH,
+        )
+        incoming.wait_recv()
+    own_piece.wait()
+
+
+def axis_sum(values, piece, axis, count, collective, out_dtype):
     chunks = values.reshape(count, -1, 128)
-    summed = pl.pallas_call(
+    chips = count // 2
+    vmem = pl.BlockSpec(memory_space=pltpu.VMEM)
+    summed, chip_pieces = pl.pallas_call(
         lambda *refs: sum_kernel(axis, count, *refs),
-        out_shape=jax.ShapeDtypeStruct(chunks.shape, out_dtype),
-        in_specs=[pl.BlockSpec(memory_space=pltpu.VMEM)],
-        out_specs=pl.BlockSpec(memory_space=pltpu.VMEM),
+        out_shape=(
+            jax.ShapeDtypeStruct(chunks.shape, out_dtype),
+            jax.ShapeDtypeStruct((chips,) + piece.shape, piece.dtype),
+        ),
+        in_specs=[vmem, vmem],
+        out_specs=(vmem, vmem),
         scratch_shapes=[
             pltpu.VMEM(chunks.shape, values.dtype),
             pltpu.SemaphoreType.DMA((count,)),
             pltpu.SemaphoreType.DMA((count,)),
             pltpu.SemaphoreType.DMA((count,)),
             pltpu.SemaphoreType.DMA((count,)),
+            pltpu.SemaphoreType.DMA((chips,)),
+            pltpu.SemaphoreType.DMA((chips,)),
+            pltpu.SemaphoreType.DMA(()),
         ],
         compiler_params=pltpu.CompilerParams(collective_id=collective, has_side_effects=True),
-    )(chunks)
-    return summed.reshape(values.shape)
-
-
-def owner_adapter_term(received, slot_ids, down_local, up_local):
+    )(chunks, piece)
+    return summed.reshape(values.shape), chip_pieces
+
+
+def owner_adapter_term(received, slot_ids, piece, down_local, up_local):
     sources, rows, part_width = received.shape
     local_adapters, unused_item, adapter_rank = down_local.shape
     query_width = up_local.shape[2]
@@ -345,7 +416,9 @@
     pick = slot_ids.reshape(sources * rows)[:, None] == jnp.arange(local_adapters, dtype=jnp.int32)[None, :]
     partial_value_sum = jnp.sum(jnp.where(pick[:, :, None], every_down, 0.0), axis=1)
     tp_count = lax.axis_size("tp")
-    summed = axis_sum(partial_value_sum.reshape(-1, 128), "tp", tp_count, 2, jnp.bfloat16)
+    summed, chip_pieces = axis_sum(
+        partial_value_sum.reshape(-1, 128), piece, "tp", tp_count, 2, jnp.bfloat16
+    )
     adapter_middle = summed.reshape(sources * rows, adapter_rank)
     spread_rows = jnp.where(pick[:, :, None], adapter_middle[:, None, :], jnp.zeros((), jnp.bfloat16))
     spread_rows = spread_rows.reshape(sources * rows, local_adapters * adapter_rank)
@@ -354,7 +427,7 @@
         up_local.reshape(local_adapters * adapter_rank, query_width),
         preferred_element_type=jnp.float32,
     ).astype(jnp.bfloat16)
-    return adapter_output.reshape(sources, rows, query_width)
+    return adapter_output.reshape(sources, rows, query_width), chip_pieces
 
 
 def body(
@@ -405,10 +478,11 @@
     send_ids = jnp.concatenate([send_ids, jnp.zeros_like(send_ids)], axis=1)
     got_tokens, got_ids = exchange((send_tokens, send_ids), "grp", group_count, 0)
     got_ids = jnp.repeat(got_ids[:, :CAP, 0].astype(jnp.int32), step_count, axis=1)
-    owner_out = owner_adapter_term(got_tokens, got_ids, pooled_down_weights, pool_up)
-    pieces = lax.all_gather(token_rows, "tp", axis=0, tiled=False)
+    owner_out, chip_pieces = owner_adapter_term(
+        got_tokens, got_ids, token_rows, pooled_down_weights, pool_up
+    )
     back, base_query_rows, key_base, value_base = exchange_project(
-        owner_out, pieces, w_query, w_key, w_value, "grp", group_count, 1
+        owner_out, chip_pieces, w_query, w_key, w_value, "grp", group_count, "tp", 1
     )
     adapter_output = jnp.dot(
         jnp.transpose(place_tokens),

time: 100 us -> 105 us (1.050)
  Pallas kernels: 60.5 us -> 80.2 us
  between operations: 13.7 us -> 0.33 us
  local copies, waits for them, and re-layouts: 7.57 us -> 5.54 us
    pallas_call x2, Pallas kernels: 36.7 us -> 56.4 us  [the longest x1 34.1 us: axis_sum(): pl.pallas_call(lambda *refs: sum_kernel(axis, count, *refs), out_shape=(j...]
    another operation x1 -> x0, local copies, waits for them, and re-layouts: 2.04 us -> none  [body(): pieces = lax.all_gather(token_rows, 'tp', axis=0, tiled=False)]
  transfers between devices with their start and end apart: 1 -> 0, of which waited for: 0 -> 0; matrix products, arithmetic and copies ran while one was open for 12% -> 0% of each run, Pallas kernels for 38% -> 0%
where the time goes in v6:
time: 105 us
  Pallas kernels  80.2 us (76%)
  matrix products  12.2 us (12%)
  other arithmetic  6.38 us (6%)
  local copies, waits for them, and re-layouts  5.54 us (5%)
    pallas_call x1, Pallas kernels, axis_sum(): pl.pallas_call(lambda *refs: sum_kernel(axis, count, *refs), out_shape=(j...  34.1 us
    pallas_call x1, Pallas kernels, exchange(): pl.pallas_call(lambda *refs: exchange_kernel(axis, count, arrays, *refs),...  23.8 us
    pallas_call x1, Pallas kernels, exchange_project(): pl.pallas_call(lambda *refs: exchange_project_kernel(axis, count, gather_...  22.3 us
    dot_general x1, matrix products, attend(): jnp.einsum('rskgd,rtkd->rskgt', queries, key_new, preferred_element_type=...  2.58 us

profile of v6, /device:TPU:1, one launch (start us, length us, event | category | flops | bytes accessed | tf_op | source)
XLA Modules:
  0.0 104.6 jit_solution(11128716819013618936)
XLA Ops:
  0.0 0.9 select_reduce_fusion.1
  1.0 0.2 convert_reduce_fusion
  1.2 0.1 add.100
  1.4 1.2 %reshape.288.refs_1_ = bf16[256,1024]{1,0:T(8,128)(2,1)S(1)} reshape(bf16[64,4,1024]{2,1,0:T(4,128)(2,1)} %param.11) | data formatting | bytes 1048576 | tf_op jit(solution)/shard_map/reshape | solution.py:471
  2.5 1.4 %convolution_convert_fusion = bf16[512,1024]{1,0:T(8,128)(2,1)} fusion(bf16[256,1024]{1,0:T(8,128)(2,1)S(1)} %reshape.288.refs_1_, s32[256]{0:T(256)S(1)} %add.100), kind=kOutput, calls=%fused_computation.1 | convolution fusion | flops 269090816 | bytes 1573888 | tf_op jit(solution)/shard_map/dot_general | solution.py:472
  4.0 0.1 fusion.8
  4.3 0.6 concatenate.21.refs_1_
  5.0 23.8 %shard_map.109 = (bf16[16,32,1024]{2,1,0:T(8,128)(2,1)}, bf16[16,16,128]{2,1,0:T(8,128)(2,1)}) custom-call(bf16[16,32,1024]{2,1,0:T(8,128)(2,1)} %bitcast.92, bf16[16,16,128]{2,1,0:T(8,128)(2,1)} %concatenate.21.refs_1_), custom_call_target="tpu_custom_call" | custom-call | tf_op jit(solution)/shard_map/pallas_call | solution.py:140
  28.8 0.8 slice_convert_fusion
  29.5 0.2 copy.34
  29.8 0.1 eq.85
  29.9 2.0 %fusion.49 = f32[512,512]{0,1:S(1)} fusion(bf16[512,1024]{1,0:T(8,128)(2,1)} %bitcast.99, bf16[1024,512]{0,1:T(8,128)(2,1)S(1)} %bitcast.90), kind=kOutput, calls=%fused_computation.89 | convolution fusion | flops 536870912 | bytes 3145728
  31.9 0.1 select_reduce_fusion
  32.0 0.1 copy.28
  32.2 0.8 reshape_reshape.3.refs_0_
  32.9 34.1 %shard_map.110 = (bf16[8,32,128]{2,1,0:T(8,128)(2,1)}, bf16[4,256,1024]{2,1,0:T(8,128)(2,1)}) custom-call(f32[8,32,128]{2,1,0:T(8,128)} %reshape_reshape.3.refs_0_, bf16[256,1024]{1,0:T(8,128)(2,1)} %copy-done.1), custom_call_target="tpu_custom_call" | custom-call | tf_op jit(solution)/shard_map/pallas_call | solution.py:385
  67.0 0.9 broadcast_in_dim.82
  67.9 0.1 copy.29
  68.1 1.7 %bitcast_convert_fusion = bf16[512,1024]{1,0:T(8,128)(2,1)} fusion(bf16[8,64,1024]{2,1,0:T(8,128)(2,1)S(1)} %copy-done.6, pred[512,8]{0,1:T(8,128)(4,1)S(1)} %iota_compare_fusion.8, bf16[512,64]{0,1:T(8,128)(2,1)S(1)} %copy.29), kind=kOutput, calls=%fused_computation | convolution fusion | flops 537657344 | bytes 2166784 | tf_op jit(solution)/shard_map/dot_general | solution.py:425
  69.8 22.3 %shard_map.111 = (bf16[16,32,1024]{2,1,0:T(8,128)(2,1)}, f32[256,1024]{1,0:T(8,128)}, f32[256,128]{1,0:T(8,128)}, f32[256,128]{1,0:T(8,128)}) custom-call(bf16[16,32,1024]{2,1,0:T(8,128)(2,1)} %bitcast.93, bf16[4,256,1024]{2,1,0:T(8,128)(2,1)} %get-tuple-element.16.refs_1_, bf16[8192,1024]{1,0:T(8,128)(2,1)} %refs_2_.1, bf16[8192,128]{1,0:T(8,128)(2,1)} %refs_3_.1, ...), custom_call_target="tpu_custom_call" | custom-call | tf_op jit(solution)/shard_map/pallas_call | solution.py:256
  92.1 2.0 %fusion.1 = f32[32,8,8,128]{3,1,2,0:T(8,128)S(1)} fusion(f32[256,1024]{1,0:T(8,128)} %get-tuple-element.17, bf16[512,1024]{1,0:T(8,128)(2,1)} %bitcast.95, s32[256]{0:T(256)S(1)} %add.100), kind=kOutput, calls=%fused_computation.5 | convolution fusion | flops 268828672 | bytes 3146752 | tf_op jit(solution)/shard_map/dot_general | solution.py:487
  94.1 0.2 copy.35
  94.5 1.1 %multiply_cosine_fusion.1 = (f32[64,4,64]{2,1,0:T(4,128)S(1)}, f32[64,4,64]{2,1,0:T(4,128)S(1)}) fusion(f32[64]{0:T(128)S(1)} %multiply_exponential_fusion, f32[64,4]{1,0:T(8,128)S(1)} %add_convert_fusion.1), kind=kLoop, calls=%fused_computation.43 | loop fusion | flops 16384 | bytes 132352 | tf_op jit(solution)/shard_map/cos | solution.py:25
  95.6 0.5 subtract_convert_fusion
  96.1 1.2 %fusion.34 = (bf16[64,4,64]{2,1,0:T(4,128)(2,1)S(1)}, bf16[64,4,64]{2,1,0:T(4,128)(2,1)S(1)}) fusion(f32[64,4,1,128]{3,1,0,2:T(4,128)S(1)} %bitcast.96, f32[64]{0:T(128)S(1)} %multiply_exponential_fusion, f32[64,4]{1,0:T(8,128)S(1)} %add_convert_fusion.1), kind=kLoop, calls=%fused_computation.57 | loop fusion | flops 147456 | bytes 197888 | tf_op jit(solution)/shard_map/concatenate | solution.py:29
  97.3 2.6 %fusion.48 = (f32[64,4,8]{2,1,0:T(4,128)S(1)}, f32[64,4,1,8,4]{3,4,1,0,2:T(4,128)S(1)}) fusion(bf16[64,4,8,64]{3,2,1,0:T(8,128)(2,1)S(1)} %get-tuple-element.24, bf16[64,4,8,64]{3,2,1,0:T(8,128)(2,1)S(1)} %get-tuple-element.23, bf16[64,4,64]{2,1,0:T(4,128)(2,1)S(1)} %get-tuple-element.26, bf16[64,4,64]{2,1,0:T(4,128)(2,1)S(1)} %get-tuple-element.25, ...), kind=kOutput, calls=%fused_computation.88 | convolution fusion | flops 3299328 | bytes 630800 | tf_op jit(solution)/shard_map/rskgd,rtkd->rskgt/dot_general | solution.py:41
  100.0 0.9 fusion.47
  100.9 0.5 fusion.16
  101.4 0.8 fusion.11
  102.2 0.9 convolution_bitcast_fusion
  103.2 0.5 fusion.5
  103.7 0.9 reshape.297
  (30 shorter events, 0.7 us)
Async XLA Ops:
  0.0 29.9 %copy-start = (bf16[8,1024,64]{1,2,0:T(8,128)(2,1)S(1)}, bf16[8,1024,64]{1,2,0:T(8,128)(2,1)}, u32[]{:S(2)}) copy-start(bf16[8,1024,64]{1,2,0:T(8,128)(2,1)} %param.18) | copy-start | bytes 3145732
  2.5 29.4 %copy-start.1 = (bf16[256,1024]{1,0:T(8,128)(2,1)}, bf16[256,1024]{1,0:T(8,128)(2,1)S(1)}, u32[]{:S(2)}) copy-start(bf16[256,1024]{1,0:T(8,128)(2,1)S(1)} %reshape.288.refs_1_) | copy-start | bytes 1572868
  31.9 36.2 %copy-start.6 = (bf16[8,64,1024]{2,1,0:T(8,128)(2,1)S(1)}, bf16[8,64,1024]{2,1,0:T(8,128)(2,1)}, u32[]{:S(2)}) copy-start(bf16[8,64,1024]{2,1,0:T(8,128)(2,1)} %param.19) | copy-start | bytes 3145732
  92.1 2.3 %copy-start.5 = (s32[64]{0:T(128)S(1)}, s32[64]{0:T(128)}, u32[]{:S(2)}) copy-start(s32[64]{0:T(128)} %param.14) | copy-start | bytes 772
  94.4 1.7 %copy-start.3 = (f32[256,128]{1,0:T(8,128)S(1)}, f32[256,128]{1,0:T(8,128)}, u32[]{:S(2)}) copy-start(f32[256,128]{1,0:T(8,128)} %get-tuple-element.19) | copy-start | bytes 393220
  95.6 4.4 %copy-start.2 = (bf16[64,64,128]{2,1,0:T(8,128)(2,1)S(1)}, bf16[64,64,128]{2,1,0:T(8,128)(2,1)}, u32[]{:S(2)}) copy-start(bf16[64,64,128]{2,1,0:T(8,128)(2,1)} %param.20) | copy-start | bytes 3145732
  100.8 1.3 %copy-start.7 = (bf16[64,64,128]{2,1,0:T(8,128)(2,1)S(1)}, bf16[64,64,128]{2,1,0:T(8,128)(2,1)}, u32[]{:S(2)}) copy-start(bf16[64,64,128]{2,1,0:T(8,128)(2,1)} %param.21) | copy-start | bytes 3145732
  102.2 0.9 copy-start.4

commit v7 on v5

--- a/solution.py
+++ b/solution.py
@@ -151,62 +151,48 @@
     )(*values)
 
 
-def exchange_gather_kernel(
-    axis, count, gather_axis, chips, arrays, *refs
-):
+def exchange_ring_kernel(axis, count, gather_axis, arrays, *refs):
     send_refs = refs[:arrays]
     piece_ref = refs[arrays]
     got_refs = refs[arrays + 1 : 2 * arrays + 1]
-    pieces_ref = refs[2 * arrays + 1]
-    send_sem, recv_sem, local_sem, chip_send, chip_recv, core_send, core_recv, piece_sem = refs[
-        2 * arrays + 2 :
-    ]
+    chip_pieces = refs[2 * arrays + 1]
+    (send_sem, recv_sem, local_sem, near_send, near_recv, far_send, far_recv,
+     piece_sem) = refs[2 * arrays + 2 :]
+    chips = chip_pieces.shape[0]
+    half = chip_pieces.shape[1] // 2
     me = lax.axis_index(axis)
     mine = lax.axis_index(gather_axis)
     chip = mine // 2
     core = lax.rem(mine, 2)
-    partner = chip * 2 + (1 - core)
-
-    def chip_peer(step):
-        return lax.rem(chip + step, chips) * 2 + core
+    right_chip = lax.rem(chip + 1, chips)
+    left_chip = lax.rem(chip + chips - 1, chips)
+    far_chip = lax.rem(chip + 2, chips)
+    right = right_chip * 2 + core
+    left = left_chip * 2 + core
 
     barrier = pltpu.get_barrier_semaphore()
     offsets = peer_offsets(count)
     for offset in range(1, count):
         peer = offsets[offset - 1][0](me)
         pl.semaphore_signal(barrier, inc=1, device_id={axis: peer}, device_id_type=MESH)
-    for step in range(1, chips):
-        pl.semaphore_signal(
-            barrier, inc=1, device_id={gather_axis: chip_peer(step)}, device_id_type=MESH
-        )
-    pl.semaphore_signal(barrier, inc=1, device_id={gather_axis: partner}, device_id_type=MESH)
-    pl.semaphore_wait(barrier, count - 1 + chips)
-
-    own_piece = pltpu.make_async_copy(piece_ref, pieces_ref.at[mine], piece_sem)
-    own_piece.start()
-    chip_copies = []
-    for step in range(1, chips):
+    pl.semaphore_signal(barrier, inc=1, device_id={gather_axis: right}, device_id_type=MESH)
+    pl.semaphore_signal(barrier, inc=1, device_id={gather_axis: left}, device_id_type=MESH)
+    pl.semaphore_wait(barrier, count + 1)
+
+    near = []
+    for side, target in ((0, right), (1, left)):
         copy = pltpu.make_async_remote_copy(
             src_ref=piece_ref,
-            dst_ref=pieces_ref.at[mine],
-            send_sem=chip_send.at[step],
-            recv_sem=chip_recv.at[step],
-            device_id={gather_axis: chip_peer(step)},
+            dst_ref=chip_pieces.at[chip],
+            send_sem=near_send.at[side],
+            recv_sem=near_recv.at[side],
+            device_id={gather_axis: target},
             device_id_type=MESH,
         )
         copy.start()
-        chip_copies.append(copy)
-    core_copies = []
-    copy = pltpu.make_async_remote_copy(
-        src_ref=piece_ref,
-        dst_ref=pieces_ref.at[mine],
-        send_sem=core_send.at[0],
-        recv_sem=core_recv.at[0],
-        device_id={gather_axis: partner},
-        device_id_type=MESH,
-    )
-    copy.start()
-    core_copies.append(copy)
+        near.append(copy)
+    own_piece = pltpu.make_async_copy(piece_ref, chip_pieces.at[chip], piece_sem)
+    own_piece.start()
 
     locals_ = []
     for which in range(arrays):
@@ -230,37 +216,39 @@
             copy.start()
             outgoing.append(copy)
 
-    for step in range(1, chips):
-        chip_copies[step - 1].wait_send()
-        source = chip_peer(chips - step)
+    far = []
+    for side, source_chip, source, target, rows in (
+        (0, left_chip, left, right, pl.ds(0, half)),
+        (1, right_chip, right, left, pl.ds(half, half)),
+    ):
+        near[side].wait_send()
         incoming = pltpu.make_async_remote_copy(
             src_ref=piece_ref,
-            dst_ref=pieces_ref.at[source],
-            send_sem=chip_send.at[step],
-            recv_sem=chip_recv.at[step],
+            dst_ref=chip_pieces.at[source_chip],
+            send_sem=near_send.at[side],
+            recv_sem=near_recv.at[side],
             device_id={gather_axis: source},
             device_id_type=MESH,
         )
         incoming.wait_recv()
         copy = pltpu.make_async_remote_copy(
-            src_ref=pieces_ref.at[source],
-            dst_ref=pieces_ref.at[source],
-            send_sem=core_send.at[step],
-            recv_sem=core_recv.at[step],
-            device_id={gather_axis: partner},
+            src_ref=chip_pieces.at[source_chip, rows],
+            dst_ref=chip_pieces.at[source_chip, rows],
+            send_sem=far_send.at[side],
+            recv_sem=far_recv.at[side],
+            device_id={gather_axis: target},
             device_id_type=MESH,
         )
         copy.start()
-        core_copies.append(copy)
-    for step in range(chips):
-        core_copies[step].wait_send()
-        source = lax.rem(chip + chips - step, chips) * 2 + (1 - core)
+        far.append(copy)
+    for side, source, rows in ((0, left, pl.ds(0, half)), (1, right, pl.ds(half, half))):
+        far[side].wait_send()
         incoming = pltpu.make_async_remote_copy(
-            src_ref=piece_ref,
-            dst_ref=pieces_ref.at[source],
-            send_sem=core_send.at[step],
-            recv_sem=core_recv.at[step],
-            device_id={gather_axis: partner},
+            src_ref=chip_pieces.at[far_chip, rows],
+            dst_ref=chip_pieces.at[far_chip, rows],
+            send_sem=far_send.at[side],
+            recv_sem=far_recv.at[side],
+            device_id={gather_axis: source},
             device_id_type=MESH,
         )
         incoming.wait_recv()
@@ -283,24 +271,24 @@
     own_piece.wait()
 
 
-def exchange_gather(values, piece, axis, count, gather_axis, gather_count, collective):
+def exchange_ring(values, piece, axis, count, gather_axis, collective):
     arrays = len(values)
-    chips = gather_count // 2
+    chips = lax.axis_size(gather_axis) // 2
     vmem = pl.BlockSpec(memory_space=pltpu.VMEM)
     outs = pl.pallas_call(
-        lambda *refs: exchange_gather_kernel(axis, count, gather_axis, chips, arrays, *refs),
+        lambda *refs: exchange_ring_kernel(axis, count, gather_axis, arrays, *refs),
         out_shape=tuple(jax.ShapeDtypeStruct(v.shape, v.dtype) for v in values)
-        + (jax.ShapeDtypeStruct((gather_count,) + piece.shape, piece.dtype),),
+        + (jax.ShapeDtypeStruct((chips,) + piece.shape, piece.dtype),),
         in_specs=[vmem] * (arrays + 1),
         out_specs=tuple([vmem] * (arrays + 1)),
         scratch_shapes=[
             pltpu.SemaphoreType.DMA((arrays, count)),
             pltpu.SemaphoreType.DMA((arrays, count)),
             pltpu.SemaphoreType.DMA((arrays,)),
-            pltpu.SemaphoreType.DMA((chips,)),
-            pltpu.SemaphoreType.DMA((chips,)),
-            pltpu.SemaphoreType.DMA((chips,)),
-            pltpu.SemaphoreType.DMA((chips,)),
+            pltpu.SemaphoreType.DMA((2,)),
+            pltpu.SemaphoreType.DMA((2,)),
+            pltpu.SemaphoreType.DMA((2,)),
+            pltpu.SemaphoreType.DMA((2,)),
             pltpu.SemaphoreType.DMA(()),
         ],
         compiler_params=pltpu.CompilerParams(collective_id=collective, has_side_effects=True),
@@ -309,17 +297,30 @@
 
 
 def exchange_project_kernel(
-    axis, count, send_ref, pieces_ref, wq_hbm, wk_ref, wv_ref,
+    axis, count, gather_axis, send_ref, chip_pieces, wq_hbm, wk_ref, wv_ref,
     got_ref, q_ref, k_ref, v_ref,
-    wq_buf, send_sem, recv_sem, local_sem, wq_sem,
+    partner_pieces, wq_buf, send_sem, recv_sem, local_sem, wq_sem, partner_send, partner_recv,
 ):
     me = lax.axis_index(axis)
+    mine = lax.axis_index(gather_axis)
+    core = lax.rem(mine, 2)
+    partner = (mine // 2) * 2 + (1 - core)
     barrier = pltpu.get_barrier_semaphore()
     offsets = peer_offsets(count)
     for offset in range(1, count):
         peer = offsets[offset - 1][0](me)
         pl.semaphore_signal(barrier, inc=1, device_id={axis: peer}, device_id_type=MESH)
-    pl.semaphore_wait(barrier, count - 1)
+    pl.semaphore_signal(barrier, inc=1, device_id={gather_axis: partner}, device_id_type=MESH)
+    pl.semaphore_wait(barrier, count)
+    to_partner = pltpu.make_async_remote_copy(
+        src_ref=chip_pieces,
+        dst_ref=partner_pieces,
+        send_sem=partner_send,
+        recv_sem=partner_recv,
+        device_id={gather_axis: partner},
+        device_id_type=MESH,
+    )
+    to_partner.start()
     local = pltpu.make_async_copy(send_ref.at[me], got_ref.at[me], local_sem)
     local.start()
     outgoing = []
@@ -336,9 +337,11 @@
         copy.start()
         outgoing.append(copy)
 
-    piece_count, unused_item, piece_width = pieces_ref.shape
-
-    def chunk_copy(index, slot):
+    chips, unused_item, piece_width = chip_pieces.shape
+    steps = 2 * chips
+
+    def chunk_copy(step, slot):
+        index = lax.rem(step, chips) * 2 + core + (step // chips) * (1 - 2 * core)
         return pltpu.make_async_copy(
             wq_hbm.at[pl.ds(pl.multiple_of(index * piece_width, piece_width), piece_width)],
             wq_buf.at[slot],
@@ -350,22 +353,32 @@
     k_ref[...] = jnp.zeros_like(k_ref)
     v_ref[...] = jnp.zeros_like(v_ref)
 
-    def project(index, carry):
-        slot = lax.rem(index, 2)
-        chunk_copy(index, slot).wait()
-
-        @pl.when(index + 1 < piece_count)
+    def project(step, piece):
+        slot = lax.rem(step, 2)
+        chunk_copy(step, slot).wait()
+
+        @pl.when(step + 1 < steps)
         def _():
-            chunk_copy(index + 1, 1 - slot).start()
-
+            chunk_copy(step + 1, 1 - slot).start()
+
+        index = lax.rem(step, chips) * 2 + core + (step // chips) * (1 - 2 * core)
         rows = pl.ds(pl.multiple_of(index * piece_width, piece_width), piece_width)
-        piece = pieces_ref[index]
         q_ref[...] += jnp.dot(piece, wq_buf[slot], preferred_element_type=jnp.float32)
         k_ref[...] += jnp.dot(piece, wk_ref[rows, :], preferred_element_type=jnp.float32)
         v_ref[...] += jnp.dot(piece, wv_ref[rows, :], preferred_element_type=jnp.float32)
+
+    def own_step(step, carry):
+        project(step, chip_pieces[step])
         return carry
 
-    lax.fori_loop(0, piece_count, project, 0)
+    def partner_step(step, carry):
+        project(step, partner_pieces[step - chips])
+        return carry
+
+    lax.fori_loop(0, chips, own_step, 0)
+    to_partner.wait_send()
+    to_partner.wait_recv()
+    lax.fori_loop(chips, steps, partner_step, 0)
 
     for offset in range(1, count):
         outgoing[offset - 1].wait_send()
@@ -382,11 +395,11 @@
     local.wait()
 
 
-def exchange_project(values, pieces, w_query, w_key, w_value, axis, count, collective):
-    piece_count, token_count, piece_width = pieces.shape
+def exchange_project(values, chip_pieces, w_query, w_key, w_value, axis, count, gather_axis, collective):
+    chips, token_count, piece_width = chip_pieces.shape
     vmem = pl.BlockSpec(memory_space=pltpu.VMEM)
     return pl.pallas_call(
-        lambda *refs: exchange_project_kernel(axis, count, *refs),
+        lambda *refs: exchange_project_kernel(axis, count, gather_axis, *refs),
         out_shape=(
             jax.ShapeDtypeStruct(values.shape, values.dtype),
             jax.ShapeDtypeStruct((token_count, w_query.shape[1]), jnp.float32),
@@ -396,16 +409,19 @@
         in_specs=[vmem, vmem, pl.BlockSpec(memory_space=pl.ANY), vmem, vmem],
         out_specs=(vmem, vmem, vmem, vmem),
         scratch_shapes=[
+            pltpu.VMEM(chip_pieces.shape, chip_pieces.dtype),
             pltpu.VMEM((2, piece_width, w_query.shape[1]), w_query.dtype),
             pltpu.SemaphoreType.DMA((count,)),
             pltpu.SemaphoreType.DMA((count,)),
             pltpu.SemaphoreType.DMA(()),
             pltpu.SemaphoreType.DMA((2,)),
+            pltpu.SemaphoreType.DMA(()),
+            pltpu.SemaphoreType.DMA(()),
         ],
         compiler_params=pltpu.CompilerParams(
             collective_id=collective, has_side_effects=True, vmem_limit_bytes=60 * 1024 * 1024
         ),
-    )(values, pieces, w_query, w_key, w_value)
+    )(values, chip_pieces, w_query, w_key, w_value)
 
 
 def sum_kernel(axis, count, part_ref, total_ref, held, first_send, first_recv, second_send, second_recv):
@@ -560,13 +576,13 @@
     ).astype(jnp.bfloat16)
     send_ids = jnp.broadcast_to(send_ids.reshape(group_count, CAP, 1), (group_count, CAP, 128))
     send_ids = jnp.concatenate([send_ids, jnp.zeros_like(send_ids)], axis=1)
-    (got_tokens, got_ids), pieces = exchange_gather(
-        (send_tokens, send_ids), token_rows, "grp", group_count, "tp", tp_count, 0
+    (got_tokens, got_ids), chip_pieces = exchange_ring(
+        (send_tokens, send_ids), token_rows, "grp", group_count, "tp", 0
     )
     got_ids = jnp.repeat(got_ids[:, :CAP, 0].astype(jnp.int32), step_count, axis=1)
     owner_out = owner_adapter_term(got_tokens, got_ids, pooled_down_weights, pool_up)
     back, base_query_rows, key_base, value_base = exchange_project(
-        owner_out, pieces, w_query, w_key, w_value, "grp", group_count, 1
+        owner_out, chip_pieces, w_query, w_key, w_value, "grp", group_count, "tp", 1
     )
     adapter_output = jnp.dot(
         jnp.transpose(place_tokens),

time: 98.5 us -> 91 us (0.924)
  Pallas kernels: 73.4 us -> 65.8 us
    pallas_call x2, Pallas kernels: 63.1 us -> 52.2 us  [the longest x1 30.5 us: exchange_ring(): pl.pallas_call(lambda *refs: exchange_ring_kernel(axis, count, gather_axi...]
    pallas_call x1, Pallas kernels: 10.3 us -> 13.6 us  [axis_sum(): pl.pallas_call(lambda *refs: sum_kernel(axis, count, *refs), out_shape=ja...]
where the time goes in v7:
time: 91 us; the launch traced here: 90.2 us
  Pallas kernels  65.8 us (72%)
  matrix products  12.2 us (13%)
  other arithmetic  6.39 us (7%)
  local copies, waits for them, and re-layouts  5.56 us (6%)
    pallas_call x1, Pallas kernels, exchange_ring(): pl.pallas_call(lambda *refs: exchange_ring_kernel(axis, count, gather_axi...  30.5 us
    pallas_call x1, Pallas kernels, exchange_project(): pl.pallas_call(lambda *refs: exchange_project_kernel(axis, count, gather_...  21.7 us
    pallas_call x1, Pallas kernels, axis_sum(): pl.pallas_call(lambda *refs: sum_kernel(axis, count, *refs), out_shape=ja...  13.6 us
    dot_general x1, matrix products, attend(): jnp.einsum('rskgd,rtkd->rskgt', queries, key_new, preferred_element_type=...  2.58 us
    dot_general x1, matrix products, body(): jnp.dot(jnp.transpose(place_tokens), back.reshape(group_count * CAP * ste...  2.03 us
    unnamed x1, matrix products  1.96 us

profile of v7, /device:TPU:1, one launch (start us, length us, event | category | flops | bytes accessed | tf_op | source)
XLA Modules:
  0.0 90.2 jit_solution(16964121474142730034)
XLA Ops:
  0.0 0.9 %select_reduce_fusion.1 = s32[64]{0:T(128)S(1)} fusion(s32[128]{0:T(128)} %param.13, s32[64]{0:T(128)} %param.12), kind=kLoop, calls=%fused_computation.64 | loop fusion | flops 24512 | bytes 1024 | tf_op jit(solution)/shard_map/reduce_sum | solution.py:557
  1.0 0.2 convert_reduce_fusion
  1.2 0.1 add.100
  1.4 1.2 %reshape.288.refs_2_ = bf16[256,1024]{1,0:T(8,128)(2,1)S(1)} reshape(bf16[64,4,1024]{2,1,0:T(4,128)(2,1)} %param.11) | data formatting | bytes 1048576 | tf_op jit(solution)/shard_map/reshape | solution.py:571
  2.5 1.4 %convolution_convert_fusion = bf16[512,1024]{1,0:T(8,128)(2,1)} fusion(bf16[256,1024]{1,0:T(8,128)(2,1)S(1)} %reshape.288.refs_2_, s32[256]{0:T(256)S(1)} %add.100), kind=kOutput, calls=%fused_computation.1 | convolution fusion | flops 269090816 | bytes 1573888 | tf_op jit(solution)/shard_map/dot_general | solution.py:572
  4.0 0.1 fusion.8
  4.3 0.6 concatenate.21.refs_1_
  5.0 30.5 %shard_map.109 = (bf16[16,32,1024]{2,1,0:T(8,128)(2,1)}, bf16[16,16,128]{2,1,0:T(8,128)(2,1)}, bf16[4,256,1024]{2,1,0:T(8,128)(2,1)}) custom-call(bf16[16,32,1024]{2,1,0:T(8,128)(2,1)} %bitcast.92, bf16[16,16,128]{2,1,0:T(8,128)(2,1)} %concatenate.21.refs_1_, bf16[256,1024]{1,0:T(8,128)(2,1)} %copy-done.1), custom_call_target="tpu_custom_call" | custom-call | tf_op jit(solution)/shard_map/pallas_call | solution.py:278
  35.4 0.8 slice_convert_fusion
  36.2 0.2 copy.34
  36.4 0.1 eq.85
  36.6 2.0 %fusion.49 = f32[512,512]{0,1:S(1)} fusion(bf16[512,1024]{1,0:T(8,128)(2,1)} %bitcast.99, bf16[1024,512]{0,1:T(8,128)(2,1)S(1)} %bitcast.90), kind=kOutput, calls=%fused_computation.89 | convolution fusion | flops 536870912 | bytes 3145728
  38.6 0.1 select_reduce_fusion
  38.7 0.1 copy.28
  38.8 0.8 reshape_reshape.3.refs_0_
  39.6 13.6 %shard_map.110 = bf16[8,32,128]{2,1,0:T(8,128)(2,1)} custom-call(f32[8,32,128]{2,1,0:T(8,128)} %reshape_reshape.3.refs_0_), custom_call_target="tpu_custom_call" | custom-call | tf_op jit(solution)/shard_map/pallas_call | solution.py:493
  53.2 0.9 %broadcast_in_dim.82 = bf16[512,64]{1,0:T(8,128)(2,1)S(1)} reshape(bf16[8,32,128]{2,1,0:T(8,128)(2,1)} %shard_map.110) | data formatting | bytes 131072 | tf_op jit(solution)/shard_map/jit(_where)/broadcast_in_dim | solution.py:523
  54.2 0.1 copy.29
  54.3 1.7 %bitcast_convert_fusion = bf16[512,1024]{1,0:T(8,128)(2,1)} fusion(bf16[8,64,1024]{2,1,0:T(8,128)(2,1)S(1)} %copy-done.6, pred[512,8]{0,1:T(8,128)(4,1)S(1)} %iota_compare_fusion.8, bf16[512,64]{0,1:T(8,128)(2,1)S(1)} %copy.29), kind=kOutput, calls=%fused_computation | convolution fusion | flops 537657344 | bytes 2166784 | tf_op jit(solution)/shard_map/dot_general | solution.py:525
  56.0 21.7 %shard_map.111 = (bf16[16,32,1024]{2,1,0:T(8,128)(2,1)}, f32[256,1024]{1,0:T(8,128)}, f32[256,128]{1,0:T(8,128)}, f32[256,128]{1,0:T(8,128)}) custom-call(bf16[16,32,1024]{2,1,0:T(8,128)(2,1)} %bitcast.93, bf16[4,256,1024]{2,1,0:T(8,128)(2,1)} %get-tuple-element.14.refs_1_, bf16[8192,1024]{1,0:T(8,128)(2,1)} %refs_2_.1, bf16[8192,128]{1,0:T(8,128)(2,1)} %refs_3_.1, ...), custom_call_target="tpu_custom_call" | custom-call | tf_op jit(solution)/shard_map/pallas_call | solution.py:401
  77.7 2.0 %fusion.1 = f32[32,8,8,128]{3,1,2,0:T(8,128)S(1)} fusion(f32[256,1024]{1,0:T(8,128)} %get-tuple-element.15, bf16[512,1024]{1,0:T(8,128)(2,1)} %bitcast.95, s32[256]{0:T(256)S(1)} %add.100), kind=kOutput, calls=%fused_computation.5 | convolution fusion | flops 268828672 | bytes 3146752 | tf_op jit(solution)/shard_map/dot_general | solution.py:587
  79.8 0.2 copy.35
  80.1 1.1 %multiply_cosine_fusion.1 = (f32[64,4,64]{2,1,0:T(4,128)S(1)}, f32[64,4,64]{2,1,0:T(4,128)S(1)}) fusion(f32[64]{0:T(128)S(1)} %multiply_exponential_fusion, f32[64,4]{1,0:T(8,128)S(1)} %add_convert_fusion.1), kind=kLoop, calls=%fused_computation.43 | loop fusion | flops 16384 | bytes 132352 | tf_op jit(solution)/shard_map/cos | solution.py:25
  81.2 0.5 subtract_convert_fusion
  81.7 1.2 %fusion.34 = (bf16[64,4,64]{2,1,0:T(4,128)(2,1)S(1)}, bf16[64,4,64]{2,1,0:T(4,128)(2,1)S(1)}) fusion(f32[64,4,1,128]{3,1,0,2:T(4,128)S(1)} %bitcast.96, f32[64]{0:T(128)S(1)} %multiply_exponential_fusion, f32[64,4]{1,0:T(8,128)S(1)} %add_convert_fusion.1), kind=kLoop, calls=%fused_computation.57 | loop fusion | flops 147456 | bytes 197888 | tf_op jit(solution)/shard_map/concatenate | solution.py:29
  83.0 2.6 %fusion.48 = (f32[64,4,8]{2,1,0:T(4,128)S(1)}, f32[64,4,1,8,4]{3,4,1,0,2:T(4,128)S(1)}) fusion(bf16[64,4,8,64]{3,2,1,0:T(8,128)(2,1)S(1)} %get-tuple-element.22, bf16[64,4,8,64]{3,2,1,0:T(8,128)(2,1)S(1)} %get-tuple-element.21, bf16[64,4,64]{2,1,0:T(4,128)(2,1)S(1)} %get-tuple-element.24, bf16[64,4,64]{2,1,0:T(4,128)(2,1)S(1)} %get-tuple-element.23, ...), kind=kOutput, calls=%fused_computation.88 | convolution fusion | flops 3299328 | bytes 630800 | tf_op jit(solution)/shard_map/rskgd,rtkd->rskgt/dot_general | solution.py:41
  85.6 0.9 fusion.47
  86.5 0.5 fusion.16
  87.0 0.8 fusion.11
  87.8 0.9 %convolution_bitcast_fusion = f32[64,128,4,8]{1,3,2,0:T(8,128)S(1)} fusion(bf16[64,64,128]{2,1,0:T(8,128)(2,1)S(1)} %copy-done.7, f32[64,4,1,8,64]{4,3,1,0,2:T(8,128)S(1)} %get-tuple-element.28, f32[64,4,8]{2,1,0:T(4,128)S(1)} %add.108, f32[64,4,8]{2,1,0:T(4,128)S(1)} %max.9), kind=kOutput, calls=%fused_computation.7 | convolution fusion | flops 33947648 | bytes 2637824 | tf_op jit(solution)/shard_map/rskgl,rlkd->rskgd/dot_general | solution.py:58
  88.8 0.5 fusion.5
  89.3 0.9 %reshape.297 = bf16[64,4,1024]{2,1,0:T(4,128)(2,1)} reshape(bf16[64,4,1,8,128]{4,3,1,0,2:T(8,128)(2,1)S(1)} %fusion.5) | data formatting | bytes 1048576 | tf_op jit(solution)/shard_map/reshape | solution.py:603
  (30 shorter events, 0.7 us)
Async XLA Ops:
  0.0 36.6 %copy-start = (bf16[8,1024,64]{1,2,0:T(8,128)(2,1)S(1)}, bf16[8,1024,64]{1,2,0:T(8,128)(2,1)}, u32[]{:S(2)}) copy-start(bf16[8,1024,64]{1,2,0:T(8,128)(2,1)} %param.18) | copy-start | bytes 3145732
  2.5 2.4 %copy-start.1 = (bf16[256,1024]{1,0:T(8,128)(2,1)}, bf16[256,1024]{1,0:T(8,128)(2,1)S(1)}, u32[]{:S(2)}) copy-start(bf16[256,1024]{1,0:T(8,128)(2,1)S(1)} %reshape.288.refs_2_) | copy-start | bytes 1572868
  38.6 15.7 %copy-start.6 = (bf16[8,64,1024]{2,1,0:T(8,128)(2,1)S(1)}, bf16[8,64,1024]{2,1,0:T(8,128)(2,1)}, u32[]{:S(2)}) copy-start(bf16[8,64,1024]{2,1,0:T(8,128)(2,1)} %param.19) | copy-start | bytes 3145732
  77.7 2.3 %copy-start.5 = (s32[64]{0:T(128)S(1)}, s32[64]{0:T(128)}, u32[]{:S(2)}) copy-start(s32[64]{0:T(128)} %param.14) | copy-start | bytes 772
  80.0 1.7 %copy-start.3 = (f32[256,128]{1,0:T(8,128)S(1)}, f32[256,128]{1,0:T(8,128)}, u32[]{:S(2)}) copy-start(f32[256,128]{1,0:T(8,128)} %get-tuple-element.17) | copy-start | bytes 393220
  81.2 4.4 %copy-start.2 = (bf16[64,64,128]{2,1,0:T(8,128)(2,1)S(1)}, bf16[64,64,128]{2,1,0:T(8,128)(2,1)}, u32[]{:S(2)}) copy-start(bf16[64,64,128]{2,1,0:T(8,128)(2,1)} %param.20) | copy-start | bytes 3145732
  86.5 1.3 %copy-start.7 = (bf16[64,64,128]{2,1,0:T(8,128)(2,1)S(1)}, bf16[64,64,128]{2,1,0:T(8,128)(2,1)}, u32[]{:S(2)}) copy-start(bf16[64,64,128]{2,1,0:T(8,128)(2,1)} %param.21) | copy-start | bytes 3145732
  87.8 1.0 %copy-start.4 = (f32[256,128]{1,0:T(8,128)S(1)}, f32[256,128]{1,0:T(8,128)}, u32[]{:S(2)}) copy-start(f32[256,128]{1,0:T(8,128)} %get-tuple-element.18) | copy-start | bytes 393220

commit v8 on v7

--- a/solution.py
+++ b/solution.py
@@ -156,17 +156,14 @@
     piece_ref = refs[arrays]
     got_refs = refs[arrays + 1 : 2 * arrays + 1]
     chip_pieces = refs[2 * arrays + 1]
-    (send_sem, recv_sem, local_sem, near_send, near_recv, far_send, far_recv,
-     piece_sem) = refs[2 * arrays + 2 :]
-    chips = chip_pieces.shape[0]
-    half = chip_pieces.shape[1] // 2
+    send_sem, recv_sem, local_sem, near_send, near_recv, piece_sem = refs[2 * arrays + 2 :]
+    chips = lax.axis_size(gather_axis) // 2
     me = lax.axis_index(axis)
     mine = lax.axis_index(gather_axis)
     chip = mine // 2
     core = lax.rem(mine, 2)
     right_chip = lax.rem(chip + 1, chips)
     left_chip = lax.rem(chip + chips - 1, chips)
-    far_chip = lax.rem(chip + 2, chips)
     right = right_chip * 2 + core
     left = left_chip * 2 + core
 
@@ -183,7 +180,7 @@
     for side, target in ((0, right), (1, left)):
         copy = pltpu.make_async_remote_copy(
             src_ref=piece_ref,
-            dst_ref=chip_pieces.at[chip],
+            dst_ref=chip_pieces.at[1 + side],
             send_sem=near_send.at[side],
             recv_sem=near_recv.at[side],
             device_id={gather_axis: target},
@@ -191,7 +188,7 @@
         )
         copy.start()
         near.append(copy)
-    own_piece = pltpu.make_async_copy(piece_ref, chip_pieces.at[chip], piece_sem)
+    own_piece = pltpu.make_async_copy(piece_ref, chip_pieces.at[0], piece_sem)
     own_piece.start()
 
     locals_ = []
@@ -216,38 +213,13 @@
             copy.start()
             outgoing.append(copy)
 
-    far = []
-    for side, source_chip, source, target, rows in (
-        (0, left_chip, left, right, pl.ds(0, half)),
-        (1, right_chip, right, left, pl.ds(half, half)),
-    ):
+    for side, source in ((0, left), (1, right)):
         near[side].wait_send()
         incoming = pltpu.make_async_remote_copy(
             src_ref=piece_ref,
-            dst_ref=chip_pieces.at[source_chip],
+            dst_ref=chip_pieces.at[1 + side],
             send_sem=near_send.at[side],
             recv_sem=near_recv.at[side],
-            device_id={gather_axis: source},
-            device_id_type=MESH,
-        )
-        incoming.wait_recv()
-        copy = pltpu.make_async_remote_copy(
-            src_ref=chip_pieces.at[source_chip, rows],
-            dst_ref=chip_pieces.at[source_chip, rows],
-            send_sem=far_send.at[side],
-            recv_sem=far_recv.at[side],
-            device_id={gather_axis: target},
-            device_id_type=MESH,
-        )
-        copy.start()
-        far.append(copy)
-    for side, source, rows in ((0, left, pl.ds(0, half)), (1, right, pl.ds(half, half))):
-        far[side].wait_send()
-        incoming = pltpu.make_async_remote_copy(
-            src_ref=chip_pieces.at[far_chip, rows],
-            dst_ref=chip_pieces.at[far_chip, rows],
-            send_sem=far_send.at[side],
-            recv_sem=far_recv.at[side],
             device_id={gather_axis: source},
             device_id_type=MESH,
         )
@@ -273,12 +245,11 @@
 
 def exchange_ring(values, piece, axis, count, gather_axis, collective):
     arrays = len(values)
-    chips = lax.axis_size(gather_axis) // 2
     vmem = pl.BlockSpec(memory_space=pltpu.VMEM)
     outs = pl.pallas_call(
         lambda *refs: exchange_ring_kernel(axis, count, gather_axis, arrays, *refs),
         out_shape=tuple(jax.ShapeDtypeStruct(v.shape, v.dtype) for v in values)
-        + (jax.ShapeDtypeStruct((chips,) + piece.shape, piece.dtype),),
+        + (jax.ShapeDtypeStruct((3,) + piece.shape, piece.dtype),),
         in_specs=[vmem] * (arrays + 1),
         out_specs=tuple([vmem] * (arrays + 1)),
         scratch_shapes=[
@@ -287,8 +258,6 @@
             pltpu.SemaphoreType.DMA((arrays,)),
             pltpu.SemaphoreType.DMA((2,)),
             pltpu.SemaphoreType.DMA((2,)),
-            pltpu.SemaphoreType.DMA((2,)),
-            pltpu.SemaphoreType.DMA((2,)),
             pltpu.SemaphoreType.DMA(()),
         ],
         compiler_params=pltpu.CompilerParams(collective_id=collective, has_side_effects=True),
@@ -297,26 +266,46 @@
 
 
 def exchange_project_kernel(
-    axis, count, gather_axis, send_ref, chip_pieces, wq_hbm, wk_ref, wv_ref,
+    axis, count, gather_axis, send_ref, near_pieces, wq_hbm, wk_ref, wv_ref,
     got_ref, q_ref, k_ref, v_ref,
-    partner_pieces, wq_buf, send_sem, recv_sem, local_sem, wq_sem, partner_send, partner_recv,
+    far_piece, partner_near, partner_far, wq_buf, send_sem, recv_sem, local_sem, wq_sem,
+    far_send, far_recv, partner_send, partner_recv,
 ):
     me = lax.axis_index(axis)
     mine = lax.axis_index(gather_axis)
+    chips = lax.axis_size(gather_axis) // 2
+    chip = mine // 2
     core = lax.rem(mine, 2)
-    partner = (mine // 2) * 2 + (1 - core)
+    partner = chip * 2 + (1 - core)
+    right = lax.rem(chip + 1, chips) * 2 + core
+    left = lax.rem(chip + chips - 1, chips) * 2 + core
+    half = far_piece.shape[0] // 2
     barrier = pltpu.get_barrier_semaphore()
     offsets = peer_offsets(count)
     for offset in range(1, count):
         peer = offsets[offset - 1][0](me)
         pl.semaphore_signal(barrier, inc=1, device_id={axis: peer}, device_id_type=MESH)
-    pl.semaphore_signal(barrier, inc=1, device_id={gather_axis: partner}, device_id_type=MESH)
-    pl.semaphore_wait(barrier, count)
+    for neighbour in (partner, right, left):
+        pl.semaphore_signal(barrier, inc=1, device_id={gather_axis: neighbour}, device_id_type=MESH)
+    pl.semaphore_wait(barrier, count + 2)
+
+    far_out = []
+    for side, slot, target, rows in ((0, 1, right, pl.ds(0, half)), (1, 2, left, pl.ds(half, half))):
+        copy = pltpu.make_async_remote_copy(
+            src_ref=near_pieces.at[slot, rows],
+            dst_ref=far_piece.at[rows],
+            send_sem=far_send.at[side],
+            recv_sem=far_recv.at[side],
+            device_id={gather_axis: target},
+            device_id_type=MESH,
+        )
+        copy.start()
+        far_out.append(copy)
     to_partner = pltpu.make_async_remote_copy(
-        src_ref=chip_pieces,
-        dst_ref=partner_pieces,
-        send_sem=partner_send,
-        recv_sem=partner_recv,
+        src_ref=near_pieces,
+        dst_ref=partner_near,
+        send_sem=partner_send.at[0],
+        recv_sem=partner_recv.at[0],
         device_id={gather_axis: partner},
         device_id_type=MESH,
     )
@@ -337,48 +326,66 @@
         copy.start()
         outgoing.append(copy)
 
-    chips, unused_item, piece_width = chip_pieces.shape
-    steps = 2 * chips
-
-    def chunk_copy(step, slot):
-        index = lax.rem(step, chips) * 2 + core + (step // chips) * (1 - 2 * core)
+    piece_width = near_pieces.shape[2]
+    chip_shift = (0, chips - 1, 1, 2)
+
+    def piece_index(step):
+        piece_core = core if step < 4 else 1 - core
+        return lax.rem(chip + chip_shift[step % 4], chips) * 2 + piece_core
+
+    def chunk_copy(step):
+        index = piece_index(step)
         return pltpu.make_async_copy(
             wq_hbm.at[pl.ds(pl.multiple_of(index * piece_width, piece_width), piece_width)],
-            wq_buf.at[slot],
-            wq_sem.at[slot],
-        )
-
-    chunk_copy(0, 0).start()
+            wq_buf.at[step % 2],
+            wq_sem.at[step % 2],
+        )
+
+    chunk_copy(0).start()
     q_ref[...] = jnp.zeros_like(q_ref)
     k_ref[...] = jnp.zeros_like(k_ref)
     v_ref[...] = jnp.zeros_like(v_ref)
 
     def project(step, piece):
-        slot = lax.rem(step, 2)
-        chunk_copy(step, slot).wait()
-
-        @pl.when(step + 1 < steps)
-        def _():
-            chunk_copy(step + 1, 1 - slot).start()
-
-        index = lax.rem(step, chips) * 2 + core + (step // chips) * (1 - 2 * core)
+        chunk_copy(step).wait()
+        if step + 1 < 8:
+            chunk_copy(step + 1).start()
+        index = piece_index(step)
         rows = pl.ds(pl.multiple_of(index * piece_width, piece_width), piece_width)
-        q_ref[...] += jnp.dot(piece, wq_buf[slot], preferred_element_type=jnp.float32)
+        q_ref[...] += jnp.dot(piece, wq_buf[step % 2], preferred_element_type=jnp.float32)
         k_ref[...] += jnp.dot(piece, wk_ref[rows, :], preferred_element_type=jnp.float32)
         v_ref[...] += jnp.dot(piece, wv_ref[rows, :], preferred_element_type=jnp.float32)
 
-    def own_step(step, carry):
-        project(step, chip_pieces[step])
-        return carry
-
-    def partner_step(step, carry):
-        project(step, partner_pieces[step - chips])
-        return carry
-
-    lax.fori_loop(0, chips, own_step, 0)
+    for step in range(3):
+        project(step, near_pieces[step])
+    for side, source, rows in ((0, left, pl.ds(0, half)), (1, right, pl.ds(half, half))):
+        far_out[side].wait_send()
+        incoming = pltpu.make_async_remote_copy(
+            src_ref=near_pieces.at[1, rows],
+            dst_ref=far_piece.at[rows],
+            send_sem=far_send.at[side],
+            recv_sem=far_recv.at[side],
+            device_id={gather_axis: source},
+            device_id_type=MESH,
+        )
+        incoming.wait_recv()
+    far_to_partner = pltpu.make_async_remote_copy(
+        src_ref=far_piece,
+        dst_ref=partner_far,
+        send_sem=partner_send.at[1],
+        recv_sem=partner_recv.at[1],
+        device_id={gather_axis: partner},
+        device_id_type=MESH,
+    )
+    far_to_partner.start()
+    project(3, far_piece[...])
     to_partner.wait_send()
     to_partner.wait_recv()
-    lax.fori_loop(chips, steps, partner_step, 0)
+    for step in range(3):
+        project(4 + step, partner_near[step])
+    far_to_partner.wait_send()
+    far_to_partner.wait_recv()
+    project(7, partner_far[...])
 
     for offset in range(1, count):
         outgoing[offset - 1].wait_send()
@@ -395,8 +402,8 @@
     local.wait()
 
 
-def exchange_project(values, chip_pieces, w_query, w_key, w_value, axis, count, gather_axis, collective):
-    chips, token_count, piece_width = chip_pieces.shape
+def exchange_project(values, near_pieces, w_query, w_key, w_value, axis, count, gather_axis, collective):
+    unused_item, token_count, piece_width = near_pieces.shape
     vmem = pl.BlockSpec(memory_space=pltpu.VMEM)
     return pl.pallas_call(
         lambda *refs: exchange_project_kernel(axis, count, gather_axis, *refs),
@@ -409,19 +416,23 @@
         in_specs=[vmem, vmem, pl.BlockSpec(memory_space=pl.ANY), vmem, vmem],
         out_specs=(vmem, vmem, vmem, vmem),
         scratch_shapes=[
-            pltpu.VMEM(chip_pieces.shape, chip_pieces.dtype),
+            pltpu.VMEM((token_count, piece_width), near_pieces.dtype),
+            pltpu.VMEM(near_pieces.shape, near_pieces.dtype),
+            pltpu.VMEM((token_count, piece_width), near_pieces.dtype),
             pltpu.VMEM((2, piece_width, w_query.shape[1]), w_query.dtype),
             pltpu.SemaphoreType.DMA((count,)),
             pltpu.SemaphoreType.DMA((count,)),
             pltpu.SemaphoreType.DMA(()),
             pltpu.SemaphoreType.DMA((2,)),
-            pltpu.SemaphoreType.DMA(()),
-            pltpu.SemaphoreType.DMA(()),
+            pltpu.SemaphoreType.DMA((2,)),
+            pltpu.SemaphoreType.DMA((2,)),
+            pltpu.SemaphoreType.DMA((2,)),
+            pltpu.SemaphoreType.DMA((2,)),
         ],
         compiler_params=pltpu.CompilerParams(
             collective_id=collective, has_side_effects=True, vmem_limit_bytes=60 * 1024 * 1024
         ),
-    )(values, chip_pieces, w_query, w_key, w_value)
+    )(values, near_pieces, w_query, w_key, w_value)
 
 
 def sum_kernel(axis, count, part_ref, total_ref, held, first_send, first_recv, second_send, second_recv):

time: 91 us -> 85.8 us (0.943)
  Pallas kernels: 65.8 us -> 60.6 us
    pallas_call x1, Pallas kernels: 30.5 us -> 24.9 us  [exchange_ring(): pl.pallas_call(lambda *refs: exchange_ring_kernel(axis, count, gather_axi...]
where the time goes in v8:
time: 85.8 us; the launch traced here: 85.2 us
  Pallas kernels  60.6 us (71%)
  matrix products  12.1 us (14%)
  other arithmetic  6.57 us (8%)
  local copies, waits for them, and re-layouts  5.54 us (6%)
    pallas_call x1, Pallas kernels, exchange_ring(): pl.pallas_call(lambda *refs: exchange_ring_kernel(axis, count, gather_axi...  24.9 us
    pallas_call x1, Pallas kernels, exchange_project(): pl.pallas_call(lambda *refs: exchange_project_kernel(axis, count, gather_...  22.3 us
    pallas_call x1, Pallas kernels, axis_sum(): pl.pallas_call(lambda *refs: sum_kernel(axis, count, *refs), out_shape=ja...  13.4 us
    dot_general x1, matrix products, attend(): jnp.einsum('rskgd,rtkd->rskgt', queries, key_new, preferred_element_type=...  2.58 us
    dot_general x1, matrix products, body(): jnp.dot(jnp.transpose(place_tokens), back.reshape(group_count * CAP * ste...  2.03 us
    unnamed x1, matrix products  1.96 us

profile of v8, /device:TPU:1, one launch (start us, length us, event | category | flops | bytes accessed | tf_op | source)
XLA Modules:
  0.0 85.2 jit_solution(4627098082043503162)
XLA Ops:
  0.0 0.9 %select_reduce_fusion.1 = s32[64]{0:T(128)S(1)} fusion(s32[128]{0:T(128)} %param.13, s32[64]{0:T(128)} %param.12), kind=kLoop, calls=%fused_computation.64 | loop fusion | flops 24512 | bytes 1024 | tf_op jit(solution)/shard_map/reduce_sum | solution.py:568
  1.0 0.2 convert_reduce_fusion
  1.2 0.1 add.100
  1.4 1.2 %reshape.288.refs_2_ = bf16[256,1024]{1,0:T(8,128)(2,1)S(1)} reshape(bf16[64,4,1024]{2,1,0:T(4,128)(2,1)} %param.11) | data formatting | bytes 1048576 | tf_op jit(solution)/shard_map/reshape | solution.py:582
  2.5 1.4 %convolution_convert_fusion = bf16[512,1024]{1,0:T(8,128)(2,1)} fusion(bf16[256,1024]{1,0:T(8,128)(2,1)S(1)} %reshape.288.refs_2_, s32[256]{0:T(256)S(1)} %add.100), kind=kOutput, calls=%fused_computation.1 | convolution fusion | flops 269090816 | bytes 1573888 | tf_op jit(solution)/shard_map/dot_general | solution.py:583
  4.0 0.1 fusion.8
  4.3 0.6 concatenate.21.refs_1_
  4.9 24.9 %shard_map.109 = (bf16[16,32,1024]{2,1,0:T(8,128)(2,1)}, bf16[16,16,128]{2,1,0:T(8,128)(2,1)}, bf16[3,256,1024]{2,1,0:T(8,128)(2,1)}) custom-call(bf16[16,32,1024]{2,1,0:T(8,128)(2,1)} %bitcast.92, bf16[16,16,128]{2,1,0:T(8,128)(2,1)} %concatenate.21.refs_1_, bf16[256,1024]{1,0:T(8,128)(2,1)} %copy-done.1), custom_call_target="tpu_custom_call" | custom-call | tf_op jit(solution)/shard_map/pallas_call | solution.py:249
  29.9 0.8 slice_convert_fusion
  30.6 0.2 copy.34
  30.9 0.1 eq.85
  31.0 2.0 %fusion.49 = f32[512,512]{0,1:S(1)} fusion(bf16[512,1024]{1,0:T(8,128)(2,1)} %bitcast.99, bf16[1024,512]{0,1:T(8,128)(2,1)S(1)} %bitcast.90), kind=kOutput, calls=%fused_computation.89 | convolution fusion | flops 536870912 | bytes 3145728
  33.0 0.1 select_reduce_fusion
  33.1 0.1 copy.28
  33.3 0.8 reshape_reshape.3.refs_0_
  34.0 13.4 %shard_map.110 = bf16[8,32,128]{2,1,0:T(8,128)(2,1)} custom-call(f32[8,32,128]{2,1,0:T(8,128)} %reshape_reshape.3.refs_0_), custom_call_target="tpu_custom_call" | custom-call | tf_op jit(solution)/shard_map/pallas_call | solution.py:504
  47.5 0.9 %broadcast_in_dim.82 = bf16[512,64]{1,0:T(8,128)(2,1)S(1)} reshape(bf16[8,32,128]{2,1,0:T(8,128)(2,1)} %shard_map.110) | data formatting | bytes 131072 | tf_op jit(solution)/shard_map/jit(_where)/broadcast_in_dim | solution.py:534
  48.4 0.1 copy.29
  48.5 1.7 %bitcast_convert_fusion = bf16[512,1024]{1,0:T(8,128)(2,1)} fusion(bf16[8,64,1024]{2,1,0:T(8,128)(2,1)S(1)} %copy-done.6, pred[512,8]{0,1:T(8,128)(4,1)S(1)} %iota_compare_fusion.8, bf16[512,64]{0,1:T(8,128)(2,1)S(1)} %copy.29), kind=kOutput, calls=%fused_computation | convolution fusion | flops 537657344 | bytes 2166784 | tf_op jit(solution)/shard_map/dot_general | solution.py:536
  50.2 22.3 %shard_map.111 = (bf16[16,32,1024]{2,1,0:T(8,128)(2,1)}, f32[256,1024]{1,0:T(8,128)}, f32[256,128]{1,0:T(8,128)}, f32[256,128]{1,0:T(8,128)}) custom-call(bf16[16,32,1024]{2,1,0:T(8,128)(2,1)} %bitcast.93, bf16[3,256,1024]{2,1,0:T(8,128)(2,1)} %get-tuple-element.14.refs_1_, bf16[8192,1024]{1,0:T(8,128)(2,1)} %refs_2_.1, bf16[8192,128]{1,0:T(8,128)(2,1)} %refs_3_.1, ...), custom_call_target="tpu_custom_call" | custom-call | tf_op jit(solution)/shard_map/pallas_call | solution.py:408
  72.5 2.0 %fusion.1 = f32[32,8,8,128]{3,1,2,0:T(8,128)S(1)} fusion(f32[256,1024]{1,0:T(8,128)} %get-tuple-element.15, bf16[512,1024]{1,0:T(8,128)(2,1)} %bitcast.95, s32[256]{0:T(256)S(1)} %add.100), kind=kOutput, calls=%fused_computation.5 | convolution fusion | flops 268828672 | bytes 3146752 | tf_op jit(solution)/shard_map/dot_general | solution.py:598
  74.6 0.2 copy.35
  74.9 1.1 %multiply_cosine_fusion.1 = (f32[64,4,64]{2,1,0:T(4,128)S(1)}, f32[64,4,64]{2,1,0:T(4,128)S(1)}) fusion(f32[64]{0:T(128)S(1)} %multiply_exponential_fusion, f32[64,4]{1,0:T(8,128)S(1)} %add_convert_fusion.1), kind=kLoop, calls=%fused_computation.43 | loop fusion | flops 16384 | bytes 132352 | tf_op jit(solution)/shard_map/cos | solution.py:25
  76.0 0.5 subtract_convert_fusion
  76.5 1.4 %fusion.34 = (bf16[64,4,64]{2,1,0:T(4,128)(2,1)S(1)}, bf16[64,4,64]{2,1,0:T(4,128)(2,1)S(1)}) fusion(f32[64,4,1,128]{3,1,0,2:T(4,128)S(1)} %bitcast.96, f32[64]{0:T(128)S(1)} %multiply_exponential_fusion, f32[64,4]{1,0:T(8,128)S(1)} %add_convert_fusion.1), kind=kLoop, calls=%fused_computation.57 | loop fusion | flops 147456 | bytes 197888 | tf_op jit(solution)/shard_map/concatenate | solution.py:29
  77.9 2.6 %fusion.48 = (f32[64,4,8]{2,1,0:T(4,128)S(1)}, f32[64,4,1,8,4]{3,4,1,0,2:T(4,128)S(1)}) fusion(bf16[64,4,8,64]{3,2,1,0:T(8,128)(2,1)S(1)} %get-tuple-element.22, bf16[64,4,8,64]{3,2,1,0:T(8,128)(2,1)S(1)} %get-tuple-element.21, bf16[64,4,64]{2,1,0:T(4,128)(2,1)S(1)} %get-tuple-element.24, bf16[64,4,64]{2,1,0:T(4,128)(2,1)S(1)} %get-tuple-element.23, ...), kind=kOutput, calls=%fused_computation.88 | convolution fusion | flops 3299328 | bytes 630800 | tf_op jit(solution)/shard_map/rskgd,rtkd->rskgt/dot_general | solution.py:41
  80.6 0.9 %fusion.47 = (f32[64,4,8]{2,1,0:T(4,128)S(1)}, f32[64,4,1,8,64]{4,3,1,0,2:T(8,128)S(1)}) fusion(bf16[64,64,128]{2,1,0:T(8,128)(2,1)S(1)} %copy-done.2, bf16[64,4,8,64]{3,2,1,0:T(8,128)(2,1)S(1)} %get-tuple-element.22, bf16[64,4,8,64]{3,2,1,0:T(8,128)(2,1)S(1)} %get-tuple-element.21, pred[64,64]{1,0:T(8,128)(4,1)S(1)} %iota_compare_fusion.7), kind=kOutput, calls=%fused_computation.87 | convolution fusion | flops 34994176 | bytes 2109440 | tf_op jit(solution)/shard_map/rskgd,rlkd->rskgl/dot_general | solution.py:37
  81.5 0.5 fusion.16
  82.0 0.8 fusion.11
  82.8 0.9 %convolution_bitcast_fusion = f32[64,128,4,8]{1,3,2,0:T(8,128)S(1)} fusion(bf16[64,64,128]{2,1,0:T(8,128)(2,1)S(1)} %copy-done.7, f32[64,4,1,8,64]{4,3,1,0,2:T(8,128)S(1)} %get-tuple-element.28, f32[64,4,8]{2,1,0:T(4,128)S(1)} %add.108, f32[64,4,8]{2,1,0:T(4,128)S(1)} %max.9), kind=kOutput, calls=%fused_computation.7 | convolution fusion | flops 33947648 | bytes 2637824 | tf_op jit(solution)/shard_map/rskgl,rlkd->rskgd/dot_general | solution.py:58
  83.8 0.5 fusion.5
  84.3 0.9 %reshape.297 = bf16[64,4,1024]{2,1,0:T(4,128)(2,1)} reshape(bf16[64,4,1,8,128]{4,3,1,0,2:T(8,128)(2,1)S(1)} %fusion.5) | data formatting | bytes 1048576 | tf_op jit(solution)/shard_map/reshape | solution.py:614
  (30 shorter events, 0.7 us)
Async XLA Ops:
  0.0 31.0 %copy-start = (bf16[8,1024,64]{1,2,0:T(8,128)(2,1)S(1)}, bf16[8,1024,64]{1,2,0:T(8,128)(2,1)}, u32[]{:S(2)}) copy-start(bf16[8,1024,64]{1,2,0:T(8,128)(2,1)} %param.18) | copy-start | bytes 3145732
  2.5 2.4 %copy-start.1 = (bf16[256,1024]{1,0:T(8,128)(2,1)}, bf16[256,1024]{1,0:T(8,128)(2,1)S(1)}, u32[]{:S(2)}) copy-start(bf16[256,1024]{1,0:T(8,128)(2,1)S(1)} %reshape.288.refs_2_) | copy-start | bytes 1572868
  33.0 15.5 %copy-start.6 = (bf16[8,64,1024]{2,1,0:T(8,128)(2,1)S(1)}, bf16[8,64,1024]{2,1,0:T(8,128)(2,1)}, u32[]{:S(2)}) copy-start(bf16[8,64,1024]{2,1,0:T(8,128)(2,1)} %param.19) | copy-start | bytes 3145732
  72.5 2.3 %copy-start.5 = (s32[64]{0:T(128)S(1)}, s32[64]{0:T(128)}, u32[]{:S(2)}) copy-start(s32[64]{0:T(128)} %param.14) | copy-start | bytes 772
  74.8 1.7 %copy-start.3 = (f32[256,128]{1,0:T(8,128)S(1)}, f32[256,128]{1,0:T(8,128)}, u32[]{:S(2)}) copy-start(f32[256,128]{1,0:T(8,128)} %get-tuple-element.17) | copy-start | bytes 393220
  76.0 4.6 %copy-start.2 = (bf16[64,64,128]{2,1,0:T(8,128)(2,1)S(1)}, bf16[64,64,128]{2,1,0:T(8,128)(2,1)}, u32[]{:S(2)}) copy-start(bf16[64,64,128]{2,1,0:T(8,128)(2,1)} %param.20) | copy-start | bytes 3145732
  81.4 1.3 %copy-start.7 = (bf16[64,64,128]{2,1,0:T(8,128)(2,1)S(1)}, bf16[64,64,128]{2,1,0:T(8,128)(2,1)}, u32[]{:S(2)}) copy-start(bf16[64,64,128]{2,1,0:T(8,128)(2,1)} %param.21) | copy-start | bytes 3145732
  82.8 1.0 %copy-start.4 = (f32[256,128]{1,0:T(8,128)S(1)}, f32[256,128]{1,0:T(8,128)}, u32[]{:S(2)}) copy-start(f32[256,128]{1,0:T(8,128)} %get-tuple-element.18) | copy-start | bytes 393220

commit v9 on v8

--- a/solution.py
+++ b/solution.py
@@ -265,15 +265,17 @@
     return outs[:arrays], outs[arrays]
 
 
-def exchange_project_kernel(
-    axis, count, gather_axis, send_ref, near_pieces, wq_hbm, wk_ref, wv_ref,
+def tail_kernel(
+    axis, count, gather_axis, part_ref, ids_ref, up_ref, near_pieces, wq_hbm, wk_ref, wv_ref,
     got_ref, q_ref, k_ref, v_ref,
-    far_piece, partner_near, partner_far, wq_buf, send_sem, recv_sem, local_sem, wq_sem,
+    held, total, send_buf, far_piece, partner_near, partner_far, wq_buf,
+    first_send, first_recv, second_send, second_recv, send_sem, recv_sem, local_sem, wq_sem,
     far_send, far_recv, partner_send, partner_recv,
 ):
     me = lax.axis_index(axis)
     mine = lax.axis_index(gather_axis)
-    chips = lax.axis_size(gather_axis) // 2
+    members = lax.axis_size(gather_axis)
+    chips = members // 2
     chip = mine // 2
     core = lax.rem(mine, 2)
     partner = chip * 2 + (1 - core)
@@ -285,10 +287,24 @@
     for offset in range(1, count):
         peer = offsets[offset - 1][0](me)
         pl.semaphore_signal(barrier, inc=1, device_id={axis: peer}, device_id_type=MESH)
-    for neighbour in (partner, right, left):
-        pl.semaphore_signal(barrier, inc=1, device_id={gather_axis: neighbour}, device_id_type=MESH)
-    pl.semaphore_wait(barrier, count + 2)
-
+    for offset in range(1, members):
+        peer = lax.rem(mine + offset, members)
+        pl.semaphore_signal(barrier, inc=1, device_id={gather_axis: peer}, device_id_type=MESH)
+    pl.semaphore_wait(barrier, count + members - 2)
+
+    first_out = []
+    for offset in range(1, members):
+        peer = lax.rem(mine + offset, members)
+        copy = pltpu.make_async_remote_copy(
+            src_ref=part_ref.at[peer],
+            dst_ref=held.at[mine],
+            send_sem=first_send.at[offset],
+            recv_sem=first_recv.at[offset],
+            device_id={gather_axis: peer},
+            device_id_type=MESH,
+        )
+        copy.start()
+        first_out.append(copy)
     far_out = []
     for side, slot, target, rows in ((0, 1, right, pl.ds(0, half)), (1, 2, left, pl.ds(half, half))):
         copy = pltpu.make_async_remote_copy(
@@ -310,21 +326,7 @@
         device_id_type=MESH,
     )
     to_partner.start()
-    local = pltpu.make_async_copy(send_ref.at[me], got_ref.at[me], local_sem)
-    local.start()
-    outgoing = []
-    for offset in range(1, count):
-        peer = offsets[offset - 1][0](me)
-        copy = pltpu.make_async_remote_copy(
-            src_ref=send_ref.at[peer],
-            dst_ref=got_ref.at[me],
-            send_sem=send_sem.at[offset],
-            recv_sem=recv_sem.at[offset],
-            device_id={axis: peer},
-            device_id_type=MESH,
-        )
-        copy.start()
-        outgoing.append(copy)
+    held[mine] = part_ref[mine]
 
     piece_width = near_pieces.shape[2]
     chip_shift = (0, chips - 1, 1, 2)
@@ -358,6 +360,37 @@
 
     for step in range(3):
         project(step, near_pieces[step])
+
+    for offset in range(1, members):
+        first_out[offset - 1].wait_send()
+        source = lax.rem(mine + members - offset, members)
+        incoming = pltpu.make_async_remote_copy(
+            src_ref=part_ref.at[source],
+            dst_ref=held.at[source],
+            send_sem=first_send.at[offset],
+            recv_sem=first_recv.at[offset],
+            device_id={gather_axis: source},
+            device_id_type=MESH,
+        )
+        incoming.wait_recv()
+    summed = held[0]
+    for index in range(1, members):
+        summed = summed + held[index]
+    total[mine] = summed.astype(total.dtype)
+    second_out = []
+    for offset in range(1, members):
+        peer = lax.rem(mine + offset, members)
+        copy = pltpu.make_async_remote_copy(
+            src_ref=total.at[mine],
+            dst_ref=total.at[mine],
+            send_sem=second_send.at[offset],
+            recv_sem=second_recv.at[offset],
+            device_id={gather_axis: peer},
+            device_id_type=MESH,
+        )
+        copy.start()
+        second_out.append(copy)
+
     for side, source, rows in ((0, left, pl.ds(0, half)), (1, right, pl.ds(half, half))):
         far_out[side].wait_send()
         incoming = pltpu.make_async_remote_copy(
@@ -378,6 +411,44 @@
         device_id_type=MESH,
     )
     far_to_partner.start()
+
+    for offset in range(1, members):
+        second_out[offset - 1].wait_send()
+        source = lax.rem(mine + members - offset, members)
+        incoming = pltpu.make_async_remote_copy(
+            src_ref=total.at[source],
+            dst_ref=total.at[source],
+            send_sem=second_send.at[offset],
+            recv_sem=second_recv.at[offset],
+            device_id={gather_axis: source},
+            device_id_type=MESH,
+        )
+        incoming.wait_recv()
+
+    middle = total[...].reshape(ids_ref.shape[0], total.shape[2])
+    slot_ids = ids_ref[...]
+    upward = jnp.zeros((ids_ref.shape[0], up_ref.shape[2]), jnp.float32)
+    for adapter in range(up_ref.shape[0]):
+        chosen = jnp.where(slot_ids == adapter, middle, jnp.zeros_like(middle))
+        upward = upward + jnp.dot(chosen, up_ref[adapter], preferred_element_type=jnp.float32)
+    send_buf[...] = upward.astype(send_buf.dtype).reshape(send_buf.shape)
+
+    local = pltpu.make_async_copy(send_buf.at[me], got_ref.at[me], local_sem)
+    local.start()
+    outgoing = []
+    for offset in range(1, count):
+        peer = offsets[offset - 1][0](me)
+        copy = pltpu.make_async_remote_copy(
+            src_ref=send_buf.at[peer],
+            dst_ref=got_ref.at[me],
+            send_sem=send_sem.at[offset],
+            recv_sem=recv_sem.at[offset],
+            device_id={axis: peer},
+            device_id_type=MESH,
+        )
+        copy.start()
+        outgoing.append(copy)
+
     project(3, far_piece[...])
     to_partner.wait_send()
     to_partner.wait_recv()
@@ -391,7 +462,7 @@
         outgoing[offset - 1].wait_send()
         source = offsets[offset - 1][1](me)
         incoming = pltpu.make_async_remote_copy(
-            src_ref=send_ref.at[source],
+            src_ref=send_buf.at[source],
             dst_ref=got_ref.at[source],
             send_sem=send_sem.at[offset],
             recv_sem=recv_sem.at[offset],
@@ -402,24 +473,36 @@
     local.wait()
 
 
-def exchange_project(values, near_pieces, w_query, w_key, w_value, axis, count, gather_axis, collective):
+def tail(partial, slot_ids, up_local, near_pieces, w_query, w_key, w_value, axis, count, gather_axis, collective):
+    members = lax.axis_size(gather_axis)
+    token_rows, adapter_rank = partial.shape
+    chunks = partial.reshape(members, token_rows // members, adapter_rank)
+    query_width = up_local.shape[2]
     unused_item, token_count, piece_width = near_pieces.shape
+    got_shape = (count, token_rows // count, query_width)
     vmem = pl.BlockSpec(memory_space=pltpu.VMEM)
     return pl.pallas_call(
-        lambda *refs: exchange_project_kernel(axis, count, gather_axis, *refs),
+        lambda *refs: tail_kernel(axis, count, gather_axis, *refs),
         out_shape=(
-            jax.ShapeDtypeStruct(values.shape, values.dtype),
+            jax.ShapeDtypeStruct(got_shape, jnp.bfloat16),
             jax.ShapeDtypeStruct((token_count, w_query.shape[1]), jnp.float32),
             jax.ShapeDtypeStruct((token_count, w_key.shape[1]), jnp.float32),
             jax.ShapeDtypeStruct((token_count, w_value.shape[1]), jnp.float32),
         ),
-        in_specs=[vmem, vmem, pl.BlockSpec(memory_space=pl.ANY), vmem, vmem],
+        in_specs=[vmem, vmem, vmem, vmem, pl.BlockSpec(memory_space=pl.ANY), vmem, vmem],
         out_specs=(vmem, vmem, vmem, vmem),
         scratch_shapes=[
+            pltpu.VMEM(chunks.shape, jnp.float32),
+            pltpu.VMEM(chunks.shape, jnp.bfloat16),
+            pltpu.VMEM(got_shape, jnp.bfloat16),
             pltpu.VMEM((token_count, piece_width), near_pieces.dtype),
             pltpu.VMEM(near_pieces.shape, near_pieces.dtype),
             pltpu.VMEM((token_count, piece_width), near_pieces.dtype),
             pltpu.VMEM((2, piece_width, w_query.shape[1]), w_query.dtype),
+            pltpu.SemaphoreType.DMA((members,)),
+            pltpu.SemaphoreType.DMA((members,)),
+            pltpu.SemaphoreType.DMA((members,)),
+            pltpu.SemaphoreType.DMA((members,)),
             pltpu.SemaphoreType.DMA((count,)),
             pltpu.SemaphoreType.DMA((count,)),
             pltpu.SemaphoreType.DMA(()),
@@ -432,113 +515,18 @@
         compiler_params=pltpu.CompilerParams(
             collective_id=collective, has_side_effects=True, vmem_limit_bytes=60 * 1024 * 1024
         ),
-    )(values, near_pieces, w_query, w_key, w_value)
-
-
-def sum_kernel(axis, count, part_ref, total_ref, held, first_send, first_recv, second_send, second_recv):
-    me = lax.axis_index(axis)
-    barrier = pltpu.get_barrier_semaphore()
-    for offset in range(1, count):
-        peer = lax.rem(me + offset, count)
-        pl.semaphore_signal(barrier, inc=1, device_id={axis: peer}, device_id_type=MESH)
-    pl.semaphore_wait(barrier, count - 1)
-    outgoing = []
-    for offset in range(1, count):
-        peer = lax.rem(me + offset, count)
-        copy = pltpu.make_async_remote_copy(
-            src_ref=part_ref.at[peer],
-            dst_ref=held.at[me],
-            send_sem=first_send.at[offset],
-            recv_sem=first_recv.at[offset],
-            device_id={axis: peer},
-            device_id_type=MESH,
-        )
-        copy.start()
-        outgoing.append(copy)
-    held[me] = part_ref[me]
-    for offset in range(1, count):
-        outgoing[offset - 1].wait_send()
-        source = lax.rem(me + count - offset, count)
-        incoming = pltpu.make_async_remote_copy(
-            src_ref=part_ref.at[source],
-            dst_ref=held.at[source],
-            send_sem=first_send.at[offset],
-            recv_sem=first_recv.at[offset],
-            device_id={axis: source},
-            device_id_type=MESH,
-        )
-        incoming.wait_recv()
-    total = held[0]
-    for index in range(1, count):
-        total = total + held[index]
-    total_ref[me] = total.astype(total_ref.dtype)
-    outgoing = []
-    for offset in range(1, count):
-        peer = lax.rem(me + offset, count)
-        copy = pltpu.make_async_remote_copy(
-            src_ref=total_ref.at[me],
-            dst_ref=total_ref.at[me],
-            send_sem=second_send.at[offset],
-            recv_sem=second_recv.at[offset],
-            device_id={axis: peer},
-            device_id_type=MESH,
-        )
-        copy.start()
-        outgoing.append(copy)
-    for offset in range(1, count):
-        outgoing[offset - 1].wait_send()
-        source = lax.rem(me + count - offset, count)
-        incoming = pltpu.make_async_remote_copy(
-            src_ref=total_ref.at[source],
-            dst_ref=total_ref.at[source],
-            send_sem=second_send.at[offset],
-            recv_sem=second_recv.at[offset],
-            device_id={axis: source},
-            device_id_type=MESH,
-        )
-        incoming.wait_recv()
-
-
-def axis_sum(values, axis, count, collective, out_dtype):
-    chunks = values.reshape(count, -1, 128)
-    summed = pl.pallas_call(
-        lambda *refs: sum_kernel(axis, count, *refs),
-        out_shape=jax.ShapeDtypeStruct(chunks.shape, out_dtype),
-        in_specs=[pl.BlockSpec(memory_space=pltpu.VMEM)],
-        out_specs=pl.BlockSpec(memory_space=pltpu.VMEM),
-        scratch_shapes=[
-            pltpu.VMEM(chunks.shape, values.dtype),
-            pltpu.SemaphoreType.DMA((count,)),
-            pltpu.SemaphoreType.DMA((count,)),
-            pltpu.SemaphoreType.DMA((count,)),
-            pltpu.SemaphoreType.DMA((count,)),
-        ],
-        compiler_params=pltpu.CompilerParams(collective_id=collective, has_side_effects=True),
-    )(chunks)
-    return summed.reshape(values.shape)
-
-
-def owner_adapter_term(received, slot_ids, down_local, up_local):
+    )(chunks, slot_ids, up_local, near_pieces, w_query, w_key, w_value)
+
+
+def down_partial(received, slot_ids, down_local):
     sources, rows, part_width = received.shape
     local_adapters, unused_item, adapter_rank = down_local.shape
-    query_width = up_local.shape[2]
     token_rows = received.reshape(sources * rows, part_width)
     every_down = jnp.einsum(
         "td,adr->tar", token_rows, down_local, preferred_element_type=jnp.float32
     )
     pick = slot_ids.reshape(sources * rows)[:, None] == jnp.arange(local_adapters, dtype=jnp.int32)[None, :]
-    partial_value_sum = jnp.sum(jnp.where(pick[:, :, None], every_down, 0.0), axis=1)
-    tp_count = lax.axis_size("tp")
-    summed = axis_sum(partial_value_sum.reshape(-1, 128), "tp", tp_count, 2, jnp.bfloat16)
-    adapter_middle = summed.reshape(sources * rows, adapter_rank)
-    spread_rows = jnp.where(pick[:, :, None], adapter_middle[:, None, :], jnp.zeros((), jnp.bfloat16))
-    spread_rows = spread_rows.reshape(sources * rows, local_adapters * adapter_rank)
-    adapter_output = jnp.dot(
-        spread_rows,
-        up_local.reshape(local_adapters * adapter_rank, query_width),
-        preferred_element_type=jnp.float32,
-    ).astype(jnp.bfloat16)
-    return adapter_output.reshape(sources, rows, query_width)
+    return jnp.sum(jnp.where(pick[:, :, None], every_down, 0.0), axis=1)
 
 
 def body(
@@ -591,9 +579,10 @@
         (send_tokens, send_ids), token_rows, "grp", group_count, "tp", 0
     )
     got_ids = jnp.repeat(got_ids[:, :CAP, 0].astype(jnp.int32), step_count, axis=1)
-    owner_out = owner_adapter_term(got_tokens, got_ids, pooled_down_weights, pool_up)
-    back, base_query_rows, key_base, value_base = exchange_project(
-        owner_out, chip_pieces, w_query, w_key, w_value, "grp", group_count, "tp", 1
+    partial = down_partial(got_tokens, got_ids, pooled_down_weights)
+    back, base_query_rows, key_base, value_base = tail(
+        partial, got_ids.reshape(-1, 1), pool_up, chip_pieces, w_query, w_key, w_value,
+        "grp", group_count, "tp", 1
     )
     adapter_output = jnp.dot(
         jnp.transpose(place_tokens),

time: 85.8 us -> 87.1 us (1.015)
  Pallas kernels: 60.6 us -> 64 us
  matrix products: 12.1 us -> 10.4 us
    pallas_call x2 -> x1, Pallas kernels: 35.7 us -> 39.1 us  [tail(): pl.pallas_call(lambda *refs: tail_kernel(axis, count, gather_axis, *refs)...]
    dot_general x1 -> x0, matrix products: 1.71 us -> none  [owner_adapter_term(): jnp.dot(spread_rows, up_local.reshape(local_adapters * adapter_rank, quer...]
    broadcast_in_dim x2 -> x0, local copies, waits for them, and re-layouts: 1.04 us -> none  [owner_adapter_term(): jnp.where(pick[:, :, None], adapter_middle[:, None, :], jnp.zeros((), jnp...]
where the time goes in v9:
time: 87.1 us; the launch traced here: 86.5 us
  Pallas kernels  64 us (73%)
  matrix products  10.4 us (12%)
  other arithmetic  6.56 us (8%)
  local copies, waits for them, and re-layouts  5.26 us (6%)
    pallas_call x1, Pallas kernels, tail(): pl.pallas_call(lambda *refs: tail_kernel(axis, count, gather_axis, *refs)...  39.1 us
    pallas_call x1, Pallas kernels, exchange_ring(): pl.pallas_call(lambda *refs: exchange_ring_kernel(axis, count, gather_axi...  24.9 us
    dot_general x1, matrix products, attend(): jnp.einsum('rskgd,rtkd->rskgt', queries, key_new, preferred_element_type=...  2.58 us
    dot_general x1, matrix products, body(): jnp.dot(jnp.transpose(place_tokens), back.reshape(group_count * CAP * ste...  2.03 us
    unnamed x1, matrix products  1.96 us

profile of v9, /device:TPU:1, one launch (start us, length us, event | category | flops | bytes accessed | tf_op | source)
XLA Modules:
  0.0 86.5 jit_solution(17091390077397568349)
XLA Ops:
  0.0 0.9 %select_reduce_fusion.1 = s32[64]{0:T(128)S(1)} fusion(s32[128]{0:T(128)} %param.13, s32[64]{0:T(128)} %param.12), kind=kLoop, calls=%fused_computation.59 | loop fusion | flops 24512 | bytes 1024 | tf_op jit(solution)/shard_map/reduce_sum | solution.py:556
  1.0 0.2 convert_reduce_fusion
  1.2 0.1 add.100
  1.4 1.2 %reshape.285.refs_2_ = bf16[256,1024]{1,0:T(8,128)(2,1)S(1)} reshape(bf16[64,4,1024]{2,1,0:T(4,128)(2,1)} %param.11) | data formatting | bytes 1048576 | tf_op jit(solution)/shard_map/reshape | solution.py:570
  2.5 1.4 %convolution_convert_fusion = bf16[512,1024]{1,0:T(8,128)(2,1)} fusion(bf16[256,1024]{1,0:T(8,128)(2,1)S(1)} %reshape.285.refs_2_, s32[256]{0:T(256)S(1)} %add.100), kind=kOutput, calls=%fused_computation | convolution fusion | flops 269090816 | bytes 1573888 | tf_op jit(solution)/shard_map/dot_general | solution.py:571
  4.0 0.1 fusion.8
  4.1 0.1 broadcast_in_dim.53
  4.2 0.1 broadcast_in_dim.54
  4.3 0.6 concatenate.21.refs_1_
  4.9 24.9 %shard_map.109 = (bf16[16,32,1024]{2,1,0:T(8,128)(2,1)}, bf16[16,16,128]{2,1,0:T(8,128)(2,1)}, bf16[3,256,1024]{2,1,0:T(8,128)(2,1)}) custom-call(bf16[16,32,1024]{2,1,0:T(8,128)(2,1)} %bitcast.89, bf16[16,16,128]{2,1,0:T(8,128)(2,1)} %concatenate.21.refs_1_, bf16[256,1024]{1,0:T(8,128)(2,1)} %copy-done.1), custom_call_target="tpu_custom_call" | custom-call | tf_op jit(solution)/shard_map/pallas_call | solution.py:249
  29.9 0.8 slice_convert_fusion
  30.6 0.2 copy.33
  30.8 0.1 broadcast_in_dim.55
  30.9 0.1 eq.85
  31.0 2.0 %fusion.44 = f32[512,512]{0,1:S(1)} fusion(bf16[512,1024]{1,0:T(8,128)(2,1)} %bitcast.96, bf16[1024,512]{0,1:T(8,128)(2,1)S(1)} %bitcast.87), kind=kOutput, calls=%fused_computation.83 | convolution fusion | flops 536870912 | bytes 3145728
  33.0 0.1 select_reduce_fusion
  33.1 0.8 copy.27
  34.0 0.8 broadcast_in_dim_reshape_reshape.4.refs_1_
  34.8 39.1 %shard_map.110 = (bf16[16,32,1024]{2,1,0:T(8,128)(2,1)}, f32[256,1024]{1,0:T(8,128)}, f32[256,128]{1,0:T(8,128)}, f32[256,128]{1,0:T(8,128)}) custom-call(f32[8,64,64]{2,1,0:T(8,128)} %bitcast.90, s32[512,1]{1,0:T(8,128)} %broadcast_in_dim_reshape_reshape.4.refs_1_, bf16[8,64,1024]{2,1,0:T(8,128)(2,1)} %refs_2_.1, ...), custom_call_target="tpu_custom_call" | custom-call | tf_op jit(solution)/shard_map/pallas_call | solution.py:484
  73.9 2.0 %fusion.1 = f32[32,8,8,128]{3,1,2,0:T(8,128)S(1)} fusion(f32[256,1024]{1,0:T(8,128)} %get-tuple-element.15, bf16[512,1024]{1,0:T(8,128)(2,1)} %bitcast.92, s32[256]{0:T(256)S(1)} %add.100), kind=kOutput, calls=%fused_computation.4 | convolution fusion | flops 268828672 | bytes 3146752 | tf_op jit(solution)/shard_map/dot_general | solution.py:587
  75.9 0.2 copy.34
  76.2 1.1 %multiply_cosine_fusion.1 = (f32[64,4,64]{2,1,0:T(4,128)S(1)}, f32[64,4,64]{2,1,0:T(4,128)S(1)}) fusion(f32[64]{0:T(128)S(1)} %multiply_exponential_fusion, f32[64,4]{1,0:T(8,128)S(1)} %add_convert_fusion.1), kind=kLoop, calls=%fused_computation.38 | loop fusion | flops 16384 | bytes 132352 | tf_op jit(solution)/shard_map/cos | solution.py:25
  77.4 0.5 subtract_convert_fusion
  77.9 1.4 %fusion.30 = (bf16[64,4,64]{2,1,0:T(4,128)(2,1)S(1)}, bf16[64,4,64]{2,1,0:T(4,128)(2,1)S(1)}) fusion(f32[64,4,1,128]{3,1,0,2:T(4,128)S(1)} %bitcast.93, f32[64]{0:T(128)S(1)} %multiply_exponential_fusion, f32[64,4]{1,0:T(8,128)S(1)} %add_convert_fusion.1), kind=kLoop, calls=%fused_computation.52 | loop fusion | flops 147456 | bytes 197888 | tf_op jit(solution)/shard_map/concatenate | solution.py:29
  79.3 2.6 %fusion.43 = (f32[64,4,8]{2,1,0:T(4,128)S(1)}, f32[64,4,1,8,4]{3,4,1,0,2:T(4,128)S(1)}) fusion(bf16[64,4,8,64]{3,2,1,0:T(8,128)(2,1)S(1)} %get-tuple-element.22, bf16[64,4,8,64]{3,2,1,0:T(8,128)(2,1)S(1)} %get-tuple-element.21, bf16[64,4,64]{2,1,0:T(4,128)(2,1)S(1)} %get-tuple-element.24, bf16[64,4,64]{2,1,0:T(4,128)(2,1)S(1)} %get-tuple-element.23, ...), kind=kOutput, calls=%fused_computation.82 | convolution fusion | flops 3299328 | bytes 630800 | tf_op jit(solution)/shard_map/rskgd,rtkd->rskgt/dot_general | solution.py:41
  81.8 0.1 iota_compare_fusion.7
  81.9 0.9 fusion.42
  82.8 0.5 fusion.14
  83.3 0.8 fusion.11
  84.1 0.9 %convolution_bitcast_fusion = f32[64,128,4,8]{1,3,2,0:T(8,128)S(1)} fusion(bf16[64,64,128]{2,1,0:T(8,128)(2,1)S(1)} %copy-done.6, f32[64,4,1,8,64]{4,3,1,0,2:T(8,128)S(1)} %get-tuple-element.28, f32[64,4,8]{2,1,0:T(4,128)S(1)} %add.108, f32[64,4,8]{2,1,0:T(4,128)S(1)} %max.9), kind=kOutput, calls=%fused_computation.6 | convolution fusion | flops 33947648 | bytes 2637824 | tf_op jit(solution)/shard_map/rskgl,rlkd->rskgd/dot_general | solution.py:58
  85.1 0.5 fusion.5
  85.6 0.9 %reshape.294 = bf16[64,4,1024]{2,1,0:T(4,128)(2,1)} reshape(bf16[64,4,1,8,128]{4,3,1,0,2:T(8,128)(2,1)S(1)} %fusion.5) | data formatting | bytes 1048576 | tf_op jit(solution)/shard_map/reshape | solution.py:603
  (24 shorter events, 0.3 us)
Async XLA Ops:
  0.0 31.0 %copy-start = (bf16[8,1024,64]{1,2,0:T(8,128)(2,1)S(1)}, bf16[8,1024,64]{1,2,0:T(8,128)(2,1)}, u32[]{:S(2)}) copy-start(bf16[8,1024,64]{1,2,0:T(8,128)(2,1)} %param.18) | copy-start | bytes 3145732
  2.5 2.4 %copy-start.1 = (bf16[256,1024]{1,0:T(8,128)(2,1)}, bf16[256,1024]{1,0:T(8,128)(2,1)S(1)}, u32[]{:S(2)}) copy-start(bf16[256,1024]{1,0:T(8,128)(2,1)S(1)} %reshape.285.refs_2_) | copy-start | bytes 1572868
  73.9 2.3 %copy-start.5 = (s32[64]{0:T(128)S(1)}, s32[64]{0:T(128)}, u32[]{:S(2)}) copy-start(s32[64]{0:T(128)} %param.14) | copy-start | bytes 772
  76.1 1.7 %copy-start.3 = (f32[256,128]{1,0:T(8,128)S(1)}, f32[256,128]{1,0:T(8,128)}, u32[]{:S(2)}) copy-start(f32[256,128]{1,0:T(8,128)} %get-tuple-element.17) | copy-start | bytes 393220
  77.3 4.6 %copy-start.2 = (bf16[64,64,128]{2,1,0:T(8,128)(2,1)S(1)}, bf16[64,64,128]{2,1,0:T(8,128)(2,1)}, u32[]{:S(2)}) copy-start(bf16[64,64,128]{2,1,0:T(8,128)(2,1)} %param.20) | copy-start | bytes 3145732
  82.8 1.3 %copy-start.6 = (bf16[64,64,128]{2,1,0:T(8,128)(2,1)S(1)}, bf16[64,64,128]{2,1,0:T(8,128)(2,1)}, u32[]{:S(2)}) copy-start(bf16[64,64,128]{2,1,0:T(8,128)(2,1)} %param.21) | copy-start | bytes 3145732
  84.1 0.9 %copy-start.4 = (f32[256,128]{1,0:T(8,128)S(1)}, f32[256,128]{1,0:T(8,128)}, u32[]{:S(2)}) copy-start(f32[256,128]{1,0:T(8,128)} %get-tuple-element.18) | copy-start | bytes 393220

commit v10 on v9

--- a/solution.py
+++ b/solution.py
@@ -358,9 +358,6 @@
         k_ref[...] += jnp.dot(piece, wk_ref[rows, :], preferred_element_type=jnp.float32)
         v_ref[...] += jnp.dot(piece, wv_ref[rows, :], preferred_element_type=jnp.float32)
 
-    for step in range(3):
-        project(step, near_pieces[step])
-
     for offset in range(1, members):
         first_out[offset - 1].wait_send()
         source = lax.rem(mine + members - offset, members)
@@ -449,6 +446,8 @@
         copy.start()
         outgoing.append(copy)
 
+    for step in range(3):
+        project(step, near_pieces[step])
     project(3, far_piece[...])
     to_partner.wait_send()
     to_partner.wait_recv()

time: 87.1 us -> 87.1 us (level)
  no operation moved by 1% of the time
where the time goes in v10:
time: 87.1 us; the launch traced here: 86.5 us
  Pallas kernels  64 us (73%)
  matrix products  10.4 us (12%)
  other arithmetic  6.56 us (8%)
  local copies, waits for them, and re-layouts  5.26 us (6%)
    pallas_call x1, Pallas kernels, tail(): pl.pallas_call(lambda *refs: tail_kernel(axis, count, gather_axis, *refs)...  39.1 us
    pallas_call x1, Pallas kernels, exchange_ring(): pl.pallas_call(lambda *refs: exchange_ring_kernel(axis, count, gather_axi...  24.9 us
    dot_general x1, matrix products, attend(): jnp.einsum('rskgd,rtkd->rskgt', queries, key_new, preferred_element_type=...  2.58 us
    dot_general x1, matrix products, body(): jnp.dot(jnp.transpose(place_tokens), back.reshape(group_count * CAP * ste...  2.03 us
    unnamed x1, matrix products  1.96 us

profile of v10, /device:TPU:1, one launch (start us, length us, event | category | flops | bytes accessed | tf_op | source)
XLA Modules:
  0.0 86.5 jit_solution(13565898104042494098)
XLA Ops:
  0.0 0.9 %select_reduce_fusion.1 = s32[64]{0:T(128)S(1)} fusion(s32[128]{0:T(128)} %param.13, s32[64]{0:T(128)} %param.12), kind=kLoop, calls=%fused_computation.59 | loop fusion | flops 24512 | bytes 1024 | tf_op jit(solution)/shard_map/reduce_sum | solution.py:555
  1.0 0.2 convert_reduce_fusion
  1.2 0.1 add.100
  1.4 1.2 %reshape.285.refs_2_ = bf16[256,1024]{1,0:T(8,128)(2,1)S(1)} reshape(bf16[64,4,1024]{2,1,0:T(4,128)(2,1)} %param.11) | data formatting | bytes 1048576 | tf_op jit(solution)/shard_map/reshape | solution.py:569
  2.5 1.4 %convolution_convert_fusion = bf16[512,1024]{1,0:T(8,128)(2,1)} fusion(bf16[256,1024]{1,0:T(8,128)(2,1)S(1)} %reshape.285.refs_2_, s32[256]{0:T(256)S(1)} %add.100), kind=kOutput, calls=%fused_computation | convolution fusion | flops 269090816 | bytes 1573888 | tf_op jit(solution)/shard_map/dot_general | solution.py:570
  4.0 0.1 fusion.8
  4.1 0.1 broadcast_in_dim.53
  4.2 0.1 broadcast_in_dim.54
  4.3 0.6 concatenate.21.refs_1_
  4.9 24.9 %shard_map.109 = (bf16[16,32,1024]{2,1,0:T(8,128)(2,1)}, bf16[16,16,128]{2,1,0:T(8,128)(2,1)}, bf16[3,256,1024]{2,1,0:T(8,128)(2,1)}) custom-call(bf16[16,32,1024]{2,1,0:T(8,128)(2,1)} %bitcast.89, bf16[16,16,128]{2,1,0:T(8,128)(2,1)} %concatenate.21.refs_1_, bf16[256,1024]{1,0:T(8,128)(2,1)} %copy-done.1), custom_call_target="tpu_custom_call" | custom-call | tf_op jit(solution)/shard_map/pallas_call | solution.py:249
  29.9 0.8 slice_convert_fusion
  30.6 0.2 copy.33
  30.8 0.1 broadcast_in_dim.55
  30.9 0.1 eq.85
  31.0 2.0 %fusion.44 = f32[512,512]{0,1:S(1)} fusion(bf16[512,1024]{1,0:T(8,128)(2,1)} %bitcast.96, bf16[1024,512]{0,1:T(8,128)(2,1)S(1)} %bitcast.87), kind=kOutput, calls=%fused_computation.83 | convolution fusion | flops 536870912 | bytes 3145728
  33.0 0.1 select_reduce_fusion
  33.1 0.8 copy.27
  34.0 0.8 broadcast_in_dim_reshape_reshape.4.refs_1_
  34.8 39.1 %shard_map.110 = (bf16[16,32,1024]{2,1,0:T(8,128)(2,1)}, f32[256,1024]{1,0:T(8,128)}, f32[256,128]{1,0:T(8,128)}, f32[256,128]{1,0:T(8,128)}) custom-call(f32[8,64,64]{2,1,0:T(8,128)} %bitcast.90, s32[512,1]{1,0:T(8,128)} %broadcast_in_dim_reshape_reshape.4.refs_1_, bf16[8,64,1024]{2,1,0:T(8,128)(2,1)} %refs_2_.1, ...), custom_call_target="tpu_custom_call" | custom-call | tf_op jit(solution)/shard_map/pallas_call | solution.py:483
  73.9 2.0 %fusion.1 = f32[32,8,8,128]{3,1,2,0:T(8,128)S(1)} fusion(f32[256,1024]{1,0:T(8,128)} %get-tuple-element.15, bf16[512,1024]{1,0:T(8,128)(2,1)} %bitcast.92, s32[256]{0:T(256)S(1)} %add.100), kind=kOutput, calls=%fused_computation.4 | convolution fusion | flops 268828672 | bytes 3146752 | tf_op jit(solution)/shard_map/dot_general | solution.py:586
  75.9 0.2 copy.34
  76.2 1.1 %multiply_cosine_fusion.1 = (f32[64,4,64]{2,1,0:T(4,128)S(1)}, f32[64,4,64]{2,1,0:T(4,128)S(1)}) fusion(f32[64]{0:T(128)S(1)} %multiply_exponential_fusion, f32[64,4]{1,0:T(8,128)S(1)} %add_convert_fusion.1), kind=kLoop, calls=%fused_computation.38 | loop fusion | flops 16384 | bytes 132352 | tf_op jit(solution)/shard_map/cos | solution.py:25
  77.4 0.5 subtract_convert_fusion
  77.9 1.4 %fusion.30 = (bf16[64,4,64]{2,1,0:T(4,128)(2,1)S(1)}, bf16[64,4,64]{2,1,0:T(4,128)(2,1)S(1)}) fusion(f32[64,4,1,128]{3,1,0,2:T(4,128)S(1)} %bitcast.93, f32[64]{0:T(128)S(1)} %multiply_exponential_fusion, f32[64,4]{1,0:T(8,128)S(1)} %add_convert_fusion.1), kind=kLoop, calls=%fused_computation.52 | loop fusion | flops 147456 | bytes 197888 | tf_op jit(solution)/shard_map/concatenate | solution.py:29
  79.3 2.6 %fusion.43 = (f32[64,4,8]{2,1,0:T(4,128)S(1)}, f32[64,4,1,8,4]{3,4,1,0,2:T(4,128)S(1)}) fusion(bf16[64,4,8,64]{3,2,1,0:T(8,128)(2,1)S(1)} %get-tuple-element.22, bf16[64,4,8,64]{3,2,1,0:T(8,128)(2,1)S(1)} %get-tuple-element.21, bf16[64,4,64]{2,1,0:T(4,128)(2,1)S(1)} %get-tuple-element.24, bf16[64,4,64]{2,1,0:T(4,128)(2,1)S(1)} %get-tuple-element.23, ...), kind=kOutput, calls=%fused_computation.82 | convolution fusion | flops 3299328 | bytes 630800 | tf_op jit(solution)/shard_map/rskgd,rtkd->rskgt/dot_general | solution.py:41
  81.8 0.1 iota_compare_fusion.7
  81.9 0.9 fusion.42
  82.8 0.5 fusion.14
  83.3 0.8 fusion.11
  84.1 0.9 %convolution_bitcast_fusion = f32[64,128,4,8]{1,3,2,0:T(8,128)S(1)} fusion(bf16[64,64,128]{2,1,0:T(8,128)(2,1)S(1)} %copy-done.6, f32[64,4,1,8,64]{4,3,1,0,2:T(8,128)S(1)} %get-tuple-element.28, f32[64,4,8]{2,1,0:T(4,128)S(1)} %add.108, f32[64,4,8]{2,1,0:T(4,128)S(1)} %max.9), kind=kOutput, calls=%fused_computation.6 | convolution fusion | flops 33947648 | bytes 2637824 | tf_op jit(solution)/shard_map/rskgl,rlkd->rskgd/dot_general | solution.py:58
  85.1 0.5 fusion.5
  85.6 0.9 %reshape.294 = bf16[64,4,1024]{2,1,0:T(4,128)(2,1)} reshape(bf16[64,4,1,8,128]{4,3,1,0,2:T(8,128)(2,1)S(1)} %fusion.5) | data formatting | bytes 1048576 | tf_op jit(solution)/shard_map/reshape | solution.py:602
  (24 shorter events, 0.3 us)
Async XLA Ops:
  0.0 31.0 %copy-start = (bf16[8,1024,64]{1,2,0:T(8,128)(2,1)S(1)}, bf16[8,1024,64]{1,2,0:T(8,128)(2,1)}, u32[]{:S(2)}) copy-start(bf16[8,1024,64]{1,2,0:T(8,128)(2,1)} %param.18) | copy-start | bytes 3145732
  2.5 2.4 %copy-start.1 = (bf16[256,1024]{1,0:T(8,128)(2,1)}, bf16[256,1024]{1,0:T(8,128)(2,1)S(1)}, u32[]{:S(2)}) copy-start(bf16[256,1024]{1,0:T(8,128)(2,1)S(1)} %reshape.285.refs_2_) | copy-start | bytes 1572868
  73.9 2.3 %copy-start.5 = (s32[64]{0:T(128)S(1)}, s32[64]{0:T(128)}, u32[]{:S(2)}) copy-start(s32[64]{0:T(128)} %param.14) | copy-start | bytes 772
  76.1 1.7 %copy-start.3 = (f32[256,128]{1,0:T(8,128)S(1)}, f32[256,128]{1,0:T(8,128)}, u32[]{:S(2)}) copy-start(f32[256,128]{1,0:T(8,128)} %get-tuple-element.17) | copy-start | bytes 393220
  77.3 4.6 %copy-start.2 = (bf16[64,64,128]{2,1,0:T(8,128)(2,1)S(1)}, bf16[64,64,128]{2,1,0:T(8,128)(2,1)}, u32[]{:S(2)}) copy-start(bf16[64,64,128]{2,1,0:T(8,128)(2,1)} %param.20) | copy-start | bytes 3145732
  82.8 1.3 %copy-start.6 = (bf16[64,64,128]{2,1,0:T(8,128)(2,1)S(1)}, bf16[64,64,128]{2,1,0:T(8,128)(2,1)}, u32[]{:S(2)}) copy-start(bf16[64,64,128]{2,1,0:T(8,128)(2,1)} %param.21) | copy-start | bytes 3145732
  84.1 0.9 %copy-start.4 = (f32[256,128]{1,0:T(8,128)S(1)}, f32[256,128]{1,0:T(8,128)}, u32[]{:S(2)}) copy-start(f32[256,128]{1,0:T(8,128)} %get-tuple-element.18) | copy-start | bytes 393220

commit v11 on v8

--- a/solution.py
+++ b/solution.py
@@ -267,6 +267,8 @@
 
 def exchange_project_kernel(
     axis, count, gather_axis, send_ref, near_pieces, wq_hbm, wk_ref, wv_ref,
+    place_ref, cos_ref, sin_ref,
+    queries_ref, key_ref, value_ref,
     got_ref, q_ref, k_ref, v_ref,
     far_piece, partner_near, partner_far, wq_buf, send_sem, recv_sem, local_sem, wq_sem,
     far_send, far_recv, partner_send, partner_recv,
@@ -401,21 +403,46 @@
         incoming.wait_recv()
     local.wait()
 
-
-def exchange_project(values, near_pieces, w_query, w_key, w_value, axis, count, gather_axis, collective):
+    slots, slot_rows, width = got_ref.shape
+    adapter_rows = jnp.dot(
+        place_ref[...], got_ref[...].reshape(slots * slot_rows, width),
+        preferred_element_type=jnp.float32,
+    )
+    cosine = cos_ref[...]
+    sines = sin_ref[...]
+    half_turn = HD // 2
+
+    def rotated(values):
+        return values * cosine + pltpu.roll(values, half_turn, 1) * sines
+
+    for head in range(width // HD):
+        lanes = slice(head * HD, (head + 1) * HD)
+        summed = q_ref[:, lanes] + adapter_rows[:, lanes]
+        queries_ref[:, lanes] = rotated(summed).astype(queries_ref.dtype)
+    for head in range(key_ref.shape[1] // HD):
+        lanes = slice(head * HD, (head + 1) * HD)
+        key_ref[:, lanes] = rotated(k_ref[:, lanes]).astype(key_ref.dtype)
+    value_ref[...] = v_ref[...].astype(value_ref.dtype)
+
+
+def exchange_project(values, near_pieces, w_query, w_key, w_value, place_t, cosine, sines,
+                     axis, count, gather_axis, collective):
     unused_item, token_count, piece_width = near_pieces.shape
     vmem = pl.BlockSpec(memory_space=pltpu.VMEM)
     return pl.pallas_call(
         lambda *refs: exchange_project_kernel(axis, count, gather_axis, *refs),
         out_shape=(
-            jax.ShapeDtypeStruct(values.shape, values.dtype),
-            jax.ShapeDtypeStruct((token_count, w_query.shape[1]), jnp.float32),
-            jax.ShapeDtypeStruct((token_count, w_key.shape[1]), jnp.float32),
-            jax.ShapeDtypeStruct((token_count, w_value.shape[1]), jnp.float32),
+            jax.ShapeDtypeStruct((token_count, w_query.shape[1]), jnp.bfloat16),
+            jax.ShapeDtypeStruct((token_count, w_key.shape[1]), jnp.bfloat16),
+            jax.ShapeDtypeStruct((token_count, w_value.shape[1]), jnp.bfloat16),
         ),
-        in_specs=[vmem, vmem, pl.BlockSpec(memory_space=pl.ANY), vmem, vmem],
-        out_specs=(vmem, vmem, vmem, vmem),
+        in_specs=[vmem, vmem, pl.BlockSpec(memory_space=pl.ANY), vmem, vmem, vmem, vmem, vmem],
+        out_specs=(vmem, vmem, vmem),
         scratch_shapes=[
+            pltpu.VMEM(values.shape, values.dtype),
+            pltpu.VMEM((token_count, w_query.shape[1]), jnp.float32),
+            pltpu.VMEM((token_count, w_key.shape[1]), jnp.float32),
+            pltpu.VMEM((token_count, w_value.shape[1]), jnp.float32),
             pltpu.VMEM((token_count, piece_width), near_pieces.dtype),
             pltpu.VMEM(near_pieces.shape, near_pieces.dtype),
             pltpu.VMEM((token_count, piece_width), near_pieces.dtype),
@@ -432,7 +459,7 @@
         compiler_params=pltpu.CompilerParams(
             collective_id=collective, has_side_effects=True, vmem_limit_bytes=60 * 1024 * 1024
         ),
-    )(values, near_pieces, w_query, w_key, w_value)
+    )(values, near_pieces, w_query, w_key, w_value, place_t, cosine, sines)
 
 
 def sum_kernel(axis, count, part_ref, total_ref, held, first_send, first_recv, second_send, second_recv):
@@ -592,22 +619,21 @@
     )
     got_ids = jnp.repeat(got_ids[:, :CAP, 0].astype(jnp.int32), step_count, axis=1)
     owner_out = owner_adapter_term(got_tokens, got_ids, pooled_down_weights, pool_up)
-    back, base_query_rows, key_base, value_base = exchange_project(
-        owner_out, chip_pieces, w_query, w_key, w_value, "grp", group_count, "tp", 1
-    )
-    adapter_output = jnp.dot(
-        jnp.transpose(place_tokens),
-        back.reshape(group_count * CAP * step_count, query_width),
-        preferred_element_type=jnp.float32,
-    )
-    base_query_rows = base_query_rows + adapter_output
     position = lengths[:, None] + jnp.arange(step_count, dtype=jnp.int32)[None, :]
-    queries = rotate(base_query_rows.reshape(row_count, step_count, q_local, HD), position)
-    queries = queries.astype(jnp.bfloat16).reshape(row_count, step_count, kv_local, group_size, HD)
-    key_new = rotate(key_base.reshape(row_count, step_count, kv_local, HD), position).astype(
-        jnp.bfloat16
-    )
-    value_new = value_base.reshape(row_count, step_count, kv_local, HD).astype(jnp.bfloat16)
+    half_width = HD // 2
+    inv_freq = jnp.exp(
+        jnp.arange(half_width, dtype=jnp.float32) * (-2.0 * math.log(rope_base) / HD)
+    )
+    angles = position.reshape(count_of_tokens).astype(jnp.float32)[:, None] * inv_freq
+    cosine = jnp.concatenate([jnp.cos(angles), jnp.cos(angles)], axis=1)
+    sines = jnp.concatenate([-jnp.sin(angles), jnp.sin(angles)], axis=1)
+    queries, key_new, value_new = exchange_project(
+        owner_out, chip_pieces, w_query, w_key, w_value, jnp.transpose(place_tokens), cosine, sines,
+        "grp", group_count, "tp", 1
+    )
+    queries = queries.reshape(row_count, step_count, kv_local, group_size, HD)
+    key_new = key_new.reshape(row_count, step_count, kv_local, HD)
+    value_new = value_new.reshape(row_count, step_count, kv_local, HD)
     cache_keys = cache_key.reshape(row_count, cache_key.shape[1], kv_local, HD)
     cache_values = cache_value.reshape(row_count, cache_value.shape[1], kv_local, HD)
     combined = attend(queries, key_new, value_new, cache_keys, cache_values, lengths)

time: 85.8 us -> 84.9 us (0.990)
  matrix products: 12.1 us -> 10.7 us
  local copies, waits for them, and re-layouts: 5.54 us -> 6.67 us
    dot_general x1 -> x0, matrix products: 2.03 us -> none  [body(): jnp.dot(jnp.transpose(place_tokens), back.reshape(group_count * CAP * ste...]
    cos x1 -> x0, other arithmetic: 1.1 us -> none  [rotate(): cosine = jnp.cos(angles)]
    unnamed x17 -> x15, local copies, waits for them, and re-layouts: 0.24 us -> 1.26 us
where the time goes in v11:
time: 84.9 us; the launch traced here: 84.2 us
  Pallas kernels  60.8 us (72%)
  matrix products  10.7 us (13%)
  local copies, waits for them, and re-layouts  6.67 us (8%)
  other arithmetic  5.79 us (7%)
    pallas_call x1, Pallas kernels, exchange_ring(): pl.pallas_call(lambda *refs: exchange_ring_kernel(axis, count, gather_axi...  24.9 us
    pallas_call x1, Pallas kernels, exchange_project(): pl.pallas_call(lambda *refs: exchange_project_kernel(axis, count, gather_...  22.4 us
    pallas_call x1, Pallas kernels, axis_sum(): pl.pallas_call(lambda *refs: sum_kernel(axis, count, *refs), out_shape=ja...  13.4 us
    dot_general x1, matrix products, attend(): jnp.einsum('rskgd,rtkd->rskgt', queries, key_new, preferred_element_type=...  3.3 us
    unnamed x1, matrix products  1.96 us
    dot_general x1, matrix products, owner_adapter_term(): jnp.dot(spread_rows, up_local.reshape(local_adapters * adapter_rank, quer...  1.71 us

profile of v11, /device:TPU:1, one launch (start us, length us, event | category | flops | bytes accessed | tf_op | source)
XLA Modules:
  0.0 84.2 jit_solution(14283046664243191088)
XLA Ops:
  0.0 0.9 %select_reduce_fusion.1 = s32[64]{0:T(128)S(1)} fusion(s32[128]{0:T(128)} %param.13, s32[64]{0:T(128)} %param.12), kind=kLoop, calls=%fused_computation.48 | loop fusion | flops 24512 | bytes 1024 | tf_op jit(solution)/shard_map/reduce_sum | solution.py:595
  1.0 0.2 convert_reduce_fusion
  1.2 0.1 add.93
  1.4 1.2 %reshape.241.refs_2_ = bf16[256,1024]{1,0:T(8,128)(2,1)S(1)} reshape(bf16[64,4,1024]{2,1,0:T(4,128)(2,1)} %param.11) | data formatting | bytes 1048576 | tf_op jit(solution)/shard_map/reshape | solution.py:609
  2.5 1.4 %convolution_convert_fusion = bf16[512,1024]{1,0:T(8,128)(2,1)} fusion(bf16[256,1024]{1,0:T(8,128)(2,1)S(1)} %reshape.241.refs_2_, s32[256]{0:T(256)S(1)} %add.93), kind=kOutput, calls=%fused_computation.1 | convolution fusion | flops 269090816 | bytes 1573888 | tf_op jit(solution)/shard_map/dot_general | solution.py:610
  4.0 0.1 fusion.7
  4.3 0.6 concatenate.9.refs_1_
  4.9 24.9 %shard_map.109 = (bf16[16,32,1024]{2,1,0:T(8,128)(2,1)}, bf16[16,16,128]{2,1,0:T(8,128)(2,1)}, bf16[3,256,1024]{2,1,0:T(8,128)(2,1)}) custom-call(bf16[16,32,1024]{2,1,0:T(8,128)(2,1)} %bitcast.84, bf16[16,16,128]{2,1,0:T(8,128)(2,1)} %concatenate.9.refs_1_, bf16[256,1024]{1,0:T(8,128)(2,1)} %copy-done.1), custom_call_target="tpu_custom_call" | custom-call | tf_op jit(solution)/shard_map/pallas_call | solution.py:249
  29.9 0.8 slice_convert_fusion
  30.6 0.2 copy.34
  30.9 0.1 eq.92
  31.0 2.0 %fusion.35 = f32[512,512]{0,1:S(1)} fusion(bf16[512,1024]{1,0:T(8,128)(2,1)} %bitcast.91, bf16[1024,512]{0,1:T(8,128)(2,1)S(1)} %bitcast.83), kind=kOutput, calls=%fused_computation.71 | convolution fusion | flops 536870912 | bytes 3145728
  33.0 0.1 select_reduce_fusion
  33.1 0.1 copy.28
  33.3 0.8 reshape_reshape.3.refs_0_
  34.0 13.4 %shard_map.110 = bf16[8,32,128]{2,1,0:T(8,128)(2,1)} custom-call(f32[8,32,128]{2,1,0:T(8,128)} %reshape_reshape.3.refs_0_), custom_call_target="tpu_custom_call" | custom-call | tf_op jit(solution)/shard_map/pallas_call | solution.py:531
  47.5 0.9 %broadcast_in_dim.117 = bf16[512,64]{1,0:T(8,128)(2,1)S(1)} reshape(bf16[8,32,128]{2,1,0:T(8,128)(2,1)} %shard_map.110) | data formatting | bytes 131072 | tf_op jit(solution)/shard_map/jit(_where)/broadcast_in_dim | solution.py:561
  48.4 0.1 copy.29
  48.5 1.7 %bitcast_convert_fusion = bf16[512,1024]{1,0:T(8,128)(2,1)} fusion(bf16[8,64,1024]{2,1,0:T(8,128)(2,1)S(1)} %copy-done.4, pred[512,8]{0,1:T(8,128)(4,1)S(1)} %iota_compare_fusion.8, bf16[512,64]{0,1:T(8,128)(2,1)S(1)} %copy.29), kind=kOutput, calls=%fused_computation | convolution fusion | flops 537657344 | bytes 2166784 | tf_op jit(solution)/shard_map/dot_general | solution.py:563
  50.3 0.1 convert_element_type.63
  50.5 0.5 fusion.22
  51.0 0.9 %pad_maximum_fusion = (f32[256,128]{1,0:T(8,128)}, f32[256,128]{1,0:T(8,128)}) fusion(f32[256,64]{1,0:T(8,128)S(1)} %get-tuple-element.21, f32[256,64]{1,0:T(8,128)S(1)} %get-tuple-element.20, f32[256,64]{1,0:T(8,128)S(1)} %get-tuple-element.19), kind=kLoop, calls=%fused_computation.38 | loop fusion | flops 65536 | bytes 458752 | tf_op jit(solution)/shard_map/concatenate | solution.py:628
  51.9 0.8 fusion.14.refs_5_
  52.7 22.4 %shard_map.111 = (bf16[256,1024]{1,0:T(8,128)(2,1)}, bf16[256,128]{1,0:T(8,128)(2,1)}, bf16[256,128]{1,0:T(8,128)(2,1)}) custom-call(bf16[16,32,1024]{2,1,0:T(8,128)(2,1)} %bitcast.87, bf16[3,256,1024]{2,1,0:T(8,128)(2,1)} %get-tuple-element.13.refs_1_, bf16[8192,1024]{1,0:T(8,128)(2,1)} %refs_2_.1, bf16[8192,128]{1,0:T(8,128)(2,1)} %refs_3_.1, ...), custom_call_target="tpu_custom_call" | custom-call | tf_op jit(solution)/shard_map/pallas_call | solution.py:432
  75.1 1.2 %copy.35 = bf16[32,8,8,128]{3,2,1,0:T(8,128)(2,1)S(1)} copy(bf16[32,8,8,128]{3,1,2,0:T(8,128)(2,1)} %bitcast.89) | data formatting | bytes 1048576
  76.3 3.3 %fusion.34 = (f32[64,4,8]{2,1,0:T(4,128)S(1)}, f32[64,4,1,8,4]{3,4,1,0,2:T(4,128)S(1)}) fusion(bf16[64,4,128,1]{2,1,3,0:T(4,128)(2,1)} %bitcast.93, bf16[64,4,8,128]{3,2,1,0:T(8,128)(2,1)S(1)} %bitcast.85, pred[4,4]{1,0:T(4,128)(4,1)S(1)} %iota_compare_fusion.9), kind=kOutput, calls=%fused_computation.70 | convolution fusion | flops 2119680 | bytes 630800 | tf_op jit(solution)/shard_map/rskgd,rtkd->rskgt/dot_general | solution.py:41
  79.7 0.8 fusion.33
  80.6 0.5 fusion.16
  81.1 0.8 fusion.10
  81.9 0.9 %convolution_bitcast_fusion = f32[64,128,4,8]{1,3,2,0:T(8,128)S(1)} fusion(bf16[64,64,128]{2,1,0:T(8,128)(2,1)S(1)} %copy-done.5, f32[64,4,1,8,64]{4,3,1,0,2:T(8,128)S(1)} %get-tuple-element.23, f32[64,4,8]{2,1,0:T(4,128)S(1)} %add.98, f32[64,4,8]{2,1,0:T(4,128)S(1)} %max.9), kind=kOutput, calls=%fused_computation.5 | convolution fusion | flops 33947648 | bytes 2637824 | tf_op jit(solution)/shard_map/rskgl,rlkd->rskgd/dot_general | solution.py:58
  82.8 0.5 fusion.4
  83.3 0.9 %reshape.250 = bf16[64,4,1024]{2,1,0:T(4,128)(2,1)} reshape(bf16[64,4,1,8,128]{4,3,1,0,2:T(8,128)(2,1)S(1)} %fusion.4) | data formatting | bytes 1048576 | tf_op jit(solution)/shard_map/reshape | solution.py:640
  (27 shorter events, 0.7 us)
Async XLA Ops:
  0.0 31.0 %copy-start = (bf16[8,1024,64]{1,2,0:T(8,128)(2,1)S(1)}, bf16[8,1024,64]{1,2,0:T(8,128)(2,1)}, u32[]{:S(2)}) copy-start(bf16[8,1024,64]{1,2,0:T(8,128)(2,1)} %param.18) | copy-start | bytes 3145732
  2.5 2.4 %copy-start.1 = (bf16[256,1024]{1,0:T(8,128)(2,1)}, bf16[256,1024]{1,0:T(8,128)(2,1)S(1)}, u32[]{:S(2)}) copy-start(bf16[256,1024]{1,0:T(8,128)(2,1)S(1)} %reshape.241.refs_2_) | copy-start | bytes 1572868
  33.0 15.5 %copy-start.4 = (bf16[8,64,1024]{2,1,0:T(8,128)(2,1)S(1)}, bf16[8,64,1024]{2,1,0:T(8,128)(2,1)}, u32[]{:S(2)}) copy-start(bf16[8,64,1024]{2,1,0:T(8,128)(2,1)} %param.19) | copy-start | bytes 3145732
  48.5 1.7 %copy-start.3 = (s32[64]{0:T(128)S(1)}, s32[64]{0:T(128)}, u32[]{:S(2)}) copy-start(s32[64]{0:T(128)} %param.14) | copy-start | bytes 772
  75.1 4.6 %copy-start.2 = (bf16[64,64,128]{2,1,0:T(8,128)(2,1)S(1)}, bf16[64,64,128]{2,1,0:T(8,128)(2,1)}, u32[]{:S(2)}) copy-start(bf16[64,64,128]{2,1,0:T(8,128)(2,1)} %param.20) | copy-start | bytes 3145732
  80.5 1.3 %copy-start.5 = (bf16[64,64,128]{2,1,0:T(8,128)(2,1)S(1)}, bf16[64,64,128]{2,1,0:T(8,128)(2,1)}, u32[]{:S(2)}) copy-start(bf16[64,64,128]{2,1,0:T(8,128)(2,1)} %param.21) | copy-start | bytes 3145732
  81.9 0.9 %copy-start.6 = (bf16[256,128]{1,0:T(8,128)(2,1)S(1)}, bf16[256,128]{1,0:T(8,128)(2,1)}, u32[]{:S(2)}) copy-start(bf16[256,128]{1,0:T(8,128)(2,1)} %get-tuple-element.16) | copy-start | bytes 196612

commit v12 on v11

--- a/solution.py
+++ b/solution.py
@@ -624,11 +624,14 @@
     inv_freq = jnp.exp(
         jnp.arange(half_width, dtype=jnp.float32) * (-2.0 * math.log(rope_base) / HD)
     )
-    angles = position.reshape(count_of_tokens).astype(jnp.float32)[:, None] * inv_freq
-    cosine = jnp.concatenate([jnp.cos(angles), jnp.cos(angles)], axis=1)
-    sines = jnp.concatenate([-jnp.sin(angles), jnp.sin(angles)], axis=1)
+    both_halves = jnp.concatenate([inv_freq, inv_freq])
+    turn_sign = jnp.where(jnp.arange(HD, dtype=jnp.int32) < half_width, -1.0, 1.0).astype(jnp.float32)
+    angles = position.reshape(count_of_tokens).astype(jnp.float32)[:, None] * both_halves[None, :]
+    cosine = jnp.cos(angles)
+    sines = jnp.sin(angles) * turn_sign[None, :]
+    place_back = (token_slot[:, None] == token_span[None, :]).astype(jnp.bfloat16)
     queries, key_new, value_new = exchange_project(
-        owner_out, chip_pieces, w_query, w_key, w_value, jnp.transpose(place_tokens), cosine, sines,
+        owner_out, chip_pieces, w_query, w_key, w_value, place_back, cosine, sines,
         "grp", group_count, "tp", 1
     )
     queries = queries.reshape(row_count, step_count, kv_local, group_size, HD)

time: 84.9 us -> 84.8 us (level)
    mul x0 -> x1, other arithmetic: none -> 1.27 us  [body(): sines = jnp.sin(angles) * turn_sign[None, :]]
    concatenate x1 -> x0, other arithmetic: 0.86 us -> none  [body(): cosine = jnp.concatenate([jnp.cos(angles), jnp.cos(angles)], axis=1)]
where the time goes in v12:
time: 84.8 us; the launch traced here: 84.2 us
  Pallas kernels  60.8 us (72%)
  matrix products  10.7 us (13%)
  local copies, waits for them, and re-layouts  6.67 us (8%)
  other arithmetic  5.74 us (7%)
    pallas_call x1, Pallas kernels, exchange_ring(): pl.pallas_call(lambda *refs: exchange_ring_kernel(axis, count, gather_axi...  24.9 us
    pallas_call x1, Pallas kernels, exchange_project(): pl.pallas_call(lambda *refs: exchange_project_kernel(axis, count, gather_...  22.4 us
    pallas_call x1, Pallas kernels, axis_sum(): pl.pallas_call(lambda *refs: sum_kernel(axis, count, *refs), out_shape=ja...  13.4 us
    dot_general x1, matrix products, attend(): jnp.einsum('rskgd,rtkd->rskgt', queries, key_new, preferred_element_type=...  3.3 us
    unnamed x1, matrix products  1.96 us
    dot_general x1, matrix products, owner_adapter_term(): jnp.dot(spread_rows, up_local.reshape(local_adapters * adapter_rank, quer...  1.71 us

profile of v12, /device:TPU:1, one launch (start us, length us, event | category | flops | bytes accessed | tf_op | source)
XLA Modules:
  0.0 84.2 jit_solution(4064066503175953392)
XLA Ops:
  0.0 0.9 %select_reduce_fusion.1 = s32[64]{0:T(128)S(1)} fusion(s32[128]{0:T(128)} %param.13, s32[64]{0:T(128)} %param.12), kind=kLoop, calls=%fused_computation.46 | loop fusion | flops 24512 | bytes 1024 | tf_op jit(solution)/shard_map/reduce_sum | solution.py:595
  1.0 0.2 convert_reduce_fusion
  1.2 0.1 add.97
  1.4 1.2 %reshape.255.refs_2_ = bf16[256,1024]{1,0:T(8,128)(2,1)S(1)} reshape(bf16[64,4,1024]{2,1,0:T(4,128)(2,1)} %param.11) | data formatting | bytes 1048576 | tf_op jit(solution)/shard_map/reshape | solution.py:609
  2.5 1.4 %convolution_convert_fusion = bf16[512,1024]{1,0:T(8,128)(2,1)} fusion(bf16[256,1024]{1,0:T(8,128)(2,1)S(1)} %reshape.255.refs_2_, s32[256]{0:T(256)S(1)} %add.97), kind=kOutput, calls=%fused_computation.1 | convolution fusion | flops 269090816 | bytes 1573888 | tf_op jit(solution)/shard_map/dot_general | solution.py:610
  4.0 0.1 fusion.7
  4.1 0.1 broadcast_in_dim.85
  4.3 0.6 concatenate.6.refs_1_
  4.9 24.9 %shard_map.109 = (bf16[16,32,1024]{2,1,0:T(8,128)(2,1)}, bf16[16,16,128]{2,1,0:T(8,128)(2,1)}, bf16[3,256,1024]{2,1,0:T(8,128)(2,1)}) custom-call(bf16[16,32,1024]{2,1,0:T(8,128)(2,1)} %bitcast.84, bf16[16,16,128]{2,1,0:T(8,128)(2,1)} %concatenate.6.refs_1_, bf16[256,1024]{1,0:T(8,128)(2,1)} %copy-done.1), custom_call_target="tpu_custom_call" | custom-call | tf_op jit(solution)/shard_map/pallas_call | solution.py:249
  29.9 0.8 slice_convert_fusion
  30.6 0.2 copy.34
  30.9 0.1 eq.98
  31.0 2.0 %fusion.35 = f32[512,512]{0,1:S(1)} fusion(bf16[512,1024]{1,0:T(8,128)(2,1)} %bitcast.91, bf16[1024,512]{0,1:T(8,128)(2,1)S(1)} %bitcast.83), kind=kOutput, calls=%fused_computation.71 | convolution fusion | flops 536870912 | bytes 3145728
  33.0 0.1 select_reduce_fusion
  33.1 0.1 copy.28
  33.3 0.8 reshape_reshape.3.refs_0_
  34.0 13.4 %shard_map.110 = bf16[8,32,128]{2,1,0:T(8,128)(2,1)} custom-call(f32[8,32,128]{2,1,0:T(8,128)} %reshape_reshape.3.refs_0_), custom_call_target="tpu_custom_call" | custom-call | tf_op jit(solution)/shard_map/pallas_call | solution.py:531
  47.5 0.9 %broadcast_in_dim.127 = bf16[512,64]{1,0:T(8,128)(2,1)S(1)} reshape(bf16[8,32,128]{2,1,0:T(8,128)(2,1)} %shard_map.110) | data formatting | bytes 131072 | tf_op jit(solution)/shard_map/jit(_where)/broadcast_in_dim | solution.py:561
  48.4 0.1 copy.29
  48.5 1.7 %bitcast_convert_fusion = bf16[512,1024]{1,0:T(8,128)(2,1)} fusion(bf16[8,64,1024]{2,1,0:T(8,128)(2,1)S(1)} %copy-done.4, pred[512,8]{0,1:T(8,128)(4,1)S(1)} %iota_compare_fusion.8, bf16[512,64]{0,1:T(8,128)(2,1)S(1)} %copy.29), kind=kOutput, calls=%fused_computation | convolution fusion | flops 537657344 | bytes 2166784 | tf_op jit(solution)/shard_map/dot_general | solution.py:563
  50.3 0.8 fusion.14.refs_5_
  51.2 0.1 convert_element_type.63
  51.3 1.3 %fusion.22 = (f32[256,128]{1,0:T(8,128)}, f32[256,128]{1,0:T(8,128)}) fusion(f32[128]{0:T(128)S(1)} %get-tuple-element.25, f32[128]{0:T(128)S(1)} %get-tuple-element.26, f32[256]{0:T(256)S(1)} %convert_element_type.63), kind=kLoop, calls=%fused_computation.38 | loop fusion | flops 65536 | bytes 264192 | tf_op jit(solution)/shard_map/mul | solution.py:631
  52.6 22.4 %shard_map.111 = (bf16[256,1024]{1,0:T(8,128)(2,1)}, bf16[256,128]{1,0:T(8,128)(2,1)}, bf16[256,128]{1,0:T(8,128)(2,1)}) custom-call(bf16[16,32,1024]{2,1,0:T(8,128)(2,1)} %bitcast.87, bf16[3,256,1024]{2,1,0:T(8,128)(2,1)} %get-tuple-element.13.refs_1_, bf16[8192,1024]{1,0:T(8,128)(2,1)} %refs_2_.1, bf16[8192,128]{1,0:T(8,128)(2,1)} %refs_3_.1, ...), custom_call_target="tpu_custom_call" | custom-call | tf_op jit(solution)/shard_map/pallas_call | solution.py:432
  75.0 1.2 %copy.35 = bf16[32,8,8,128]{3,2,1,0:T(8,128)(2,1)S(1)} copy(bf16[32,8,8,128]{3,1,2,0:T(8,128)(2,1)} %bitcast.89) | data formatting | bytes 1048576
  76.3 3.3 %fusion.34 = (f32[64,4,8]{2,1,0:T(4,128)S(1)}, f32[64,4,1,8,4]{3,4,1,0,2:T(4,128)S(1)}) fusion(bf16[64,4,128,1]{2,1,3,0:T(4,128)(2,1)} %bitcast.93, bf16[64,4,8,128]{3,2,1,0:T(8,128)(2,1)S(1)} %bitcast.85, pred[4,4]{1,0:T(4,128)(4,1)S(1)} %iota_compare_fusion.9), kind=kOutput, calls=%fused_computation.70 | convolution fusion | flops 2119680 | bytes 630800 | tf_op jit(solution)/shard_map/rskgd,rtkd->rskgt/dot_general | solution.py:41
  79.7 0.8 fusion.33
  80.5 0.5 fusion.16
  81.0 0.8 fusion.10
  81.8 0.9 %convolution_bitcast_fusion = f32[64,128,4,8]{1,3,2,0:T(8,128)S(1)} fusion(bf16[64,64,128]{2,1,0:T(8,128)(2,1)S(1)} %copy-done.5, f32[64,4,1,8,64]{4,3,1,0,2:T(8,128)S(1)} %get-tuple-element.22, f32[64,4,8]{2,1,0:T(4,128)S(1)} %add.102, f32[64,4,8]{2,1,0:T(4,128)S(1)} %max.9), kind=kOutput, calls=%fused_computation.5 | convolution fusion | flops 33947648 | bytes 2637824 | tf_op jit(solution)/shard_map/rskgl,rlkd->rskgd/dot_general | solution.py:58
  82.8 0.5 fusion.4
  83.3 0.9 %reshape.264 = bf16[64,4,1024]{2,1,0:T(4,128)(2,1)} reshape(bf16[64,4,1,8,128]{4,3,1,0,2:T(8,128)(2,1)S(1)} %fusion.4) | data formatting | bytes 1048576 | tf_op jit(solution)/shard_map/reshape | solution.py:643
  (27 shorter events, 0.6 us)
Async XLA Ops:
  0.0 31.0 %copy-start = (bf16[8,1024,64]{1,2,0:T(8,128)(2,1)S(1)}, bf16[8,1024,64]{1,2,0:T(8,128)(2,1)}, u32[]{:S(2)}) copy-start(bf16[8,1024,64]{1,2,0:T(8,128)(2,1)} %param.18) | copy-start | bytes 3145732
  2.5 2.4 %copy-start.1 = (bf16[256,1024]{1,0:T(8,128)(2,1)}, bf16[256,1024]{1,0:T(8,128)(2,1)S(1)}, u32[]{:S(2)}) copy-start(bf16[256,1024]{1,0:T(8,128)(2,1)S(1)} %reshape.255.refs_2_) | copy-start | bytes 1572868
  33.0 15.5 %copy-start.4 = (bf16[8,64,1024]{2,1,0:T(8,128)(2,1)S(1)}, bf16[8,64,1024]{2,1,0:T(8,128)(2,1)}, u32[]{:S(2)}) copy-start(bf16[8,64,1024]{2,1,0:T(8,128)(2,1)} %param.19) | copy-start | bytes 3145732
  48.5 2.6 %copy-start.3 = (s32[64]{0:T(128)S(1)}, s32[64]{0:T(128)}, u32[]{:S(2)}) copy-start(s32[64]{0:T(128)} %param.14) | copy-start | bytes 772
  75.0 4.6 %copy-start.2 = (bf16[64,64,128]{2,1,0:T(8,128)(2,1)S(1)}, bf16[64,64,128]{2,1,0:T(8,128)(2,1)}, u32[]{:S(2)}) copy-start(bf16[64,64,128]{2,1,0:T(8,128)(2,1)} %param.20) | copy-start | bytes 3145732
  80.5 1.3 %copy-start.5 = (bf16[64,64,128]{2,1,0:T(8,128)(2,1)S(1)}, bf16[64,64,128]{2,1,0:T(8,128)(2,1)}, u32[]{:S(2)}) copy-start(bf16[64,64,128]{2,1,0:T(8,128)(2,1)} %param.21) | copy-start | bytes 3145732
  81.8 0.9 %copy-start.6 = (bf16[256,128]{1,0:T(8,128)(2,1)S(1)}, bf16[256,128]{1,0:T(8,128)(2,1)}, u32[]{:S(2)}) copy-start(bf16[256,128]{1,0:T(8,128)(2,1)} %get-tuple-element.16) | copy-start | bytes 196612

commit v13 on v12

--- a/solution.py
+++ b/solution.py
@@ -154,9 +154,13 @@
 def exchange_ring_kernel(axis, count, gather_axis, arrays, *refs):
     send_refs = refs[:arrays]
     piece_ref = refs[arrays]
-    got_refs = refs[arrays + 1 : 2 * arrays + 1]
-    chip_pieces = refs[2 * arrays + 1]
-    send_sem, recv_sem, local_sem, near_send, near_recv, piece_sem = refs[2 * arrays + 2 :]
+    down_ref = refs[arrays + 1]
+    total = refs[arrays + 2]
+    chip_pieces = refs[arrays + 3]
+    got_refs = (refs[arrays + 5], refs[arrays + 4])
+    (part, held, send_sem, recv_sem, local_sem, near_send, near_recv, piece_sem,
+     first_send, first_recv, second_send, second_recv) = refs[arrays + 6 :]
+    members = lax.axis_size(gather_axis)
     chips = lax.axis_size(gather_axis) // 2
     me = lax.axis_index(axis)
     mine = lax.axis_index(gather_axis)
@@ -172,9 +176,10 @@
     for offset in range(1, count):
         peer = offsets[offset - 1][0](me)
         pl.semaphore_signal(barrier, inc=1, device_id={axis: peer}, device_id_type=MESH)
-    pl.semaphore_signal(barrier, inc=1, device_id={gather_axis: right}, device_id_type=MESH)
-    pl.semaphore_signal(barrier, inc=1, device_id={gather_axis: left}, device_id_type=MESH)
-    pl.semaphore_wait(barrier, count + 1)
+    for offset in range(1, members):
+        peer = lax.rem(mine + offset, members)
+        pl.semaphore_signal(barrier, inc=1, device_id={gather_axis: peer}, device_id_type=MESH)
+    pl.semaphore_wait(barrier, count + members - 2)
 
     near = []
     for side, target in ((0, right), (1, left)):
@@ -240,29 +245,107 @@
             incoming.wait_recv()
     for local in locals_:
         local.wait()
+
+    sources, slot_rows, part_width = got_refs[0].shape
+    token_count = sources * slot_rows
+    tokens_here = got_refs[0][...].reshape(token_count, part_width)
+    adapter_of = got_refs[1][...].reshape(token_count, got_refs[1].shape[2])[:, 0:1].astype(jnp.int32)
+    partial = jnp.zeros((token_count, down_ref.shape[2]), jnp.float32)
+    for adapter in range(down_ref.shape[0]):
+        product = jnp.dot(tokens_here, down_ref[adapter], preferred_element_type=jnp.float32)
+        partial = partial + jnp.where(adapter_of == adapter, product, jnp.zeros_like(product))
+    part[...] = partial.reshape(part.shape)
+
+    first_out = []
+    for offset in range(1, members):
+        peer = lax.rem(mine + offset, members)
+        copy = pltpu.make_async_remote_copy(
+            src_ref=part.at[peer],
+            dst_ref=held.at[mine],
+            send_sem=first_send.at[offset],
+            recv_sem=first_recv.at[offset],
+            device_id={gather_axis: peer},
+            device_id_type=MESH,
+        )
+        copy.start()
+        first_out.append(copy)
+    held[mine] = part[mine]
+    for offset in range(1, members):
+        first_out[offset - 1].wait_send()
+        source = lax.rem(mine + members - offset, members)
+        incoming = pltpu.make_async_remote_copy(
+            src_ref=part.at[source],
+            dst_ref=held.at[source],
+            send_sem=first_send.at[offset],
+            recv_sem=first_recv.at[offset],
+            device_id={gather_axis: source},
+            device_id_type=MESH,
+        )
+        incoming.wait_recv()
+    summed = held[0]
+    for index in range(1, members):
+        summed = summed + held[index]
+    total[mine] = summed.astype(total.dtype)
+    second_out = []
+    for offset in range(1, members):
+        peer = lax.rem(mine + offset, members)
+        copy = pltpu.make_async_remote_copy(
+            src_ref=total.at[mine],
+            dst_ref=total.at[mine],
+            send_sem=second_send.at[offset],
+            recv_sem=second_recv.at[offset],
+            device_id={gather_axis: peer},
+            device_id_type=MESH,
+        )
+        copy.start()
+        second_out.append(copy)
+    for offset in range(1, members):
+        second_out[offset - 1].wait_send()
+        source = lax.rem(mine + members - offset, members)
+        incoming = pltpu.make_async_remote_copy(
+            src_ref=total.at[source],
+            dst_ref=total.at[source],
+            send_sem=second_send.at[offset],
+            recv_sem=second_recv.at[offset],
+            device_id={gather_axis: source},
+            device_id_type=MESH,
+        )
+        incoming.wait_recv()
     own_piece.wait()
 
 
-def exchange_ring(values, piece, axis, count, gather_axis, collective):
+def exchange_ring(values, piece, down_local, axis, count, gather_axis, collective):
     arrays = len(values)
+    members = lax.axis_size(gather_axis)
+    sources, slot_rows, unused_item = values[0].shape
+    adapter_rank = down_local.shape[2]
+    chunk_shape = (members, sources * slot_rows // members, adapter_rank)
     vmem = pl.BlockSpec(memory_space=pltpu.VMEM)
     outs = pl.pallas_call(
         lambda *refs: exchange_ring_kernel(axis, count, gather_axis, arrays, *refs),
-        out_shape=tuple(jax.ShapeDtypeStruct(v.shape, v.dtype) for v in values)
-        + (jax.ShapeDtypeStruct((3,) + piece.shape, piece.dtype),),
-        in_specs=[vmem] * (arrays + 1),
-        out_specs=tuple([vmem] * (arrays + 1)),
-        scratch_shapes=[
+        out_shape=(jax.ShapeDtypeStruct(chunk_shape, jnp.bfloat16),
+                   jax.ShapeDtypeStruct((3,) + piece.shape, piece.dtype),
+                   jax.ShapeDtypeStruct(values[1].shape, values[1].dtype)),
+        in_specs=[vmem] * (arrays + 2),
+        out_specs=(vmem, vmem, vmem),
+        scratch_shapes=[pltpu.VMEM(values[0].shape, values[0].dtype)]
+        + [
+            pltpu.VMEM(chunk_shape, jnp.float32),
+            pltpu.VMEM(chunk_shape, jnp.float32),
             pltpu.SemaphoreType.DMA((arrays, count)),
             pltpu.SemaphoreType.DMA((arrays, count)),
             pltpu.SemaphoreType.DMA((arrays,)),
             pltpu.SemaphoreType.DMA((2,)),
             pltpu.SemaphoreType.DMA((2,)),
             pltpu.SemaphoreType.DMA(()),
+            pltpu.SemaphoreType.DMA((members,)),
+            pltpu.SemaphoreType.DMA((members,)),
+            pltpu.SemaphoreType.DMA((members,)),
+            pltpu.SemaphoreType.DMA((members,)),
         ],
         compiler_params=pltpu.CompilerParams(collective_id=collective, has_side_effects=True),
-    )(*values, piece)
-    return outs[:arrays], outs[arrays]
+    )(*values, piece, down_local)
+    return outs
 
 
 def exchange_project_kernel(
@@ -545,19 +628,10 @@
     return summed.reshape(values.shape)
 
 
-def owner_adapter_term(received, slot_ids, down_local, up_local):
-    sources, rows, part_width = received.shape
-    local_adapters, unused_item, adapter_rank = down_local.shape
-    query_width = up_local.shape[2]
-    token_rows = received.reshape(sources * rows, part_width)
-    every_down = jnp.einsum(
-        "td,adr->tar", token_rows, down_local, preferred_element_type=jnp.float32
-    )
+def adapter_up(adapter_middle, slot_ids, up_local):
+    sources, rows = slot_ids.shape
+    local_adapters, adapter_rank, query_width = up_local.shape
     pick = slot_ids.reshape(sources * rows)[:, None] == jnp.arange(local_adapters, dtype=jnp.int32)[None, :]
-    partial_value_sum = jnp.sum(jnp.where(pick[:, :, None], every_down, 0.0), axis=1)
-    tp_count = lax.axis_size("tp")
-    summed = axis_sum(partial_value_sum.reshape(-1, 128), "tp", tp_count, 2, jnp.bfloat16)
-    adapter_middle = summed.reshape(sources * rows, adapter_rank)
     spread_rows = jnp.where(pick[:, :, None], adapter_middle[:, None, :], jnp.zeros((), jnp.bfloat16))
     spread_rows = spread_rows.reshape(sources * rows, local_adapters * adapter_rank)
     adapter_output = jnp.dot(
@@ -610,15 +684,17 @@
     send_tokens = jnp.dot(place_tokens, token_rows, preferred_element_type=jnp.float32).astype(jnp.bfloat16)
     send_tokens = send_tokens.reshape(group_count, CAP * step_count, part_width)
     send_ids = jnp.dot(
-        place, local_slot.astype(jnp.bfloat16)[:, None], preferred_element_type=jnp.float32
+        place_tokens, local_slot.astype(jnp.bfloat16)[:, None].repeat(step_count, axis=0),
+        preferred_element_type=jnp.float32,
     ).astype(jnp.bfloat16)
-    send_ids = jnp.broadcast_to(send_ids.reshape(group_count, CAP, 1), (group_count, CAP, 128))
-    send_ids = jnp.concatenate([send_ids, jnp.zeros_like(send_ids)], axis=1)
-    (got_tokens, got_ids), chip_pieces = exchange_ring(
-        (send_tokens, send_ids), token_rows, "grp", group_count, "tp", 0
-    )
-    got_ids = jnp.repeat(got_ids[:, :CAP, 0].astype(jnp.int32), step_count, axis=1)
-    owner_out = owner_adapter_term(got_tokens, got_ids, pooled_down_weights, pool_up)
+    send_ids = jnp.broadcast_to(
+        send_ids.reshape(group_count, CAP * step_count, 1), (group_count, CAP * step_count, 128)
+    )
+    total, chip_pieces, got_ids = exchange_ring(
+        (send_tokens, send_ids), token_rows, pooled_down_weights, "grp", group_count, "tp", 0
+    )
+    adapter_middle = total.reshape(group_count * CAP * step_count, adapter_rank)
+    owner_out = adapter_up(adapter_middle, got_ids[:, :, 0].astype(jnp.int32), pool_up)
     position = lengths[:, None] + jnp.arange(step_count, dtype=jnp.int32)[None, :]
     half_width = HD // 2
     inv_freq = jnp.exp(

time: 84.8 us -> 85.2 us (level)
  matrix products: 10.7 us -> 8.85 us
  Pallas kernels: 60.8 us -> 62 us
  local copies, waits for them, and re-layouts: 6.67 us -> 7.54 us
    pallas_call x1, Pallas kernels: 24.9 us -> 39.8 us  [exchange_ring(): pl.pallas_call(lambda *refs: exchange_ring_kernel(axis, count, gather_axi...]
    pallas_call x1 -> x0, Pallas kernels: 13.4 us -> none  [axis_sum(): pl.pallas_call(lambda *refs: sum_kernel(axis, count, *refs), out_shape=ja...]
    unnamed x1 -> x0, matrix products: 1.96 us -> none
    unnamed x15 -> x16, local copies, waits for them, and re-layouts: 1.26 us -> 3.08 us
where the time goes in v13:
time: 85.2 us; the launch traced here: 84.7 us
  Pallas kernels  62 us (73%)
  matrix products  8.85 us (10%)
  local copies, waits for them, and re-layouts  7.54 us (9%)
  other arithmetic  6.13 us (7%)
    pallas_call x1, Pallas kernels, exchange_ring(): pl.pallas_call(lambda *refs: exchange_ring_kernel(axis, count, gather_axi...  39.8 us
    pallas_call x1, Pallas kernels, exchange_project(): pl.pallas_call(lambda *refs: exchange_project_kernel(axis, count, gather_...  22.2 us
    dot_general x1, matrix products, attend(): jnp.einsum('rskgd,rtkd->rskgt', queries, key_new, preferred_element_type=...  3.3 us
    unnamed x16, local copies, waits for them, and re-layouts  3.08 us
    dot_general x1, matrix products, adapter_up(): jnp.dot(spread_rows, up_local.reshape(local_adapters * adapter_rank, quer...  1.73 us

profile of v13, /device:TPU:1, one launch (start us, length us, event | category | flops | bytes accessed | tf_op | source)
XLA Modules:
  0.0 84.7 jit_solution(6598954335905659937)
XLA Ops:
  0.0 1.0 %select_reduce_fusion = s32[64]{0:T(128)S(1)} fusion(s32[128]{0:T(128)} %param.13, s32[64]{0:T(128)} %param.12), kind=kLoop, calls=%fused_computation.43 | loop fusion | flops 24512 | bytes 1024 | tf_op jit(solution)/shard_map/reduce_sum | solution.py:669
  1.0 0.2 convert_reduce_fusion.1
  1.2 0.1 iota_add_fusion
  1.3 0.1 add.86
  1.4 1.2 %reshape.249.refs_2_ = bf16[256,1024]{1,0:T(8,128)(2,1)S(1)} reshape(bf16[64,4,1024]{2,1,0:T(4,128)(2,1)} %param.11) | data formatting | bytes 1048576 | tf_op jit(solution)/shard_map/reshape | solution.py:683
  2.6 1.4 %convolution_convert_fusion = bf16[512,1024]{1,0:T(8,128)(2,1)} fusion(bf16[256,1024]{1,0:T(8,128)(2,1)S(1)} %reshape.249.refs_2_, s32[256]{0:T(256)S(1)} %add.86), kind=kOutput, calls=%fused_computation.1 | convolution fusion | flops 269090816 | bytes 1573888 | tf_op jit(solution)/shard_map/dot_general | solution.py:684
  4.0 0.1 broadcast_in_dim.110
  4.1 0.1 reshape.259
  4.2 0.2 fusion.13
  4.4 0.1 broadcast_in_dim.112
  4.5 0.8 broadcast_in_dim.113.refs_1_
  5.3 1.8 %copy.16.refs_3_ = bf16[8,1024,64]{2,1,0:T(8,128)(2,1)} copy(bf16[8,1024,64]{1,2,0:T(8,128)(2,1)S(1)} %copy-done.2) | data formatting | bytes 2097152 | tf_op args[7]
  7.1 39.8 %shard_map.109 = (bf16[8,64,64]{2,1,0:T(8,128)(2,1)}, bf16[3,256,1024]{2,1,0:T(8,128)(2,1)}, bf16[16,32,128]{2,1,0:T(8,128)(2,1)}) custom-call(bf16[16,32,1024]{2,1,0:T(8,128)(2,1)} %bitcast.70, bf16[16,32,128]{2,1,0:T(8,128)(2,1)} %broadcast_in_dim.113.refs_1_, bf16[256,1024]{1,0:T(8,128)(2,1)} %copy-done.1, bf16[8,1024,64]{2,1,0:T(8,128)(2,1)} %copy.16.refs_3_), custom_call_target="tpu_custom_call" | custom-call | tf_op jit(solution)/shard_map/pallas_call | solution.py:324
  46.9 1.0 %copy.17 = bf16[512,64]{0,1:T(8,128)(2,1)S(1)} copy(bf16[512,64]{1,0:T(8,128)(2,1)} %bitcast.75) | data formatting | bytes 131072 | tf_op jit(solution)/shard_map/jit(_where)/broadcast_in_dim | solution.py:635
  47.9 1.2 %convert_reduce_fusion = s32[16,32]{1,0:T(8,128)S(1)} fusion(bf16[16,32,128]{2,1,0:T(8,128)(2,1)} %get-tuple-element.11), kind=kLoop, calls=%fused_computation.30 | loop fusion | flops 512 | bytes 3072 | tf_op jit(solution)/shard_map/convert_element_type | solution.py:697
  49.2 0.1 reshape.258
  49.3 1.7 %bitcast_convert_fusion = bf16[512,1024]{1,0:T(8,128)(2,1)} fusion(bf16[8,64,1024]{2,1,0:T(8,128)(2,1)S(1)} %copy-done, pred[512,8]{0,1:T(8,128)(4,1)S(1)} %iota_compare_fusion.7, bf16[512,64]{0,1:T(8,128)(2,1)S(1)} %copy.17), kind=kOutput, calls=%fused_computation | convolution fusion | flops 537657344 | bytes 2166784 | tf_op jit(solution)/shard_map/dot_general | solution.py:637
  51.0 0.8 fusion.14.refs_5_
  51.9 0.1 compare_select_fusion
  51.9 0.1 add_convert_fusion
  52.0 0.1 convert_element_type.64
  52.1 1.2 %fusion.23 = (f32[256,128]{1,0:T(8,128)}, f32[256,128]{1,0:T(8,128)}) fusion(f32[128]{0:T(128)S(1)} %get-tuple-element.25, f32[128]{0:T(128)S(1)} %get-tuple-element.26, f32[256]{0:T(256)S(1)} %convert_element_type.64), kind=kLoop, calls=%fused_computation.38 | loop fusion | flops 65536 | bytes 264192 | tf_op jit(solution)/shard_map/mul | solution.py:707
  53.4 22.2 %shard_map.110 = (bf16[256,1024]{1,0:T(8,128)(2,1)}, bf16[256,128]{1,0:T(8,128)(2,1)}, bf16[256,128]{1,0:T(8,128)(2,1)}) custom-call(bf16[16,32,1024]{2,1,0:T(8,128)(2,1)} %bitcast.73, bf16[3,256,1024]{2,1,0:T(8,128)(2,1)} %get-tuple-element.13.refs_1_, bf16[8192,1024]{1,0:T(8,128)(2,1)} %refs_2_.1, bf16[8192,128]{1,0:T(8,128)(2,1)} %refs_3_.2, ...), custom_call_target="tpu_custom_call" | custom-call | tf_op jit(solution)/shard_map/pallas_call | solution.py:515
  75.6 1.2 %copy.22 = bf16[32,8,8,128]{3,2,1,0:T(8,128)(2,1)S(1)} copy(bf16[32,8,8,128]{3,1,2,0:T(8,128)(2,1)} %bitcast.74) | data formatting | bytes 1048576
  76.8 3.3 %fusion.28 = (f32[64,4,8]{2,1,0:T(4,128)S(1)}, f32[64,4,1,8,4]{3,4,1,0,2:T(4,128)S(1)}) fusion(bf16[64,4,128,1]{2,1,3,0:T(4,128)(2,1)} %bitcast.78, bf16[64,4,8,128]{3,2,1,0:T(8,128)(2,1)S(1)} %bitcast.71, pred[4,4]{1,0:T(4,128)(4,1)S(1)} %iota_compare_fusion.8), kind=kOutput, calls=%fused_computation.61 | convolution fusion | flops 2119680 | bytes 630800 | tf_op jit(solution)/shard_map/rskgd,rtkd->rskgt/dot_general | solution.py:41
  80.1 0.1 iota_compare_fusion.6
  80.2 0.8 fusion.27
  81.1 0.5 fusion.16
  81.5 0.8 fusion.9
  82.4 0.9 %convolution_bitcast_fusion = f32[64,128,4,8]{1,3,2,0:T(8,128)S(1)} fusion(bf16[64,64,128]{2,1,0:T(8,128)(2,1)S(1)} %copy-done.5, f32[64,4,1,8,64]{4,3,1,0,2:T(8,128)S(1)} %get-tuple-element.22, f32[64,4,8]{2,1,0:T(4,128)S(1)} %add.91, f32[64,4,8]{2,1,0:T(4,128)S(1)} %max.9), kind=kOutput, calls=%fused_computation.5 | convolution fusion | flops 33947648 | bytes 2637824 | tf_op jit(solution)/shard_map/rskgl,rlkd->rskgd/dot_general | solution.py:58
  83.3 0.5 fusion.4
  83.8 0.9 %reshape.257 = bf16[64,4,1024]{2,1,0:T(4,128)(2,1)} reshape(bf16[64,4,1,8,128]{4,3,1,0,2:T(8,128)(2,1)S(1)} %fusion.4) | data formatting | bytes 1048576 | tf_op jit(solution)/shard_map/reshape | solution.py:719
  (22 shorter events, 0.2 us)
Async XLA Ops:
  0.0 49.3 %copy-start = (bf16[8,64,1024]{2,1,0:T(8,128)(2,1)S(1)}, bf16[8,64,1024]{2,1,0:T(8,128)(2,1)}, u32[]{:S(2)}) copy-start(bf16[8,64,1024]{2,1,0:T(8,128)(2,1)} %param.19) | copy-start | bytes 3145732
  0.0 5.3 %copy-start.2 = (bf16[8,1024,64]{1,2,0:T(8,128)(2,1)S(1)}, bf16[8,1024,64]{1,2,0:T(8,128)(2,1)}, u32[]{:S(2)}) copy-start(bf16[8,1024,64]{1,2,0:T(8,128)(2,1)} %param.18) | copy-start | bytes 3145732
  2.6 4.5 %copy-start.1 = (bf16[256,1024]{1,0:T(8,128)(2,1)}, bf16[256,1024]{1,0:T(8,128)(2,1)S(1)}, u32[]{:S(2)}) copy-start(bf16[256,1024]{1,0:T(8,128)(2,1)S(1)} %reshape.249.refs_2_) | copy-start | bytes 1572868
  49.3 2.6 %copy-start.4 = (s32[64]{0:T(128)S(1)}, s32[64]{0:T(128)}, u32[]{:S(2)}) copy-start(s32[64]{0:T(128)} %param.14) | copy-start | bytes 772
  75.6 4.6 %copy-start.3 = (bf16[64,64,128]{2,1,0:T(8,128)(2,1)S(1)}, bf16[64,64,128]{2,1,0:T(8,128)(2,1)}, u32[]{:S(2)}) copy-start(bf16[64,64,128]{2,1,0:T(8,128)(2,1)} %param.20) | copy-start | bytes 3145732
  81.0 1.3 %copy-start.5 = (bf16[64,64,128]{2,1,0:T(8,128)(2,1)S(1)}, bf16[64,64,128]{2,1,0:T(8,128)(2,1)}, u32[]{:S(2)}) copy-start(bf16[64,64,128]{2,1,0:T(8,128)(2,1)} %param.21) | copy-start | bytes 3145732
  82.4 0.9 %copy-start.6 = (bf16[256,128]{1,0:T(8,128)(2,1)S(1)}, bf16[256,128]{1,0:T(8,128)(2,1)}, u32[]{:S(2)}) copy-start(bf16[256,128]{1,0:T(8,128)(2,1)} %get-tuple-element.16) | copy-start | bytes 196612

commit v14 on v11

--- a/solution.py
+++ b/solution.py
@@ -37,8 +37,12 @@
         jnp.einsum("rskgd,rlkd->rskgl", queries, cache_key, preferred_element_type=jnp.float32)
         * score_scale
     )
+    fresh_keys = jnp.transpose(key_new, (0, 2, 1, 3)).astype(jnp.float32)
     fresh_scores = (
-        jnp.einsum("rskgd,rtkd->rskgt", queries, key_new, preferred_element_type=jnp.float32)
+        jnp.sum(
+            queries.astype(jnp.float32)[:, :, :, :, None, :] * fresh_keys[:, None, :, None, :, :],
+            axis=-1,
+        )
         * score_scale
     )
     live_mask = jnp.arange(cache_key.shape[1], dtype=jnp.int32)[None, :] < lengths[:, None]

time: 84.9 us -> 84.1 us (level)
  matrix products: 10.7 us -> 7.58 us
  other arithmetic: 5.79 us -> 8.17 us
    dot_general x1 -> x0, matrix products: 3.3 us -> none  [attend(): jnp.einsum('rskgd,rtkd->rskgt', queries, key_new, preferred_element_type=...]
    reduce_sum x0 -> x1, other arithmetic: none -> 1.59 us  [attend(): jnp.sum(queries.astype(jnp.float32)[:, :, :, :, None, :] * fresh_keys[:,...]
where the time goes in v14:
time: 84.1 us; the launch traced here: 83.4 us
  Pallas kernels  60.8 us (72%)
  other arithmetic  8.17 us (10%)
  matrix products  7.58 us (9%)
  local copies, waits for them, and re-layouts  6.61 us (8%)
    pallas_call x1, Pallas kernels, exchange_ring(): pl.pallas_call(lambda *refs: exchange_ring_kernel(axis, count, gather_axi...  24.9 us
    pallas_call x1, Pallas kernels, exchange_project(): pl.pallas_call(lambda *refs: exchange_project_kernel(axis, count, gather_...  22.4 us
    pallas_call x1, Pallas kernels, axis_sum(): pl.pallas_call(lambda *refs: sum_kernel(axis, count, *refs), out_shape=ja...  13.4 us
    unnamed x1, matrix products  1.96 us
    dot_general x1, matrix products, owner_adapter_term(): jnp.dot(spread_rows, up_local.reshape(local_adapters * adapter_rank, quer...  1.71 us

profile of v14, /device:TPU:1, one launch (start us, length us, event | category | flops | bytes accessed | tf_op | source)
XLA Modules:
  0.0 83.4 jit_solution(13471377585717704499)
XLA Ops:
  0.0 0.9 %select_reduce_fusion.1 = s32[64]{0:T(128)S(1)} fusion(s32[128]{0:T(128)} %param.13, s32[64]{0:T(128)} %param.12), kind=kLoop, calls=%fused_computation.51 | loop fusion | flops 24512 | bytes 1024 | tf_op jit(solution)/shard_map/reduce_sum | solution.py:599
  1.0 0.2 convert_reduce_fusion
  1.2 0.1 add.93
  1.4 1.2 %reshape.271.refs_2_ = bf16[256,1024]{1,0:T(8,128)(2,1)S(1)} reshape(bf16[64,4,1024]{2,1,0:T(4,128)(2,1)} %param.11) | data formatting | bytes 1048576 | tf_op jit(solution)/shard_map/reshape | solution.py:613
  2.5 1.4 %convolution_convert_fusion = bf16[512,1024]{1,0:T(8,128)(2,1)} fusion(bf16[256,1024]{1,0:T(8,128)(2,1)S(1)} %reshape.271.refs_2_, s32[256]{0:T(256)S(1)} %add.93), kind=kOutput, calls=%fused_computation.2 | convolution fusion | flops 269090816 | bytes 1573888 | tf_op jit(solution)/shard_map/dot_general | solution.py:614
  4.0 0.1 fusion.5
  4.3 0.6 concatenate.9.refs_1_
  4.9 24.9 %shard_map.109 = (bf16[16,32,1024]{2,1,0:T(8,128)(2,1)}, bf16[16,16,128]{2,1,0:T(8,128)(2,1)}, bf16[3,256,1024]{2,1,0:T(8,128)(2,1)}) custom-call(bf16[16,32,1024]{2,1,0:T(8,128)(2,1)} %bitcast.72, bf16[16,16,128]{2,1,0:T(8,128)(2,1)} %concatenate.9.refs_1_, bf16[256,1024]{1,0:T(8,128)(2,1)} %copy-done.1), custom_call_target="tpu_custom_call" | custom-call | tf_op jit(solution)/shard_map/pallas_call | solution.py:253
  29.9 0.8 slice_convert_fusion
  30.6 0.2 copy.33
  30.9 0.1 eq.92
  31.0 2.0 %fusion.38 = f32[512,512]{0,1:S(1)} fusion(bf16[512,1024]{1,0:T(8,128)(2,1)} %bitcast.78, bf16[1024,512]{0,1:T(8,128)(2,1)S(1)} %bitcast.69), kind=kOutput, calls=%fused_computation.75 | convolution fusion | flops 536870912 | bytes 3145728
  33.0 0.1 select_reduce_fusion
  33.1 0.1 copy.28
  33.3 0.8 reshape_reshape.3.refs_0_
  34.0 13.4 %shard_map.110 = bf16[8,32,128]{2,1,0:T(8,128)(2,1)} custom-call(f32[8,32,128]{2,1,0:T(8,128)} %reshape_reshape.3.refs_0_), custom_call_target="tpu_custom_call" | custom-call | tf_op jit(solution)/shard_map/pallas_call | solution.py:535
  47.5 0.9 %broadcast_in_dim.82 = bf16[512,64]{1,0:T(8,128)(2,1)S(1)} reshape(bf16[8,32,128]{2,1,0:T(8,128)(2,1)} %shard_map.110) | data formatting | bytes 131072 | tf_op jit(solution)/shard_map/jit(_where)/broadcast_in_dim | solution.py:565
  48.5 1.7 %bitcast_convert_fusion = bf16[512,1024]{1,0:T(8,128)(2,1)} fusion(bf16[8,64,1024]{2,1,0:T(8,128)(2,1)S(1)} %copy-done.5, pred[512,8]{0,1:T(8,128)(4,1)S(1)} %iota_compare_fusion.8, bf16[512,64]{0,1:T(8,128)(2,1)S(1)} %copy.29), kind=kOutput, calls=%fused_computation.1 | convolution fusion | flops 537657344 | bytes 2166784 | tf_op jit(solution)/shard_map/dot_general | solution.py:567
  50.5 0.5 fusion.24
  51.0 0.9 %pad_maximum_fusion = (f32[256,128]{1,0:T(8,128)}, f32[256,128]{1,0:T(8,128)}) fusion(f32[256,64]{1,0:T(8,128)S(1)} %get-tuple-element.21, f32[256,64]{1,0:T(8,128)S(1)} %get-tuple-element.20, f32[256,64]{1,0:T(8,128)S(1)} %get-tuple-element.19), kind=kLoop, calls=%fused_computation.41 | loop fusion | flops 65536 | bytes 458752 | tf_op jit(solution)/shard_map/concatenate | solution.py:632
  51.9 0.8 fusion.12.refs_5_
  52.7 22.4 %shard_map.111 = (bf16[256,1024]{1,0:T(8,128)(2,1)}, bf16[256,128]{1,0:T(8,128)(2,1)}, bf16[256,128]{1,0:T(8,128)(2,1)}) custom-call(bf16[16,32,1024]{2,1,0:T(8,128)(2,1)} %bitcast.73, bf16[3,256,1024]{2,1,0:T(8,128)(2,1)} %get-tuple-element.13.refs_1_, bf16[8192,1024]{1,0:T(8,128)(2,1)} %refs_2_.1, bf16[8192,128]{1,0:T(8,128)(2,1)} %refs_3_.1, ...), custom_call_target="tpu_custom_call" | custom-call | tf_op jit(solution)/shard_map/pallas_call | solution.py:436
  75.1 1.2 %copy.34 = bf16[32,8,8,128]{3,2,1,0:T(8,128)(2,1)S(1)} copy(bf16[32,8,8,128]{3,1,2,0:T(8,128)(2,1)} %bitcast.75) | data formatting | bytes 1048576
  76.3 0.1 convert_element_type.88
  76.5 1.6 %multiply_reduce_fusion = f32[64,4,8,4]{2,3,1,0:T(4,128)S(1)} fusion(f32[64,4,128]{2,1,0:T(4,128)S(1)} %convert.2, f32[64,4,8,128]{3,2,1,0:T(8,128)S(1)} %convert_element_type.88), kind=kLoop, calls=%fused_computation | loop fusion | flops 2088960 | bytes 1212416 | tf_op jit(solution)/shard_map/reduce_sum | solution.py:42
  78.1 0.5 fusion.14
  78.7 0.8 fusion.37
  79.5 0.6 fusion.15
  80.1 0.8 fusion.8
  80.9 0.9 %convolution_bitcast_fusion = f32[64,128,4,8]{1,3,2,0:T(8,128)S(1)} fusion(bf16[64,64,128]{2,1,0:T(8,128)(2,1)S(1)} %copy-done.6, f32[64,4,1,8,64]{4,3,1,0,2:T(8,128)S(1)} %get-tuple-element.23, f32[64,4,8]{2,1,0:T(4,128)S(1)} %add.98, f32[64,4,8]{2,1,0:T(4,128)S(1)} %max.9), kind=kOutput, calls=%fused_computation.6 | convolution fusion | flops 33947648 | bytes 2637824 | tf_op jit(solution)/shard_map/rskgl,rlkd->rskgd/dot_general | solution.py:62
  81.9 0.6 fusion.4
  82.5 0.9 %reshape.278 = bf16[64,4,1024]{2,1,0:T(4,128)(2,1)} reshape(bf16[64,4,1,8,128]{4,3,1,0,2:T(8,128)(2,1)S(1)} %fusion.4) | data formatting | bytes 1048576 | tf_op jit(solution)/shard_map/reshape | solution.py:644
  (32 shorter events, 0.9 us)
Async XLA Ops:
  0.0 31.0 %copy-start = (bf16[8,1024,64]{1,2,0:T(8,128)(2,1)S(1)}, bf16[8,1024,64]{1,2,0:T(8,128)(2,1)}, u32[]{:S(2)}) copy-start(bf16[8,1024,64]{1,2,0:T(8,128)(2,1)} %param.18) | copy-start | bytes 3145732
  2.5 2.4 %copy-start.1 = (bf16[256,1024]{1,0:T(8,128)(2,1)}, bf16[256,1024]{1,0:T(8,128)(2,1)S(1)}, u32[]{:S(2)}) copy-start(bf16[256,1024]{1,0:T(8,128)(2,1)S(1)} %reshape.271.refs_2_) | copy-start | bytes 1572868
  33.0 15.5 %copy-start.5 = (bf16[8,64,1024]{2,1,0:T(8,128)(2,1)S(1)}, bf16[8,64,1024]{2,1,0:T(8,128)(2,1)}, u32[]{:S(2)}) copy-start(bf16[8,64,1024]{2,1,0:T(8,128)(2,1)} %param.19) | copy-start | bytes 3145732
  48.5 1.7 %copy-start.4 = (s32[64]{0:T(128)S(1)}, s32[64]{0:T(128)}, u32[]{:S(2)}) copy-start(s32[64]{0:T(128)} %param.14) | copy-start | bytes 772
  75.1 1.3 %copy-start.3 = (bf16[256,128]{1,0:T(8,128)(2,1)S(1)}, bf16[256,128]{1,0:T(8,128)(2,1)}, u32[]{:S(2)}) copy-start(bf16[256,128]{1,0:T(8,128)(2,1)} %get-tuple-element.15) | copy-start | bytes 196612
  76.3 2.4 %copy-start.2 = (bf16[64,64,128]{2,1,0:T(8,128)(2,1)S(1)}, bf16[64,64,128]{2,1,0:T(8,128)(2,1)}, u32[]{:S(2)}) copy-start(bf16[64,64,128]{2,1,0:T(8,128)(2,1)} %param.20) | copy-start | bytes 3145732
  79.4 1.5 %copy-start.6 = (bf16[64,64,128]{2,1,0:T(8,128)(2,1)S(1)}, bf16[64,64,128]{2,1,0:T(8,128)(2,1)}, u32[]{:S(2)}) copy-start(bf16[64,64,128]{2,1,0:T(8,128)(2,1)} %param.21) | copy-start | bytes 3145732
  80.9 1.0 %copy-start.7 = (bf16[256,128]{1,0:T(8,128)(2,1)S(1)}, bf16[256,128]{1,0:T(8,128)(2,1)}, u32[]{:S(2)}) copy-start(bf16[256,128]{1,0:T(8,128)(2,1)} %get-tuple-element.16) | copy-start | bytes 196612

commit v15 on v14

--- a/solution.py
+++ b/solution.py
@@ -62,8 +62,10 @@
     combined = jnp.einsum(
         "rskgl,rlkd->rskgd", cache_weights, cache_value, preferred_element_type=jnp.float32
     )
-    combined = combined + jnp.einsum(
-        "rskgt,rtkd->rskgd", fresh_weights, value_new, preferred_element_type=jnp.float32
+    fresh_values = jnp.transpose(value_new, (0, 2, 1, 3)).astype(jnp.float32)
+    combined = combined + jnp.sum(
+        fresh_weights.astype(jnp.float32)[..., None] * fresh_values[:, None, :, None, :, :],
+        axis=4,
     )
     return combined.astype(jnp.bfloat16)
 

time: 84.1 us -> 88.6 us (1.054)
  matrix products: 7.58 us -> 9.46 us
  other arithmetic: 8.17 us -> 9.71 us
  local copies, waits for them, and re-layouts: 6.61 us -> 7.56 us
    reduce_sum x0 -> x1, other arithmetic: none -> 1.48 us  [attend(): jnp.sum(fresh_weights.astype(jnp.float32)[..., None] * fresh_values[:, No...]
    dot_general x1, matrix products: 0.94 us -> 2.22 us  [attend(): jnp.einsum('rskgl,rlkd->rskgd', cache_weights, cache_value, preferred_ele...]
    dot_general x1, matrix products: 0.79 us -> 2.01 us  [attend(): jnp.einsum('rskgd,rlkd->rskgl', queries, cache_key, preferred_element_typ...]
where the time goes in v15:
time: 88.6 us; the launch traced here: 87.8 us
  Pallas kernels  60.8 us (69%)
  other arithmetic  9.71 us (11%)
  matrix products  9.46 us (11%)
  local copies, waits for them, and re-layouts  7.56 us (9%)
    pallas_call x1, Pallas kernels, exchange_ring(): pl.pallas_call(lambda *refs: exchange_ring_kernel(axis, count, gather_axi...  24.9 us
    pallas_call x1, Pallas kernels, exchange_project(): pl.pallas_call(lambda *refs: exchange_project_kernel(axis, count, gather_...  22.4 us
    pallas_call x1, Pallas kernels, axis_sum(): pl.pallas_call(lambda *refs: sum_kernel(axis, count, *refs), out_shape=ja...  13.4 us
    dot_general x1, matrix products, attend(): jnp.einsum('rskgl,rlkd->rskgd', cache_weights, cache_value, preferred_ele...  2.22 us
    dot_general x1, matrix products, attend(): jnp.einsum('rskgd,rlkd->rskgl', queries, cache_key, preferred_element_typ...  2.01 us
    unnamed x1, matrix products  1.96 us

profile of v15, /device:TPU:1, one launch (start us, length us, event | category | flops | bytes accessed | tf_op | source)
XLA Modules:
  0.0 87.8 jit_solution(13831385814535386345)
XLA Ops:
  0.0 0.9 %select_reduce_fusion.1 = s32[64]{0:T(128)S(1)} fusion(s32[128]{0:T(128)} %param.13, s32[64]{0:T(128)} %param.12), kind=kLoop, calls=%fused_computation.47 | loop fusion | flops 24512 | bytes 1024 | tf_op jit(solution)/shard_map/reduce_sum | solution.py:601
  1.0 0.2 convert_reduce_fusion
  1.4 1.2 %reshape.288.refs_2_ = bf16[256,1024]{1,0:T(8,128)(2,1)S(1)} reshape(bf16[64,4,1024]{2,1,0:T(4,128)(2,1)} %param.11) | data formatting | bytes 1048576 | tf_op jit(solution)/shard_map/reshape | solution.py:615
  2.5 1.4 %convolution_convert_fusion = bf16[512,1024]{1,0:T(8,128)(2,1)} fusion(bf16[256,1024]{1,0:T(8,128)(2,1)S(1)} %reshape.288.refs_2_, s32[256]{0:T(256)S(1)} %add.91), kind=kOutput, calls=%fused_computation.3 | convolution fusion | flops 269090816 | bytes 1573888 | tf_op jit(solution)/shard_map/dot_general | solution.py:616
  4.0 0.1 fusion.5
  4.3 0.6 concatenate.9.refs_1_
  4.9 24.9 %shard_map.109 = (bf16[16,32,1024]{2,1,0:T(8,128)(2,1)}, bf16[16,16,128]{2,1,0:T(8,128)(2,1)}, bf16[3,256,1024]{2,1,0:T(8,128)(2,1)}) custom-call(bf16[16,32,1024]{2,1,0:T(8,128)(2,1)} %bitcast.74, bf16[16,16,128]{2,1,0:T(8,128)(2,1)} %concatenate.9.refs_1_, bf16[256,1024]{1,0:T(8,128)(2,1)} %copy-done.1), custom_call_target="tpu_custom_call" | custom-call | tf_op jit(solution)/shard_map/pallas_call | solution.py:255
  29.9 0.8 slice_convert_fusion
  30.6 0.2 copy.60
  30.9 0.1 eq.92
  31.0 2.0 %fusion.32 = f32[512,512]{0,1:S(1)} fusion(bf16[512,1024]{1,0:T(8,128)(2,1)} %bitcast.81, bf16[1024,512]{0,1:T(8,128)(2,1)S(1)} %bitcast.71), kind=kOutput, calls=%fused_computation.69 | convolution fusion | flops 536870912 | bytes 3145728
  33.0 0.1 select_reduce_fusion
  33.1 0.1 copy.50
  33.3 0.8 reshape_reshape.3.refs_0_
  34.0 13.4 %shard_map.110 = bf16[8,32,128]{2,1,0:T(8,128)(2,1)} custom-call(f32[8,32,128]{2,1,0:T(8,128)} %reshape_reshape.3.refs_0_), custom_call_target="tpu_custom_call" | custom-call | tf_op jit(solution)/shard_map/pallas_call | solution.py:537
  47.5 0.9 %broadcast_in_dim.82 = bf16[512,64]{1,0:T(8,128)(2,1)S(1)} reshape(bf16[8,32,128]{2,1,0:T(8,128)(2,1)} %shard_map.110) | data formatting | bytes 131072 | tf_op jit(solution)/shard_map/jit(_where)/broadcast_in_dim | solution.py:567
  48.5 1.7 %bitcast_convert_fusion = bf16[512,1024]{1,0:T(8,128)(2,1)} fusion(bf16[8,64,1024]{2,1,0:T(8,128)(2,1)S(1)} %copy-done.4, pred[512,8]{0,1:T(8,128)(4,1)S(1)} %iota_compare_fusion.8, bf16[512,64]{0,1:T(8,128)(2,1)S(1)} %copy.51), kind=kOutput, calls=%fused_computation.2 | convolution fusion | flops 537657344 | bytes 2166784 | tf_op jit(solution)/shard_map/dot_general | solution.py:569
  50.5 0.5 fusion.19
  51.0 0.9 pad_maximum_fusion
  51.9 0.8 fusion.12.refs_5_
  52.7 22.4 %shard_map.111 = (bf16[256,1024]{1,0:T(8,128)(2,1)}, bf16[256,128]{1,0:T(8,128)(2,1)}, bf16[256,128]{1,0:T(8,128)(2,1)}) custom-call(bf16[16,32,1024]{2,1,0:T(8,128)(2,1)} %bitcast.75, bf16[3,256,1024]{2,1,0:T(8,128)(2,1)} %get-tuple-element.13.refs_1_, bf16[8192,1024]{1,0:T(8,128)(2,1)} %refs_2_.1, bf16[8192,128]{1,0:T(8,128)(2,1)} %refs_3_.1, ...), custom_call_target="tpu_custom_call" | custom-call | tf_op jit(solution)/shard_map/pallas_call | solution.py:438
  75.1 1.1 %copy.61 = bf16[32,8,8,128]{3,2,1,0:T(8,128)(2,1)S(1)} copy(bf16[32,8,8,128]{3,1,2,0:T(8,128)(2,1)} %bitcast.77) | data formatting | bytes 1048576
  76.2 0.1 convert_element_type.106
  76.4 0.9 convert.3
  77.2 1.6 %multiply_reduce_fusion.1 = f32[64,4,8,4]{2,3,1,0:T(4,128)S(1)} fusion(f32[64,4,128]{2,1,0:T(4,128)S(1)} %convert.3, f32[64,4,8,128]{3,2,1,0:T(8,128)S(1)} %convert_element_type.106), kind=kLoop, calls=%fused_computation.1 | loop fusion | flops 2088960 | bytes 1212416 | tf_op jit(solution)/shard_map/reduce_sum | solution.py:42
  78.8 0.3 copy.52
  79.4 2.0 %fusion.31 = (f32[64,4,8]{2,1,0:T(4,128)S(1)}, f32[64,4,1,8,64]{4,3,1,0,2:T(8,128)S(1)}) fusion(bf16[64,4,8,128]{3,2,1,0:T(8,128)(2,1)S(1)} %bitcast.73, bf16[64,64,128]{2,1,0:T(8,128)(2,1)} %param.20, pred[64,64]{1,0:T(8,128)(4,1)S(1)} %iota_compare_fusion.7), kind=kOutput, calls=%fused_computation.68 | convolution fusion | flops 33945600 | bytes 2109440 | tf_op jit(solution)/shard_map/rskgd,rlkd->rskgl/dot_general | solution.py:37
  81.8 0.8 fusion.8
  82.8 0.3 copy.57
  83.2 1.5 %multiply_reduce_fusion = f32[64,4,8,128]{3,2,1,0:T(8,128)S(1)} fusion(f32[64,4,128]{2,1,0:T(4,128)S(1)} %convert.4, f32[64,4,8,4]{2,3,1,0:T(4,128)S(1)} %copy.57), kind=kLoop, calls=%fused_computation | loop fusion | flops 1835008 | bytes 1212416 | tf_op jit(solution)/shard_map/reduce_sum | solution.py:66
  84.7 2.2 %fusion.2 = bf16[64,4,1,8,128]{4,3,1,0,2:T(8,128)(2,1)S(1)} fusion(bf16[64,64,128]{2,1,0:T(8,128)(2,1)} %param.21, f32[64,4,8,128]{3,2,1,0:T(8,128)S(1)} %multiply_reduce_fusion, f32[64,4,1,8,64]{4,3,1,0,2:T(8,128)S(1)} %get-tuple-element.23, f32[64,4,8]{2,1,0:T(4,128)S(1)} %add.96, f32[64,4,8]{2,1,0:T(4,128)S(1)} %max.9), kind=kOutput, calls=%fused_computation.8 | convolution fusion | flops 34471936 | bytes 3162112 | tf_op jit(solution)/shard_map/rskgl,rlkd->rskgd/dot_general | solution.py:62
  86.9 0.9 %reshape.294 = bf16[64,4,1024]{2,1,0:T(4,128)(2,1)} reshape(bf16[64,4,1,8,128]{4,3,1,0,2:T(8,128)(2,1)S(1)} %fusion.2) | data formatting | bytes 1048576 | tf_op jit(solution)/shard_map/reshape | solution.py:646
  (34 shorter events, 1.7 us)
Async XLA Ops:
  0.0 31.0 %copy-start = (bf16[8,1024,64]{1,2,0:T(8,128)(2,1)S(1)}, bf16[8,1024,64]{1,2,0:T(8,128)(2,1)}, u32[]{:S(2)}) copy-start(bf16[8,1024,64]{1,2,0:T(8,128)(2,1)} %param.18) | copy-start | bytes 3145732
  2.5 2.4 %copy-start.1 = (bf16[256,1024]{1,0:T(8,128)(2,1)}, bf16[256,1024]{1,0:T(8,128)(2,1)S(1)}, u32[]{:S(2)}) copy-start(bf16[256,1024]{1,0:T(8,128)(2,1)S(1)} %reshape.288.refs_2_) | copy-start | bytes 1572868
  4.0 44.6 %copy-start.4 = (bf16[8,64,1024]{2,1,0:T(8,128)(2,1)S(1)}, bf16[8,64,1024]{2,1,0:T(8,128)(2,1)}, u32[]{:S(2)}) copy-start(bf16[8,64,1024]{2,1,0:T(8,128)(2,1)} %param.19) | copy-start | bytes 3145732
  33.1 17.1 %copy-start.3 = (s32[64]{0:T(128)S(1)}, s32[64]{0:T(128)}, u32[]{:S(2)}) copy-start(s32[64]{0:T(128)} %param.14) | copy-start | bytes 772
  77.2 5.9 %copy-start.2 = (bf16[256,128]{1,0:T(8,128)(2,1)S(1)}, bf16[256,128]{1,0:T(8,128)(2,1)}, u32[]{:S(2)}) copy-start(bf16[256,128]{1,0:T(8,128)(2,1)} %get-tuple-element.16) | copy-start | bytes 196612

commit v16 on v14

--- a/solution.py
+++ b/solution.py
@@ -531,7 +531,7 @@
 
 
 def axis_sum(values, axis, count, collective, out_dtype):
-    chunks = values.reshape(count, -1, 128)
+    chunks = values.reshape(count, -1, values.shape[-1])
     summed = pl.pallas_call(
         lambda *refs: sum_kernel(axis, count, *refs),
         out_shape=jax.ShapeDtypeStruct(chunks.shape, out_dtype),
@@ -560,7 +560,7 @@
     pick = slot_ids.reshape(sources * rows)[:, None] == jnp.arange(local_adapters, dtype=jnp.int32)[None, :]
     partial_value_sum = jnp.sum(jnp.where(pick[:, :, None], every_down, 0.0), axis=1)
     tp_count = lax.axis_size("tp")
-    summed = axis_sum(partial_value_sum.reshape(-1, 128), "tp", tp_count, 2, jnp.bfloat16)
+    summed = axis_sum(partial_value_sum, "tp", tp_count, 2, jnp.bfloat16)
     adapter_middle = summed.reshape(sources * rows, adapter_rank)
     spread_rows = jnp.where(pick[:, :, None], adapter_middle[:, None, :], jnp.zeros((), jnp.bfloat16))
     spread_rows = spread_rows.reshape(sources * rows, local_adapters * adapter_rank)

time: 84.1 us -> 85.7 us (1.019)
  Pallas kernels: 60.8 us -> 62.5 us
    pallas_call x1, Pallas kernels: 13.4 us -> 15.2 us  [axis_sum(): pl.pallas_call(lambda *refs: sum_kernel(axis, count, *refs), out_shape=ja...]
where the time goes in v16:
time: 85.7 us; the launch traced here: 85.2 us
  Pallas kernels  62.5 us (73%)
  other arithmetic  8.17 us (10%)
  matrix products  7.65 us (9%)
  local copies, waits for them, and re-layouts  6.52 us (8%)
    pallas_call x1, Pallas kernels, exchange_ring(): pl.pallas_call(lambda *refs: exchange_ring_kernel(axis, count, gather_axi...  24.9 us
    pallas_call x1, Pallas kernels, exchange_project(): pl.pallas_call(lambda *refs: exchange_project_kernel(axis, count, gather_...  22.4 us
    pallas_call x1, Pallas kernels, axis_sum(): pl.pallas_call(lambda *refs: sum_kernel(axis, count, *refs), out_shape=ja...  15.2 us
    unnamed x1, matrix products  2.05 us

profile of v16, /device:TPU:1, one launch (start us, length us, event | category | flops | bytes accessed | tf_op | source)
XLA Modules:
  0.0 85.2 jit_solution(6499430312190821845)
XLA Ops:
  0.0 0.9 %select_reduce_fusion.1 = s32[64]{0:T(128)S(1)} fusion(s32[128]{0:T(128)} %param.13, s32[64]{0:T(128)} %param.12), kind=kLoop, calls=%fused_computation.51 | loop fusion | flops 24512 | bytes 1024 | tf_op jit(solution)/shard_map/reduce_sum | solution.py:599
  1.0 0.2 convert_reduce_fusion
  1.2 0.1 add.93
  1.4 1.2 %reshape.274.refs_2_ = bf16[256,1024]{1,0:T(8,128)(2,1)S(1)} reshape(bf16[64,4,1024]{2,1,0:T(4,128)(2,1)} %param.11) | data formatting | bytes 1048576 | tf_op jit(solution)/shard_map/reshape | solution.py:613
  2.5 1.4 %convolution_convert_fusion = bf16[512,1024]{1,0:T(8,128)(2,1)} fusion(bf16[256,1024]{1,0:T(8,128)(2,1)S(1)} %reshape.274.refs_2_, s32[256]{0:T(256)S(1)} %add.93), kind=kOutput, calls=%fused_computation.2 | convolution fusion | flops 269090816 | bytes 1573888 | tf_op jit(solution)/shard_map/dot_general | solution.py:614
  4.0 0.1 fusion.5
  4.3 0.6 concatenate.9.refs_1_
  4.9 24.9 %shard_map.109 = (bf16[16,32,1024]{2,1,0:T(8,128)(2,1)}, bf16[16,16,128]{2,1,0:T(8,128)(2,1)}, bf16[3,256,1024]{2,1,0:T(8,128)(2,1)}) custom-call(bf16[16,32,1024]{2,1,0:T(8,128)(2,1)} %bitcast.74, bf16[16,16,128]{2,1,0:T(8,128)(2,1)} %concatenate.9.refs_1_, bf16[256,1024]{1,0:T(8,128)(2,1)} %copy-done.1), custom_call_target="tpu_custom_call" | custom-call | tf_op jit(solution)/shard_map/pallas_call | solution.py:253
  29.9 0.8 slice_convert_fusion
  30.6 0.2 copy.33
  30.9 0.1 eq.92
  31.0 2.1 %fusion.38 = f32[512,512]{0,1:S(1)} fusion(bf16[512,1024]{1,0:T(8,128)(2,1)} %bitcast.82, bf16[1024,512]{0,1:T(8,128)(2,1)S(1)} %bitcast.71), kind=kOutput, calls=%fused_computation.75 | convolution fusion | flops 536870912 | bytes 3145728
  33.1 0.1 select_reduce_fusion
  33.2 0.8 copy.28
  34.1 15.2 %shard_map.110 = bf16[8,64,64]{2,1,0:T(8,128)(2,1)} custom-call(f32[8,64,64]{2,1,0:T(8,128)} %bitcast.77), custom_call_target="tpu_custom_call" | custom-call | tf_op jit(solution)/shard_map/pallas_call | solution.py:535
  49.3 1.0 %copy.29 = bf16[512,64]{0,1:T(8,128)(2,1)S(1)} copy(bf16[512,64]{1,0:T(8,128)(2,1)} %bitcast.78) | data formatting | bytes 131072 | tf_op jit(solution)/shard_map/jit(_where)/broadcast_in_dim | solution.py:565
  50.3 1.7 %bitcast_convert_fusion = bf16[512,1024]{1,0:T(8,128)(2,1)} fusion(bf16[8,64,1024]{2,1,0:T(8,128)(2,1)S(1)} %copy-done.5, pred[512,8]{0,1:T(8,128)(4,1)S(1)} %iota_compare_fusion.8, bf16[512,64]{0,1:T(8,128)(2,1)S(1)} %copy.29), kind=kOutput, calls=%fused_computation.1 | convolution fusion | flops 537657344 | bytes 2166784 | tf_op jit(solution)/shard_map/dot_general | solution.py:567
  52.1 0.1 convert_element_type.87
  52.2 0.5 fusion.24
  52.7 0.9 %pad_maximum_fusion = (f32[256,128]{1,0:T(8,128)}, f32[256,128]{1,0:T(8,128)}) fusion(f32[256,64]{1,0:T(8,128)S(1)} %get-tuple-element.21, f32[256,64]{1,0:T(8,128)S(1)} %get-tuple-element.20, f32[256,64]{1,0:T(8,128)S(1)} %get-tuple-element.19), kind=kLoop, calls=%fused_computation.41 | loop fusion | flops 65536 | bytes 458752 | tf_op jit(solution)/shard_map/concatenate | solution.py:632
  53.6 0.8 fusion.12.refs_5_
  54.4 22.4 %shard_map.111 = (bf16[256,1024]{1,0:T(8,128)(2,1)}, bf16[256,128]{1,0:T(8,128)(2,1)}, bf16[256,128]{1,0:T(8,128)(2,1)}) custom-call(bf16[16,32,1024]{2,1,0:T(8,128)(2,1)} %bitcast.75, bf16[3,256,1024]{2,1,0:T(8,128)(2,1)} %get-tuple-element.13.refs_1_, bf16[8192,1024]{1,0:T(8,128)(2,1)} %refs_2_.1, bf16[8192,128]{1,0:T(8,128)(2,1)} %refs_3_.1, ...), custom_call_target="tpu_custom_call" | custom-call | tf_op jit(solution)/shard_map/pallas_call | solution.py:436
  76.8 1.2 %copy.34 = bf16[32,8,8,128]{3,2,1,0:T(8,128)(2,1)S(1)} copy(bf16[32,8,8,128]{3,1,2,0:T(8,128)(2,1)} %bitcast.79) | data formatting | bytes 1048576
  78.0 0.1 convert_element_type.88
  78.2 1.6 %multiply_reduce_fusion = f32[64,4,8,4]{2,3,1,0:T(4,128)S(1)} fusion(f32[64,4,128]{2,1,0:T(4,128)S(1)} %convert.2, f32[64,4,8,128]{3,2,1,0:T(8,128)S(1)} %convert_element_type.88), kind=kLoop, calls=%fused_computation | loop fusion | flops 2088960 | bytes 1212416 | tf_op jit(solution)/shard_map/reduce_sum | solution.py:42
  79.8 0.5 fusion.14
  80.4 0.8 fusion.37
  81.2 0.6 fusion.15
  81.8 0.8 fusion.8
  82.7 0.9 %convolution_bitcast_fusion = f32[64,128,4,8]{1,3,2,0:T(8,128)S(1)} fusion(bf16[64,64,128]{2,1,0:T(8,128)(2,1)S(1)} %copy-done.6, f32[64,4,1,8,64]{4,3,1,0,2:T(8,128)S(1)} %get-tuple-element.23, f32[64,4,8]{2,1,0:T(4,128)S(1)} %add.98, f32[64,4,8]{2,1,0:T(4,128)S(1)} %max.9), kind=kOutput, calls=%fused_computation.6 | convolution fusion | flops 33947648 | bytes 2637824 | tf_op jit(solution)/shard_map/rskgl,rlkd->rskgd/dot_general | solution.py:62
  83.6 0.6 fusion.4
  84.2 0.9 %reshape.282 = bf16[64,4,1024]{2,1,0:T(4,128)(2,1)} reshape(bf16[64,4,1,8,128]{4,3,1,0,2:T(8,128)(2,1)S(1)} %fusion.4) | data formatting | bytes 1048576 | tf_op jit(solution)/shard_map/reshape | solution.py:644
  (30 shorter events, 0.7 us)
Async XLA Ops:
  0.0 31.0 %copy-start = (bf16[8,1024,64]{1,2,0:T(8,128)(2,1)S(1)}, bf16[8,1024,64]{1,2,0:T(8,128)(2,1)}, u32[]{:S(2)}) copy-start(bf16[8,1024,64]{1,2,0:T(8,128)(2,1)} %param.18) | copy-start | bytes 3145732
  2.5 2.4 %copy-start.1 = (bf16[256,1024]{1,0:T(8,128)(2,1)}, bf16[256,1024]{1,0:T(8,128)(2,1)S(1)}, u32[]{:S(2)}) copy-start(bf16[256,1024]{1,0:T(8,128)(2,1)S(1)} %reshape.274.refs_2_) | copy-start | bytes 1572868
  31.0 19.2 %copy-start.5 = (bf16[8,64,1024]{2,1,0:T(8,128)(2,1)S(1)}, bf16[8,64,1024]{2,1,0:T(8,128)(2,1)}, u32[]{:S(2)}) copy-start(bf16[8,64,1024]{2,1,0:T(8,128)(2,1)} %param.19) | copy-start | bytes 3145732
  50.3 1.7 %copy-start.4 = (s32[64]{0:T(128)S(1)}, s32[64]{0:T(128)}, u32[]{:S(2)}) copy-start(s32[64]{0:T(128)} %param.14) | copy-start | bytes 772
  76.8 1.3 %copy-start.3 = (bf16[256,128]{1,0:T(8,128)(2,1)S(1)}, bf16[256,128]{1,0:T(8,128)(2,1)}, u32[]{:S(2)}) copy-start(bf16[256,128]{1,0:T(8,128)(2,1)} %get-tuple-element.15) | copy-start | bytes 196612
  78.0 2.4 %copy-start.2 = (bf16[64,64,128]{2,1,0:T(8,128)(2,1)S(1)}, bf16[64,64,128]{2,1,0:T(8,128)(2,1)}, u32[]{:S(2)}) copy-start(bf16[64,64,128]{2,1,0:T(8,128)(2,1)} %param.20) | copy-start | bytes 3145732
  81.2 1.5 %copy-start.6 = (bf16[64,64,128]{2,1,0:T(8,128)(2,1)S(1)}, bf16[64,64,128]{2,1,0:T(8,128)(2,1)}, u32[]{:S(2)}) copy-start(bf16[64,64,128]{2,1,0:T(8,128)(2,1)} %param.21) | copy-start | bytes 3145732
  82.7 0.9 %copy-start.7 = (bf16[256,128]{1,0:T(8,128)(2,1)S(1)}, bf16[256,128]{1,0:T(8,128)(2,1)}, u32[]{:S(2)}) copy-start(bf16[256,128]{1,0:T(8,128)(2,1)} %get-tuple-element.16) | copy-start | bytes 196612

commit v17 on v14

--- a/solution.py
+++ b/solution.py
@@ -180,21 +180,6 @@
     pl.semaphore_signal(barrier, inc=1, device_id={gather_axis: left}, device_id_type=MESH)
     pl.semaphore_wait(barrier, count + 1)
 
-    near = []
-    for side, target in ((0, right), (1, left)):
-        copy = pltpu.make_async_remote_copy(
-            src_ref=piece_ref,
-            dst_ref=chip_pieces.at[1 + side],
-            send_sem=near_send.at[side],
-            recv_sem=near_recv.at[side],
-            device_id={gather_axis: target},
-            device_id_type=MESH,
-        )
-        copy.start()
-        near.append(copy)
-    own_piece = pltpu.make_async_copy(piece_ref, chip_pieces.at[0], piece_sem)
-    own_piece.start()
-
     locals_ = []
     for which in range(arrays):
         local = pltpu.make_async_copy(
@@ -216,6 +201,22 @@
             )
             copy.start()
             outgoing.append(copy)
+
+    near = []
+    for side, target in ((0, right), (1, left)):
+        copy = pltpu.make_async_remote_copy(
+            src_ref=piece_ref,
+            dst_ref=chip_pieces.at[1 + side],
+            send_sem=near_send.at[side],
+            recv_sem=near_recv.at[side],
+            device_id={gather_axis: target},
+            device_id_type=MESH,
+        )
+        copy.start()
+        near.append(copy)
+    own_piece = pltpu.make_async_copy(piece_ref, chip_pieces.at[0], piece_sem)
+    own_piece.start()
+
 
     for side, source in ((0, left), (1, right)):
         near[side].wait_send()
@@ -295,6 +296,21 @@
         pl.semaphore_signal(barrier, inc=1, device_id={gather_axis: neighbour}, device_id_type=MESH)
     pl.semaphore_wait(barrier, count + 2)
 
+    local = pltpu.make_async_copy(send_ref.at[me], got_ref.at[me], local_sem)
+    local.start()
+    outgoing = []
+    for offset in range(1, count):
+        peer = offsets[offset - 1][0](me)
+        copy = pltpu.make_async_remote_copy(
+            src_ref=send_ref.at[peer],
+            dst_ref=got_ref.at[me],
+            send_sem=send_sem.at[offset],
+            recv_sem=recv_sem.at[offset],
+            device_id={axis: peer},
+            device_id_type=MESH,
+        )
+        copy.start()
+        outgoing.append(copy)
     far_out = []
     for side, slot, target, rows in ((0, 1, right, pl.ds(0, half)), (1, 2, left, pl.ds(half, half))):
         copy = pltpu.make_async_remote_copy(
@@ -316,21 +332,6 @@
         device_id_type=MESH,
     )
     to_partner.start()
-    local = pltpu.make_async_copy(send_ref.at[me], got_ref.at[me], local_sem)
-    local.start()
-    outgoing = []
-    for offset in range(1, count):
-        peer = offsets[offset - 1][0](me)
-        copy = pltpu.make_async_remote_copy(
-            src_ref=send_ref.at[peer],
-            dst_ref=got_ref.at[me],
-            send_sem=send_sem.at[offset],
-            recv_sem=recv_sem.at[offset],
-            device_id={axis: peer},
-            device_id_type=MESH,
-        )
-        copy.start()
-        outgoing.append(copy)
 
     piece_width = near_pieces.shape[2]
     chip_shift = (0, chips - 1, 1, 2)

time: 84.1 us -> 84.1 us (level)
  no operation moved by 1% of the time
where the time goes in v17:
time: 84.1 us; the launch traced here: 83.5 us
  Pallas kernels  60.9 us (72%)
  other arithmetic  8.17 us (10%)
  matrix products  7.58 us (9%)
  local copies, waits for them, and re-layouts  6.61 us (8%)
    pallas_call x1, Pallas kernels, exchange_ring(): pl.pallas_call(lambda *refs: exchange_ring_kernel(axis, count, gather_axi...  24.9 us
    pallas_call x1, Pallas kernels, exchange_project(): pl.pallas_call(lambda *refs: exchange_project_kernel(axis, count, gather_...  22.6 us
    pallas_call x1, Pallas kernels, axis_sum(): pl.pallas_call(lambda *refs: sum_kernel(axis, count, *refs), out_shape=ja...  13.4 us
    unnamed x1, matrix products  1.96 us
    dot_general x1, matrix products, owner_adapter_term(): jnp.dot(spread_rows, up_local.reshape(local_adapters * adapter_rank, quer...  1.71 us

profile of v17, /device:TPU:1, one launch (start us, length us, event | category | flops | bytes accessed | tf_op | source)
XLA Modules:
  0.0 83.5 jit_solution(2389119314898819525)
XLA Ops:
  0.0 0.9 %select_reduce_fusion.1 = s32[64]{0:T(128)S(1)} fusion(s32[128]{0:T(128)} %param.13, s32[64]{0:T(128)} %param.12), kind=kLoop, calls=%fused_computation.51 | loop fusion | flops 24512 | bytes 1024 | tf_op jit(solution)/shard_map/reduce_sum | solution.py:600
  1.0 0.2 convert_reduce_fusion
  1.2 0.1 add.93
  1.4 1.2 %reshape.271.refs_2_ = bf16[256,1024]{1,0:T(8,128)(2,1)S(1)} reshape(bf16[64,4,1024]{2,1,0:T(4,128)(2,1)} %param.11) | data formatting | bytes 1048576 | tf_op jit(solution)/shard_map/reshape | solution.py:614
  2.5 1.4 %convolution_convert_fusion = bf16[512,1024]{1,0:T(8,128)(2,1)} fusion(bf16[256,1024]{1,0:T(8,128)(2,1)S(1)} %reshape.271.refs_2_, s32[256]{0:T(256)S(1)} %add.93), kind=kOutput, calls=%fused_computation.2 | convolution fusion | flops 269090816 | bytes 1573888 | tf_op jit(solution)/shard_map/dot_general | solution.py:615
  4.0 0.1 fusion.5
  4.3 0.6 concatenate.9.refs_1_
  4.9 24.9 %shard_map.109 = (bf16[16,32,1024]{2,1,0:T(8,128)(2,1)}, bf16[16,16,128]{2,1,0:T(8,128)(2,1)}, bf16[3,256,1024]{2,1,0:T(8,128)(2,1)}) custom-call(bf16[16,32,1024]{2,1,0:T(8,128)(2,1)} %bitcast.72, bf16[16,16,128]{2,1,0:T(8,128)(2,1)} %concatenate.9.refs_1_, bf16[256,1024]{1,0:T(8,128)(2,1)} %copy-done.1), custom_call_target="tpu_custom_call" | custom-call | tf_op jit(solution)/shard_map/pallas_call | solution.py:254
  29.8 0.8 slice_convert_fusion
  30.6 0.2 copy.33
  30.8 0.1 eq.92
  30.9 2.0 %fusion.38 = f32[512,512]{0,1:S(1)} fusion(bf16[512,1024]{1,0:T(8,128)(2,1)} %bitcast.78, bf16[1024,512]{0,1:T(8,128)(2,1)S(1)} %bitcast.69), kind=kOutput, calls=%fused_computation.75 | convolution fusion | flops 536870912 | bytes 3145728
  32.9 0.1 select_reduce_fusion
  33.0 0.1 copy.28
  33.2 0.8 reshape_reshape.3.refs_0_
  33.9 13.4 %shard_map.110 = bf16[8,32,128]{2,1,0:T(8,128)(2,1)} custom-call(f32[8,32,128]{2,1,0:T(8,128)} %reshape_reshape.3.refs_0_), custom_call_target="tpu_custom_call" | custom-call | tf_op jit(solution)/shard_map/pallas_call | solution.py:536
  47.4 0.9 %broadcast_in_dim.82 = bf16[512,64]{1,0:T(8,128)(2,1)S(1)} reshape(bf16[8,32,128]{2,1,0:T(8,128)(2,1)} %shard_map.110) | data formatting | bytes 131072 | tf_op jit(solution)/shard_map/jit(_where)/broadcast_in_dim | solution.py:566
  48.5 1.7 %bitcast_convert_fusion = bf16[512,1024]{1,0:T(8,128)(2,1)} fusion(bf16[8,64,1024]{2,1,0:T(8,128)(2,1)S(1)} %copy-done.5, pred[512,8]{0,1:T(8,128)(4,1)S(1)} %iota_compare_fusion.8, bf16[512,64]{0,1:T(8,128)(2,1)S(1)} %copy.29), kind=kOutput, calls=%fused_computation.1 | convolution fusion | flops 537657344 | bytes 2166784 | tf_op jit(solution)/shard_map/dot_general | solution.py:568
  50.4 0.5 fusion.24
  50.9 0.9 %pad_maximum_fusion = (f32[256,128]{1,0:T(8,128)}, f32[256,128]{1,0:T(8,128)}) fusion(f32[256,64]{1,0:T(8,128)S(1)} %get-tuple-element.21, f32[256,64]{1,0:T(8,128)S(1)} %get-tuple-element.20, f32[256,64]{1,0:T(8,128)S(1)} %get-tuple-element.19), kind=kLoop, calls=%fused_computation.41 | loop fusion | flops 65536 | bytes 458752 | tf_op jit(solution)/shard_map/concatenate | solution.py:633
  51.8 0.8 fusion.12.refs_5_
  52.6 22.6 %shard_map.111 = (bf16[256,1024]{1,0:T(8,128)(2,1)}, bf16[256,128]{1,0:T(8,128)(2,1)}, bf16[256,128]{1,0:T(8,128)(2,1)}) custom-call(bf16[16,32,1024]{2,1,0:T(8,128)(2,1)} %bitcast.73, bf16[3,256,1024]{2,1,0:T(8,128)(2,1)} %get-tuple-element.13.refs_1_, bf16[8192,1024]{1,0:T(8,128)(2,1)} %refs_2_.1, bf16[8192,128]{1,0:T(8,128)(2,1)} %refs_3_.1, ...), custom_call_target="tpu_custom_call" | custom-call | tf_op jit(solution)/shard_map/pallas_call | solution.py:437
  75.2 1.2 %copy.34 = bf16[32,8,8,128]{3,2,1,0:T(8,128)(2,1)S(1)} copy(bf16[32,8,8,128]{3,1,2,0:T(8,128)(2,1)} %bitcast.75) | data formatting | bytes 1048576
  76.4 0.1 convert_element_type.88
  76.5 1.6 %multiply_reduce_fusion = f32[64,4,8,4]{2,3,1,0:T(4,128)S(1)} fusion(f32[64,4,128]{2,1,0:T(4,128)S(1)} %convert.2, f32[64,4,8,128]{3,2,1,0:T(8,128)S(1)} %convert_element_type.88), kind=kLoop, calls=%fused_computation | loop fusion | flops 2088960 | bytes 1212416 | tf_op jit(solution)/shard_map/reduce_sum | solution.py:42
  78.1 0.5 fusion.14
  78.7 0.8 fusion.37
  79.6 0.6 fusion.15
  80.2 0.8 fusion.8
  81.0 0.9 %convolution_bitcast_fusion = f32[64,128,4,8]{1,3,2,0:T(8,128)S(1)} fusion(bf16[64,64,128]{2,1,0:T(8,128)(2,1)S(1)} %copy-done.6, f32[64,4,1,8,64]{4,3,1,0,2:T(8,128)S(1)} %get-tuple-element.23, f32[64,4,8]{2,1,0:T(4,128)S(1)} %add.98, f32[64,4,8]{2,1,0:T(4,128)S(1)} %max.9), kind=kOutput, calls=%fused_computation.6 | convolution fusion | flops 33947648 | bytes 2637824 | tf_op jit(solution)/shard_map/rskgl,rlkd->rskgd/dot_general | solution.py:62
  82.0 0.6 fusion.4
  82.6 0.9 %reshape.278 = bf16[64,4,1024]{2,1,0:T(4,128)(2,1)} reshape(bf16[64,4,1,8,128]{4,3,1,0,2:T(8,128)(2,1)S(1)} %fusion.4) | data formatting | bytes 1048576 | tf_op jit(solution)/shard_map/reshape | solution.py:645
  (32 shorter events, 0.9 us)
Async XLA Ops:
  0.0 30.9 %copy-start = (bf16[8,1024,64]{1,2,0:T(8,128)(2,1)S(1)}, bf16[8,1024,64]{1,2,0:T(8,128)(2,1)}, u32[]{:S(2)}) copy-start(bf16[8,1024,64]{1,2,0:T(8,128)(2,1)} %param.18) | copy-start | bytes 3145732
  2.5 2.4 %copy-start.1 = (bf16[256,1024]{1,0:T(8,128)(2,1)}, bf16[256,1024]{1,0:T(8,128)(2,1)S(1)}, u32[]{:S(2)}) copy-start(bf16[256,1024]{1,0:T(8,128)(2,1)S(1)} %reshape.271.refs_2_) | copy-start | bytes 1572868
  32.9 15.5 %copy-start.5 = (bf16[8,64,1024]{2,1,0:T(8,128)(2,1)S(1)}, bf16[8,64,1024]{2,1,0:T(8,128)(2,1)}, u32[]{:S(2)}) copy-start(bf16[8,64,1024]{2,1,0:T(8,128)(2,1)} %param.19) | copy-start | bytes 3145732
  48.5 1.7 %copy-start.4 = (s32[64]{0:T(128)S(1)}, s32[64]{0:T(128)}, u32[]{:S(2)}) copy-start(s32[64]{0:T(128)} %param.14) | copy-start | bytes 772
  75.2 1.3 %copy-start.3 = (bf16[256,128]{1,0:T(8,128)(2,1)S(1)}, bf16[256,128]{1,0:T(8,128)(2,1)}, u32[]{:S(2)}) copy-start(bf16[256,128]{1,0:T(8,128)(2,1)} %get-tuple-element.15) | copy-start | bytes 196612
  76.4 2.4 %copy-start.2 = (bf16[64,64,128]{2,1,0:T(8,128)(2,1)S(1)}, bf16[64,64,128]{2,1,0:T(8,128)(2,1)}, u32[]{:S(2)}) copy-start(bf16[64,64,128]{2,1,0:T(8,128)(2,1)} %param.20) | copy-start | bytes 3145732
  79.5 1.5 %copy-start.6 = (bf16[64,64,128]{2,1,0:T(8,128)(2,1)S(1)}, bf16[64,64,128]{2,1,0:T(8,128)(2,1)}, u32[]{:S(2)}) copy-start(bf16[64,64,128]{2,1,0:T(8,128)(2,1)} %param.21) | copy-start | bytes 3145732
  81.0 1.0 %copy-start.7 = (bf16[256,128]{1,0:T(8,128)(2,1)S(1)}, bf16[256,128]{1,0:T(8,128)(2,1)}, u32[]{:S(2)}) copy-start(bf16[256,128]{1,0:T(8,128)(2,1)} %get-tuple-element.16) | copy-start | bytes 196612

commit v18 on v12

--- a/solution.py
+++ b/solution.py
@@ -37,8 +37,12 @@
         jnp.einsum("rskgd,rlkd->rskgl", queries, cache_key, preferred_element_type=jnp.float32)
         * score_scale
     )
+    fresh_keys = jnp.transpose(key_new, (0, 2, 1, 3)).astype(jnp.float32)
     fresh_scores = (
-        jnp.einsum("rskgd,rtkd->rskgt", queries, key_new, preferred_element_type=jnp.float32)
+        jnp.sum(
+            queries.astype(jnp.float32)[:, :, :, :, None, :] * fresh_keys[:, None, :, None, :, :],
+            axis=-1,
+        )
         * score_scale
     )
     live_mask = jnp.arange(cache_key.shape[1], dtype=jnp.int32)[None, :] < lengths[:, None]

time: 84.8 us -> 84 us (level)
  matrix products: 10.7 us -> 7.58 us
  other arithmetic: 5.74 us -> 8.11 us
    dot_general x1 -> x0, matrix products: 3.3 us -> none  [attend(): jnp.einsum('rskgd,rtkd->rskgt', queries, key_new, preferred_element_type=...]
    reduce_sum x0 -> x1, other arithmetic: none -> 1.59 us  [attend(): jnp.sum(queries.astype(jnp.float32)[:, :, :, :, None, :] * fresh_keys[:,...]
where the time goes in v18:
time: 84 us; the launch traced here: 83.4 us
  Pallas kernels  60.8 us (72%)
  other arithmetic  8.11 us (10%)
  matrix products  7.58 us (9%)
  local copies, waits for them, and re-layouts  6.62 us (8%)
    pallas_call x1, Pallas kernels, exchange_ring(): pl.pallas_call(lambda *refs: exchange_ring_kernel(axis, count, gather_axi...  24.9 us
    pallas_call x1, Pallas kernels, exchange_project(): pl.pallas_call(lambda *refs: exchange_project_kernel(axis, count, gather_...  22.4 us
    pallas_call x1, Pallas kernels, axis_sum(): pl.pallas_call(lambda *refs: sum_kernel(axis, count, *refs), out_shape=ja...  13.4 us
    unnamed x1, matrix products  1.96 us
    dot_general x1, matrix products, owner_adapter_term(): jnp.dot(spread_rows, up_local.reshape(local_adapters * adapter_rank, quer...  1.71 us

profile of v18, /device:TPU:1, one launch (start us, length us, event | category | flops | bytes accessed | tf_op | source)
XLA Modules:
  0.0 83.4 jit_solution(2609320142795187528)
XLA Ops:
  0.0 0.9 %select_reduce_fusion.1 = s32[64]{0:T(128)S(1)} fusion(s32[128]{0:T(128)} %param.13, s32[64]{0:T(128)} %param.12), kind=kLoop, calls=%fused_computation.49 | loop fusion | flops 24512 | bytes 1024 | tf_op jit(solution)/shard_map/reduce_sum | solution.py:599
  1.0 0.2 convert_reduce_fusion
  1.2 0.1 add.97
  1.4 1.2 %reshape.285.refs_2_ = bf16[256,1024]{1,0:T(8,128)(2,1)S(1)} reshape(bf16[64,4,1024]{2,1,0:T(4,128)(2,1)} %param.11) | data formatting | bytes 1048576 | tf_op jit(solution)/shard_map/reshape | solution.py:613
  2.5 1.4 %convolution_convert_fusion = bf16[512,1024]{1,0:T(8,128)(2,1)} fusion(bf16[256,1024]{1,0:T(8,128)(2,1)S(1)} %reshape.285.refs_2_, s32[256]{0:T(256)S(1)} %add.97), kind=kOutput, calls=%fused_computation.2 | convolution fusion | flops 269090816 | bytes 1573888 | tf_op jit(solution)/shard_map/dot_general | solution.py:614
  4.0 0.1 fusion.5
  4.3 0.6 concatenate.6.refs_1_
  4.9 24.9 %shard_map.109 = (bf16[16,32,1024]{2,1,0:T(8,128)(2,1)}, bf16[16,16,128]{2,1,0:T(8,128)(2,1)}, bf16[3,256,1024]{2,1,0:T(8,128)(2,1)}) custom-call(bf16[16,32,1024]{2,1,0:T(8,128)(2,1)} %bitcast.72, bf16[16,16,128]{2,1,0:T(8,128)(2,1)} %concatenate.6.refs_1_, bf16[256,1024]{1,0:T(8,128)(2,1)} %copy-done.1), custom_call_target="tpu_custom_call" | custom-call | tf_op jit(solution)/shard_map/pallas_call | solution.py:253
  29.9 0.8 slice_convert_fusion
  30.6 0.2 copy.33
  30.9 0.1 eq.98
  31.0 2.0 %fusion.38 = f32[512,512]{0,1:S(1)} fusion(bf16[512,1024]{1,0:T(8,128)(2,1)} %bitcast.78, bf16[1024,512]{0,1:T(8,128)(2,1)S(1)} %bitcast.69), kind=kOutput, calls=%fused_computation.75 | convolution fusion | flops 536870912 | bytes 3145728
  33.0 0.1 select_reduce_fusion
  33.1 0.1 copy.28
  33.3 0.8 reshape_reshape.3.refs_0_
  34.0 13.4 %shard_map.110 = bf16[8,32,128]{2,1,0:T(8,128)(2,1)} custom-call(f32[8,32,128]{2,1,0:T(8,128)} %reshape_reshape.3.refs_0_), custom_call_target="tpu_custom_call" | custom-call | tf_op jit(solution)/shard_map/pallas_call | solution.py:535
  47.5 0.9 %broadcast_in_dim.129 = bf16[512,64]{1,0:T(8,128)(2,1)S(1)} reshape(bf16[8,32,128]{2,1,0:T(8,128)(2,1)} %shard_map.110) | data formatting | bytes 131072 | tf_op jit(solution)/shard_map/jit(_where)/broadcast_in_dim | solution.py:565
  48.5 1.7 %bitcast_convert_fusion = bf16[512,1024]{1,0:T(8,128)(2,1)} fusion(bf16[8,64,1024]{2,1,0:T(8,128)(2,1)S(1)} %copy-done.5, pred[512,8]{0,1:T(8,128)(4,1)S(1)} %iota_compare_fusion.8, bf16[512,64]{0,1:T(8,128)(2,1)S(1)} %copy.29), kind=kOutput, calls=%fused_computation.1 | convolution fusion | flops 537657344 | bytes 2166784 | tf_op jit(solution)/shard_map/dot_general | solution.py:567
  50.3 0.8 fusion.12.refs_5_
  51.2 0.1 convert_element_type.87
  51.3 1.3 %fusion.24 = (f32[256,128]{1,0:T(8,128)}, f32[256,128]{1,0:T(8,128)}) fusion(f32[128]{0:T(128)S(1)} %get-tuple-element.23, f32[128]{0:T(128)S(1)} %get-tuple-element.24, f32[256]{0:T(256)S(1)} %convert_element_type.87), kind=kLoop, calls=%fused_computation.41 | loop fusion | flops 65536 | bytes 264192 | tf_op jit(solution)/shard_map/mul | solution.py:635
  52.6 22.4 %shard_map.111 = (bf16[256,1024]{1,0:T(8,128)(2,1)}, bf16[256,128]{1,0:T(8,128)(2,1)}, bf16[256,128]{1,0:T(8,128)(2,1)}) custom-call(bf16[16,32,1024]{2,1,0:T(8,128)(2,1)} %bitcast.73, bf16[3,256,1024]{2,1,0:T(8,128)(2,1)} %get-tuple-element.13.refs_1_, bf16[8192,1024]{1,0:T(8,128)(2,1)} %refs_2_.1, bf16[8192,128]{1,0:T(8,128)(2,1)} %refs_3_.1, ...), custom_call_target="tpu_custom_call" | custom-call | tf_op jit(solution)/shard_map/pallas_call | solution.py:436
  75.0 1.2 %copy.34 = bf16[32,8,8,128]{3,2,1,0:T(8,128)(2,1)S(1)} copy(bf16[32,8,8,128]{3,1,2,0:T(8,128)(2,1)} %bitcast.75) | data formatting | bytes 1048576
  76.2 0.1 convert_element_type.88
  76.4 1.6 %multiply_reduce_fusion = f32[64,4,8,4]{2,3,1,0:T(4,128)S(1)} fusion(f32[64,4,128]{2,1,0:T(4,128)S(1)} %convert.2, f32[64,4,8,128]{3,2,1,0:T(8,128)S(1)} %convert_element_type.88), kind=kLoop, calls=%fused_computation | loop fusion | flops 2088960 | bytes 1212416 | tf_op jit(solution)/shard_map/reduce_sum | solution.py:42
  78.0 0.5 fusion.14
  78.6 0.8 fusion.37
  79.4 0.6 fusion.15
  80.1 0.8 fusion.8
  80.9 0.9 %convolution_bitcast_fusion = f32[64,128,4,8]{1,3,2,0:T(8,128)S(1)} fusion(bf16[64,64,128]{2,1,0:T(8,128)(2,1)S(1)} %copy-done.6, f32[64,4,1,8,64]{4,3,1,0,2:T(8,128)S(1)} %get-tuple-element.22, f32[64,4,8]{2,1,0:T(4,128)S(1)} %add.102, f32[64,4,8]{2,1,0:T(4,128)S(1)} %max.9), kind=kOutput, calls=%fused_computation.6 | convolution fusion | flops 33947648 | bytes 2637824 | tf_op jit(solution)/shard_map/rskgl,rlkd->rskgd/dot_general | solution.py:62
  81.8 0.6 fusion.4
  82.5 0.9 %reshape.292 = bf16[64,4,1024]{2,1,0:T(4,128)(2,1)} reshape(bf16[64,4,1,8,128]{4,3,1,0,2:T(8,128)(2,1)S(1)} %fusion.4) | data formatting | bytes 1048576 | tf_op jit(solution)/shard_map/reshape | solution.py:647
  (32 shorter events, 0.9 us)
Async XLA Ops:
  0.0 31.0 %copy-start = (bf16[8,1024,64]{1,2,0:T(8,128)(2,1)S(1)}, bf16[8,1024,64]{1,2,0:T(8,128)(2,1)}, u32[]{:S(2)}) copy-start(bf16[8,1024,64]{1,2,0:T(8,128)(2,1)} %param.18) | copy-start | bytes 3145732
  2.5 2.4 %copy-start.1 = (bf16[256,1024]{1,0:T(8,128)(2,1)}, bf16[256,1024]{1,0:T(8,128)(2,1)S(1)}, u32[]{:S(2)}) copy-start(bf16[256,1024]{1,0:T(8,128)(2,1)S(1)} %reshape.285.refs_2_) | copy-start | bytes 1572868
  33.0 15.5 %copy-start.5 = (bf16[8,64,1024]{2,1,0:T(8,128)(2,1)S(1)}, bf16[8,64,1024]{2,1,0:T(8,128)(2,1)}, u32[]{:S(2)}) copy-start(bf16[8,64,1024]{2,1,0:T(8,128)(2,1)} %param.19) | copy-start | bytes 3145732
  48.5 2.6 %copy-start.4 = (s32[64]{0:T(128)S(1)}, s32[64]{0:T(128)}, u32[]{:S(2)}) copy-start(s32[64]{0:T(128)} %param.14) | copy-start | bytes 772
  75.0 1.3 %copy-start.3 = (bf16[256,128]{1,0:T(8,128)(2,1)S(1)}, bf16[256,128]{1,0:T(8,128)(2,1)}, u32[]{:S(2)}) copy-start(bf16[256,128]{1,0:T(8,128)(2,1)} %get-tuple-element.15) | copy-start | bytes 196612
  76.2 2.4 %copy-start.2 = (bf16[64,64,128]{2,1,0:T(8,128)(2,1)S(1)}, bf16[64,64,128]{2,1,0:T(8,128)(2,1)}, u32[]{:S(2)}) copy-start(bf16[64,64,128]{2,1,0:T(8,128)(2,1)} %param.20) | copy-start | bytes 3145732
  79.4 1.5 %copy-start.6 = (bf16[64,64,128]{2,1,0:T(8,128)(2,1)S(1)}, bf16[64,64,128]{2,1,0:T(8,128)(2,1)}, u32[]{:S(2)}) copy-start(bf16[64,64,128]{2,1,0:T(8,128)(2,1)} %param.21) | copy-start | bytes 3145732
  80.9 1.0 %copy-start.7 = (bf16[256,128]{1,0:T(8,128)(2,1)S(1)}, bf16[256,128]{1,0:T(8,128)(2,1)}, u32[]{:S(2)}) copy-start(bf16[256,128]{1,0:T(8,128)(2,1)} %get-tuple-element.16) | copy-start | bytes 196612

commit v19 on v18

--- a/solution.py
+++ b/solution.py
@@ -596,9 +596,7 @@
     group_size = q_local // kv_local
     count_of_tokens = row_count * step_count
     adapter_span = jnp.arange(pool_slot.shape[0], dtype=jnp.int32)
-    pool_pos = jnp.sum(
-        jnp.where(adapter_id[:, None] == adapter_span[None, :], pool_slot[None, :], 0), axis=1
-    )
+    pool_pos = jnp.take(pool_slot, adapter_id, axis=0, mode="clip")
     owner_grp = pool_pos // local_adapter_rows
     local_slot = pool_pos % local_adapter_rows
     row_span = jnp.arange(row_count, dtype=jnp.int32)

time: 84 us -> 85.2 us (1.014)
  local copies, waits for them, and re-layouts: 6.62 us -> 8.04 us
    gather x0 -> x1, local copies, waits for them, and re-layouts: none -> 1.43 us  [body(): pool_pos = jnp.take(pool_slot, adapter_id, axis=0, mode='clip')]
    reduce_sum x1 -> x0, other arithmetic: 0.93 us -> none  [body(): jnp.sum(jnp.where(adapter_id[:, None] == adapter_span[None, :], pool_slot...]
where the time goes in v19:
time: 85.2 us; the launch traced here: 84.6 us
  Pallas kernels  60.8 us (71%)
  local copies, waits for them, and re-layouts  8.04 us (9%)
  other arithmetic  7.93 us (9%)
  matrix products  7.58 us (9%)
    pallas_call x1, Pallas kernels, exchange_ring(): pl.pallas_call(lambda *refs: exchange_ring_kernel(axis, count, gather_axi...  24.9 us
    pallas_call x1, Pallas kernels, exchange_project(): pl.pallas_call(lambda *refs: exchange_project_kernel(axis, count, gather_...  22.4 us
    pallas_call x1, Pallas kernels, axis_sum(): pl.pallas_call(lambda *refs: sum_kernel(axis, count, *refs), out_shape=ja...  13.4 us
    unnamed x1, matrix products  1.96 us
    dot_general x1, matrix products, owner_adapter_term(): jnp.dot(spread_rows, up_local.reshape(local_adapters * adapter_rank, quer...  1.71 us

profile of v19, /device:TPU:1, one launch (start us, length us, event | category | flops | bytes accessed | tf_op | source)
XLA Modules:
  0.0 84.6 jit_solution(4567105261839684193)
XLA Ops:
  0.0 0.7 pad_clamp_fusion
  0.8 1.4 %gather_fusion = s32[64]{0:T(128)S(1)} fusion(s32[128]{0:T(128)} %param.13, s32[1024]{0:T(1024)S(1)} %pad_clamp_fusion), kind=kCustom, calls=%fused_computation | custom fusion | bytes 768 | tf_op jit(solution)/shard_map/jit(_take)/gather | solution.py:599
  2.2 0.2 convert_reduce_fusion
  2.5 0.1 add.97
  2.6 1.2 %reshape.283.refs_2_ = bf16[256,1024]{1,0:T(8,128)(2,1)S(1)} reshape(bf16[64,4,1024]{2,1,0:T(4,128)(2,1)} %param.11) | data formatting | bytes 1048576 | tf_op jit(solution)/shard_map/reshape | solution.py:611
  3.8 1.4 %convolution_convert_fusion = bf16[512,1024]{1,0:T(8,128)(2,1)} fusion(bf16[256,1024]{1,0:T(8,128)(2,1)S(1)} %reshape.283.refs_2_, s32[256]{0:T(256)S(1)} %add.97), kind=kOutput, calls=%fused_computation.3 | convolution fusion | flops 269090816 | bytes 1573888 | tf_op jit(solution)/shard_map/dot_general | solution.py:612
  5.2 0.1 fusion.5
  5.5 0.6 concatenate.6.refs_1_
  6.2 24.9 %shard_map.109 = (bf16[16,32,1024]{2,1,0:T(8,128)(2,1)}, bf16[16,16,128]{2,1,0:T(8,128)(2,1)}, bf16[3,256,1024]{2,1,0:T(8,128)(2,1)}) custom-call(bf16[16,32,1024]{2,1,0:T(8,128)(2,1)} %bitcast.72, bf16[16,16,128]{2,1,0:T(8,128)(2,1)} %concatenate.6.refs_1_, bf16[256,1024]{1,0:T(8,128)(2,1)} %copy-done.1), custom_call_target="tpu_custom_call" | custom-call | tf_op jit(solution)/shard_map/pallas_call | solution.py:253
  31.1 0.8 slice_convert_fusion
  31.9 0.2 copy.33
  32.1 0.1 eq.82
  32.3 2.0 %fusion.38 = f32[512,512]{0,1:S(1)} fusion(bf16[512,1024]{1,0:T(8,128)(2,1)} %bitcast.78, bf16[1024,512]{0,1:T(8,128)(2,1)S(1)} %bitcast.69), kind=kOutput, calls=%fused_computation.75 | convolution fusion | flops 536870912 | bytes 3145728
  34.2 0.1 select_reduce_fusion
  34.4 0.1 copy.28
  34.5 0.8 reshape_reshape.3.refs_0_
  35.3 13.4 %shard_map.110 = bf16[8,32,128]{2,1,0:T(8,128)(2,1)} custom-call(f32[8,32,128]{2,1,0:T(8,128)} %reshape_reshape.3.refs_0_), custom_call_target="tpu_custom_call" | custom-call | tf_op jit(solution)/shard_map/pallas_call | solution.py:535
  48.7 0.9 %broadcast_in_dim.117 = bf16[512,64]{1,0:T(8,128)(2,1)S(1)} reshape(bf16[8,32,128]{2,1,0:T(8,128)(2,1)} %shard_map.110) | data formatting | bytes 131072 | tf_op jit(solution)/shard_map/jit(_where)/broadcast_in_dim | solution.py:565
  49.8 1.7 %bitcast_convert_fusion = bf16[512,1024]{1,0:T(8,128)(2,1)} fusion(bf16[8,64,1024]{2,1,0:T(8,128)(2,1)S(1)} %copy-done.5, pred[512,8]{0,1:T(8,128)(4,1)S(1)} %iota_compare_fusion.7, bf16[512,64]{0,1:T(8,128)(2,1)S(1)} %copy.29), kind=kOutput, calls=%fused_computation.2 | convolution fusion | flops 537657344 | bytes 2166784 | tf_op jit(solution)/shard_map/dot_general | solution.py:567
  51.5 0.8 fusion.12.refs_5_
  52.6 1.3 %fusion.24 = (f32[256,128]{1,0:T(8,128)}, f32[256,128]{1,0:T(8,128)}) fusion(f32[128]{0:T(128)S(1)} %get-tuple-element.23, f32[128]{0:T(128)S(1)} %get-tuple-element.24, f32[256]{0:T(256)S(1)} %convert_element_type.87), kind=kLoop, calls=%fused_computation.42 | loop fusion | flops 65536 | bytes 264192 | tf_op jit(solution)/shard_map/mul | solution.py:633
  53.8 22.4 %shard_map.111 = (bf16[256,1024]{1,0:T(8,128)(2,1)}, bf16[256,128]{1,0:T(8,128)(2,1)}, bf16[256,128]{1,0:T(8,128)(2,1)}) custom-call(bf16[16,32,1024]{2,1,0:T(8,128)(2,1)} %bitcast.73, bf16[3,256,1024]{2,1,0:T(8,128)(2,1)} %get-tuple-element.13.refs_1_, bf16[8192,1024]{1,0:T(8,128)(2,1)} %refs_2_.1, bf16[8192,128]{1,0:T(8,128)(2,1)} %refs_3_.1, ...), custom_call_target="tpu_custom_call" | custom-call | tf_op jit(solution)/shard_map/pallas_call | solution.py:436
  76.3 1.2 %copy.34 = bf16[32,8,8,128]{3,2,1,0:T(8,128)(2,1)S(1)} copy(bf16[32,8,8,128]{3,1,2,0:T(8,128)(2,1)} %bitcast.75) | data formatting | bytes 1048576
  77.5 0.1 convert_element_type.88
  77.6 1.6 %multiply_reduce_fusion = f32[64,4,8,4]{2,3,1,0:T(4,128)S(1)} fusion(f32[64,4,128]{2,1,0:T(4,128)S(1)} %convert.2, f32[64,4,8,128]{3,2,1,0:T(8,128)S(1)} %convert_element_type.88), kind=kLoop, calls=%fused_computation.1 | loop fusion | flops 2088960 | bytes 1212416 | tf_op jit(solution)/shard_map/reduce_sum | solution.py:42
  79.2 0.5 fusion.14
  79.8 0.8 fusion.37
  80.7 0.6 fusion.15
  81.3 0.8 fusion.8
  82.1 0.9 %convolution_bitcast_fusion = f32[64,128,4,8]{1,3,2,0:T(8,128)S(1)} fusion(bf16[64,64,128]{2,1,0:T(8,128)(2,1)S(1)} %copy-done.6, f32[64,4,1,8,64]{4,3,1,0,2:T(8,128)S(1)} %get-tuple-element.22, f32[64,4,8]{2,1,0:T(4,128)S(1)} %add.102, f32[64,4,8]{2,1,0:T(4,128)S(1)} %max.9), kind=kOutput, calls=%fused_computation.7 | convolution fusion | flops 33947648 | bytes 2637824 | tf_op jit(solution)/shard_map/rskgl,rlkd->rskgd/dot_general | solution.py:62
  83.1 0.6 fusion.4
  83.7 0.9 %reshape.290 = bf16[64,4,1024]{2,1,0:T(4,128)(2,1)} reshape(bf16[64,4,1,8,128]{4,3,1,0,2:T(8,128)(2,1)S(1)} %fusion.4) | data formatting | bytes 1048576 | tf_op jit(solution)/shard_map/reshape | solution.py:645
  (33 shorter events, 1.0 us)
Async XLA Ops:
  0.0 32.2 %copy-start = (bf16[8,1024,64]{1,2,0:T(8,128)(2,1)S(1)}, bf16[8,1024,64]{1,2,0:T(8,128)(2,1)}, u32[]{:S(2)}) copy-start(bf16[8,1024,64]{1,2,0:T(8,128)(2,1)} %param.18) | copy-start | bytes 3145732
  3.8 2.4 %copy-start.1 = (bf16[256,1024]{1,0:T(8,128)(2,1)}, bf16[256,1024]{1,0:T(8,128)(2,1)S(1)}, u32[]{:S(2)}) copy-start(bf16[256,1024]{1,0:T(8,128)(2,1)S(1)} %reshape.283.refs_2_) | copy-start | bytes 1572868
  34.2 15.5 %copy-start.5 = (bf16[8,64,1024]{2,1,0:T(8,128)(2,1)S(1)}, bf16[8,64,1024]{2,1,0:T(8,128)(2,1)}, u32[]{:S(2)}) copy-start(bf16[8,64,1024]{2,1,0:T(8,128)(2,1)} %param.19) | copy-start | bytes 3145732
  49.8 2.6 %copy-start.4 = (s32[64]{0:T(128)S(1)}, s32[64]{0:T(128)}, u32[]{:S(2)}) copy-start(s32[64]{0:T(128)} %param.14) | copy-start | bytes 772
  76.3 1.3 %copy-start.3 = (bf16[256,128]{1,0:T(8,128)(2,1)S(1)}, bf16[256,128]{1,0:T(8,128)(2,1)}, u32[]{:S(2)}) copy-start(bf16[256,128]{1,0:T(8,128)(2,1)} %get-tuple-element.15) | copy-start | bytes 196612
  77.4 2.4 %copy-start.2 = (bf16[64,64,128]{2,1,0:T(8,128)(2,1)S(1)}, bf16[64,64,128]{2,1,0:T(8,128)(2,1)}, u32[]{:S(2)}) copy-start(bf16[64,64,128]{2,1,0:T(8,128)(2,1)} %param.20) | copy-start | bytes 3145732
  80.6 1.5 %copy-start.6 = (bf16[64,64,128]{2,1,0:T(8,128)(2,1)S(1)}, bf16[64,64,128]{2,1,0:T(8,128)(2,1)}, u32[]{:S(2)}) copy-start(bf16[64,64,128]{2,1,0:T(8,128)(2,1)} %param.21) | copy-start | bytes 3145732
  82.1 1.0 %copy-start.7 = (bf16[256,128]{1,0:T(8,128)(2,1)S(1)}, bf16[256,128]{1,0:T(8,128)(2,1)}, u32[]{:S(2)}) copy-start(bf16[256,128]{1,0:T(8,128)(2,1)} %get-tuple-element.16) | copy-start | bytes 196612

commit v20 on v18

--- a/solution.py
+++ b/solution.py
@@ -611,7 +611,7 @@
     token_span = jnp.arange(group_count * CAP * step_count, dtype=jnp.int32)
     place_tokens = (token_span[:, None] == token_slot[None, :]).astype(jnp.bfloat16)
     token_rows = tokens.reshape(count_of_tokens, part_width)
-    send_tokens = jnp.dot(place_tokens, token_rows, preferred_element_type=jnp.float32).astype(jnp.bfloat16)
+    send_tokens = jnp.dot(place_tokens, token_rows, preferred_element_type=jnp.bfloat16)
     send_tokens = send_tokens.reshape(group_count, CAP * step_count, part_width)
     send_ids = jnp.dot(
         place, local_slot.astype(jnp.bfloat16)[:, None], preferred_element_type=jnp.float32

time: 84 us -> 87.1 us (1.037)
  local copies, waits for them, and re-layouts: 6.62 us -> 8.61 us
  other arithmetic: 8.11 us -> 9.04 us
    reshape x1 -> x2, local copies, waits for them, and re-layouts: 1.16 us -> 3.12 us  [body(): token_rows = tokens.reshape(count_of_tokens, part_width)]
    convert_element_type x1, other arithmetic: 0.02 us -> 0.94 us  [attend(): fresh_keys = jnp.transpose(key_new, (0, 2, 1, 3)).astype(jnp.float32)]
where the time goes in v20:
time: 87.1 us; the launch traced here: 86.4 us
  Pallas kernels  60.9 us (70%)
  other arithmetic  9.04 us (10%)
  local copies, waits for them, and re-layouts  8.61 us (10%)
  matrix products  7.62 us (9%)
    pallas_call x1, Pallas kernels, exchange_ring(): pl.pallas_call(lambda *refs: exchange_ring_kernel(axis, count, gather_axi...  25 us
    pallas_call x1, Pallas kernels, exchange_project(): pl.pallas_call(lambda *refs: exchange_project_kernel(axis, count, gather_...  22.4 us
    pallas_call x1, Pallas kernels, axis_sum(): pl.pallas_call(lambda *refs: sum_kernel(axis, count, *refs), out_shape=ja...  13.4 us
    reshape x2, local copies, waits for them, and re-layouts, body(): token_rows = tokens.reshape(count_of_tokens, part_width)  3.12 us
    unnamed x1, matrix products  1.96 us

profile of v20, /device:TPU:1, one launch (start us, length us, event | category | flops | bytes accessed | tf_op | source)
XLA Modules:
  0.0 86.4 jit_solution(12954988872919097767)
XLA Ops:
  0.0 0.9 %select_reduce_fusion.1 = s32[64]{0:T(128)S(1)} fusion(s32[128]{0:T(128)} %param.13, s32[64]{0:T(128)} %param.12), kind=kLoop, calls=%fused_computation.50 | loop fusion | flops 24512 | bytes 1024 | tf_op jit(solution)/shard_map/reduce_sum | solution.py:599
  1.0 0.2 convert_reduce_fusion
  1.2 0.1 fusion.5
  1.5 0.6 concatenate.6.refs_1_
  2.3 1.2 %reshape.310 = bf16[256,1024,1]{1,0,2:T(8,128)(2,1)S(1)} reshape(bf16[64,4,1024]{2,1,0:T(4,128)(2,1)} %param.11) | data formatting | bytes 1048576 | tf_op jit(solution)/shard_map/reshape | solution.py:613
  3.5 1.5 %fusion.14.refs_0_ = bf16[16,32,1024]{2,1,0:T(8,128)(2,1)} fusion(bf16[256,1024,1]{1,0,2:T(8,128)(2,1)S(1)} %reshape.310, s32[256]{0:T(256)S(1)} %add.101, s32[16,32]{1,0:T(8,128)S(1)} %multiply_add_fusion), kind=kOutput, calls=%fused_computation.27 | convolution fusion | flops 268566528 | bytes 1575936 | tf_op jit(solution)/shard_map/dot_general | solution.py:614
  5.0 2.0 %reshape.301.refs_2_ = bf16[256,1024]{1,0:T(8,128)(2,1)} reshape(bf16[64,4,1024]{2,1,0:T(4,128)(2,1)} %param.11) | data formatting | bytes 1048576 | tf_op jit(solution)/shard_map/reshape | solution.py:613
  6.9 25.0 %shard_map.109 = (bf16[16,32,1024]{2,1,0:T(8,128)(2,1)}, bf16[16,16,128]{2,1,0:T(8,128)(2,1)}, bf16[3,256,1024]{2,1,0:T(8,128)(2,1)}) custom-call(bf16[16,32,1024]{2,1,0:T(8,128)(2,1)} %fusion.14.refs_0_, bf16[16,16,128]{2,1,0:T(8,128)(2,1)} %concatenate.6.refs_1_, bf16[256,1024]{1,0:T(8,128)(2,1)} %reshape.301.refs_2_), custom_call_target="tpu_custom_call" | custom-call | tf_op jit(solution)/shard_map/pallas_call | solution.py:253
  31.9 0.8 slice_convert_fusion
  32.7 0.2 copy.33
  32.9 0.1 eq.112
  33.1 2.0 %fusion.41 = f32[512,512]{0,1:S(1)} fusion(bf16[512,1024]{1,0:T(8,128)(2,1)} %bitcast.76, bf16[1024,512]{0,1:T(8,128)(2,1)S(1)} %bitcast.68), kind=kOutput, calls=%fused_computation.77 | convolution fusion | flops 536870912 | bytes 3145728
  35.1 0.1 select_reduce_fusion
  35.2 0.1 copy.28
  35.3 0.8 reshape_reshape.3.refs_0_
  36.1 13.4 %shard_map.110 = bf16[8,32,128]{2,1,0:T(8,128)(2,1)} custom-call(f32[8,32,128]{2,1,0:T(8,128)} %reshape_reshape.3.refs_0_), custom_call_target="tpu_custom_call" | custom-call | tf_op jit(solution)/shard_map/pallas_call | solution.py:535
  49.5 0.9 %broadcast_in_dim.129 = bf16[512,64]{1,0:T(8,128)(2,1)S(1)} reshape(bf16[8,32,128]{2,1,0:T(8,128)(2,1)} %shard_map.110) | data formatting | bytes 131072 | tf_op jit(solution)/shard_map/jit(_where)/broadcast_in_dim | solution.py:565
  50.6 1.7 %bitcast_convert_fusion = bf16[512,1024]{1,0:T(8,128)(2,1)} fusion(bf16[8,64,1024]{2,1,0:T(8,128)(2,1)S(1)} %copy-done.3, pred[512,8]{0,1:T(8,128)(4,1)S(1)} %iota_compare_fusion.6, bf16[512,64]{0,1:T(8,128)(2,1)S(1)} %copy.29), kind=kOutput, calls=%fused_computation.1 | convolution fusion | flops 537657344 | bytes 2166784 | tf_op jit(solution)/shard_map/dot_general | solution.py:567
  52.3 0.8 fusion.12.refs_5_
  53.4 1.3 %fusion.27 = (f32[256,128]{1,0:T(8,128)}, f32[256,128]{1,0:T(8,128)}) fusion(f32[128]{0:T(128)S(1)} %get-tuple-element.23, f32[128]{0:T(128)S(1)} %get-tuple-element.24, f32[256]{0:T(256)S(1)} %convert_element_type.83), kind=kLoop, calls=%fused_computation.42 | loop fusion | flops 65536 | bytes 264192 | tf_op jit(solution)/shard_map/mul | solution.py:635
  54.7 22.4 %shard_map.111 = (bf16[256,1024]{1,0:T(8,128)(2,1)}, bf16[256,128]{1,0:T(8,128)(2,1)}, bf16[256,128]{1,0:T(8,128)(2,1)}) custom-call(bf16[16,32,1024]{2,1,0:T(8,128)(2,1)} %bitcast.71, bf16[3,256,1024]{2,1,0:T(8,128)(2,1)} %get-tuple-element.13.refs_1_, bf16[8192,1024]{1,0:T(8,128)(2,1)} %refs_2_.1, bf16[8192,128]{1,0:T(8,128)(2,1)} %refs_3_.1, ...), custom_call_target="tpu_custom_call" | custom-call | tf_op jit(solution)/shard_map/pallas_call | solution.py:436
  77.1 1.2 %copy.34 = bf16[32,8,8,128]{3,2,1,0:T(8,128)(2,1)S(1)} copy(bf16[32,8,8,128]{3,1,2,0:T(8,128)(2,1)} %bitcast.73) | data formatting | bytes 1048576
  78.3 0.1 convert_element_type.84
  78.5 0.9 %convert.2 = f32[64,4,128]{2,1,0:T(4,128)S(1)} convert(bf16[64,4,128]{2,1,0:T(4,128)(2,1)} %bitcast.74) | non-fusion elementwise | flops 32768 | bytes 196608 | tf_op jit(solution)/shard_map/convert_element_type | solution.py:40
  79.4 1.6 %multiply_reduce_fusion = f32[64,4,8,4]{2,3,1,0:T(4,128)S(1)} fusion(f32[64,4,128]{2,1,0:T(4,128)S(1)} %convert.2, f32[64,4,8,128]{3,2,1,0:T(8,128)S(1)} %convert_element_type.84), kind=kLoop, calls=%fused_computation | loop fusion | flops 2088960 | bytes 1212416 | tf_op jit(solution)/shard_map/reduce_sum | solution.py:42
  81.0 0.5 fusion.16
  81.6 0.8 fusion.40
  82.5 0.6 fusion.17
  83.1 0.8 fusion.8
  83.9 0.9 %convolution_bitcast_fusion = f32[64,128,4,8]{1,3,2,0:T(8,128)S(1)} fusion(bf16[64,64,128]{2,1,0:T(8,128)(2,1)S(1)} %copy-done.4, f32[64,4,1,8,64]{4,3,1,0,2:T(8,128)S(1)} %get-tuple-element.22, f32[64,4,8]{2,1,0:T(4,128)S(1)} %add.106, f32[64,4,8]{2,1,0:T(4,128)S(1)} %max.9), kind=kOutput, calls=%fused_computation.5 | convolution fusion | flops 33947648 | bytes 2637824 | tf_op jit(solution)/shard_map/rskgl,rlkd->rskgd/dot_general | solution.py:62
  84.8 0.6 fusion.4
  85.5 0.9 %reshape.307 = bf16[64,4,1024]{2,1,0:T(4,128)(2,1)} reshape(bf16[64,4,1,8,128]{4,3,1,0,2:T(8,128)(2,1)S(1)} %fusion.4) | data formatting | bytes 1048576 | tf_op jit(solution)/shard_map/reshape | solution.py:647
  (30 shorter events, 1.1 us)
Async XLA Ops:
  0.0 33.1 %copy-start = (bf16[8,1024,64]{1,2,0:T(8,128)(2,1)S(1)}, bf16[8,1024,64]{1,2,0:T(8,128)(2,1)}, u32[]{:S(2)}) copy-start(bf16[8,1024,64]{1,2,0:T(8,128)(2,1)} %param.18) | copy-start | bytes 3145732
  6.9 43.7 %copy-start.3 = (bf16[8,64,1024]{2,1,0:T(8,128)(2,1)S(1)}, bf16[8,64,1024]{2,1,0:T(8,128)(2,1)}, u32[]{:S(2)}) copy-start(bf16[8,64,1024]{2,1,0:T(8,128)(2,1)} %param.19) | copy-start | bytes 3145732
  35.3 17.9 %copy-start.2 = (s32[64]{0:T(128)S(1)}, s32[64]{0:T(128)}, u32[]{:S(2)}) copy-start(s32[64]{0:T(128)} %param.14) | copy-start | bytes 772
  77.1 4.5 %copy-start.1 = (bf16[64,64,128]{2,1,0:T(8,128)(2,1)S(1)}, bf16[64,64,128]{2,1,0:T(8,128)(2,1)}, u32[]{:S(2)}) copy-start(bf16[64,64,128]{2,1,0:T(8,128)(2,1)} %param.20) | copy-start | bytes 3145732
  78.5 5.4 %copy-start.4 = (bf16[64,64,128]{2,1,0:T(8,128)(2,1)S(1)}, bf16[64,64,128]{2,1,0:T(8,128)(2,1)}, u32[]{:S(2)}) copy-start(bf16[64,64,128]{2,1,0:T(8,128)(2,1)} %param.21) | copy-start | bytes 3145732
  83.8 1.0 %copy-start.5 = (bf16[256,128]{1,0:T(8,128)(2,1)S(1)}, bf16[256,128]{1,0:T(8,128)(2,1)}, u32[]{:S(2)}) copy-start(bf16[256,128]{1,0:T(8,128)(2,1)} %get-tuple-element.16) | copy-start | bytes 196612
